TPU v7x, 256 devices: a whole 4x4x8 slice. The times are simulated.
256 devices in a mesh: grp: 8 (over z_hi, core), dev: 32 (over y, x, z_lo).
Axes of the slice: x: 4, y: 4, z: 8 (z_hi: 4, z_lo: 2; z = z_hi * 2 + z_lo), core: 2. Of those that a mesh axis runs over, the one named last changes fastest.
Arguments:
- queries: float32 [256, 12, 128], P(('grp', 'dev')), may hold values from -2.1 to 2.1
- pages: float32 [256, 256, 128], P(('grp', 'dev')), may hold values from -2.1 to 2.1
- positive: int32 [256], replicated, may hold values from 0 to 255
Outputs:
- loss: float32 [], replicated
- question_token_slope: float32 [256, 12, 128], P(('grp', 'dev'))
- page_grad: float32 [256, 256, 128], P(('grp', 'dev'))
All inputs are finite; a program needn't handle non-finite values.
Results may differ from a plain program's by a relative error of at most 0.00019.
Values sent between devices are 32-bit elements; how exact they have to be, the bound alone decides.
No kernel may reach another device: no remote copies, remote signals or barrier semaphores. Data moves between devices by JAX's collectives and lax.ppermute only.
A program may use at most 64 MiB of HBM per device.

v0:
```python
import functools

import jax
import jax.numpy as jnp
from jax import lax
from jax.sharding import Mesh
from jax.sharding import PartitionSpec as P

GRP_DEV = ("grp_0", "grp_1", "dev_0", "dev_1", "dev_2")


cap_value = 4.0
sharpness_divisor = 0.25
logit_scale = 8.0
z_weight = 0.001
highest = lax.Precision.HIGHEST


def one_axis_at_a_time(shard, axes):
    return functools.reduce(lax.psum, axes, shard)


def block_partial_terms(query_rows, page_rows, query_tokens):
    scores = jnp.dot(query_rows, page_rows.T, precision=highest, preferred_element_type=jnp.float32)
    tangent = jnp.tanh(scores / cap_value)
    bounded_similarity = cap_value * tangent
    exponential_grid = jnp.exp(bounded_similarity / sharpness_divisor)
    accumulated_totals = jnp.sum(exponential_grid, axis=1)
    gentle_peak = sharpness_divisor * jnp.log(accumulated_totals)
    slopes = (
        exponential_grid
        / accumulated_totals[:, None]
        * (1.0 - tangent * tangent)
        * (logit_scale / query_tokens)
    )
    return (gentle_peak, slopes)


def shards(queries, pages, positive):
    gathered = lax.all_gather(queries, GRP_DEV, axis=0, tiled=True)
    query_count, query_tokens, feature_width = gathered.shape
    page_rows = pages[0]
    page_index = lax.axis_index(GRP_DEV)
    block_size = 16
    block_count = query_count // block_size
    query_blocks = gathered.reshape(block_count, block_size * query_tokens, feature_width)
    chosen = (positive == page_index).astype(jnp.float32)

    def block_logits(gentle_peak):
        return (
            logit_scale / query_tokens * gentle_peak.reshape(block_size, query_tokens).sum(axis=1)
        )

    def evaluate_loss_and_slopes(query_rows):
        gentle_peak, slopes = block_partial_terms(query_rows, page_rows, query_tokens)
        unscaled = jnp.dot(slopes, page_rows, precision=highest, preferred_element_type=jnp.float32)
        return (block_logits(gentle_peak), unscaled)

    logits, unscaled = lax.map(evaluate_loss_and_slopes, query_blocks)
    statistics_logits = logits.reshape(query_count)
    exponential_grid = jnp.exp(statistics_logits)
    accumulated_totals = one_axis_at_a_time(exponential_grid, GRP_DEV)
    matching_logit = one_axis_at_a_time(chosen * statistics_logits, GRP_DEV)
    log_totals = jnp.log(accumulated_totals)
    loss = jnp.mean(log_totals - matching_logit + z_weight * log_totals * log_totals)
    coefficients = (
        (1.0 + 2.0 * z_weight * log_totals) * exponential_grid / accumulated_totals - chosen
    ) / query_count
    loss, coefficients = (loss, coefficients)
    factors = jnp.repeat(coefficients, query_tokens).reshape(
        block_count, block_size * query_tokens, 1
    )
    query_terms = unscaled * factors

    def page_only(page_total, inputs):
        query_rows, factor_rows = inputs
        unused_smooth, slopes = block_partial_terms(query_rows, page_rows, query_tokens)
        token_grads = slopes * factor_rows
        page_total = page_total + jnp.dot(
            token_grads.T, query_rows, precision=highest, preferred_element_type=jnp.float32
        )
        return (page_total, None)

    page_start = jnp.zeros(page_rows.shape, jnp.float32)
    page_total, unused_outputs = lax.scan(page_only, page_start, (query_blocks, factors))
    query_terms = query_terms.reshape(query_count, query_tokens, feature_width)
    summed = lax.psum(query_terms, GRP_DEV)
    own_count = queries.shape[0]
    question_token_slope = lax.dynamic_slice_in_dim(summed, page_index * own_count, own_count, 0)
    return (loss, question_token_slope, page_total[None])


def solution(mesh):
    finer = Mesh(mesh.devices.reshape(4, 2, 4, 4, 2), ("grp_0", "grp_1", "dev_0", "dev_1", "dev_2"))
    placed = (P(GRP_DEV, None, None), P(GRP_DEV, None, None), P())
    return jax.shard_map(
        shards,
        mesh=finer,
        in_specs=placed,
        out_specs=(P(), P(GRP_DEV, None, None), P(GRP_DEV, None, None)),
        check_vma=False,
    )
```

profile of v0, /device:TPU:1, one launch (start us, length us, event | category | flops | bytes accessed | tf_op | source)
XLA Modules:
  0.0 1046.8 jit_solution(13401674488803938812)
XLA Ops:
  7.2 1.3 copy.13
  8.6 699.9 %all-gather.2.cloned.1.call-done = f32[256,12,128]{2,1,0:T(8,128)} async-done(((f32[1,12,128]{2,1,0:T(8,128)}), f32[256,12,128]{2,1,0:T(8,128)}) %all-gather.2.cloned.1.call-update) | async-done | bytes 1572880 | tf_op jit(solution)/shard_map/all_gather | solution.py:40
  708.5 1.6 reshape.45
  710.2 27.7 %while.27 = (s32[]{:T(128)}, f32[16,16]{1,0:T(8,128)S(1)}, f32[16,192,128]{2,1,0:T(8,128)}, f32[16,192,128]{2,1,0:T(8,128)S(1)}, f32[256,128]{1,0:T(8,128)S(1)}, /*index=5*/s32[]{:T(128)}, f32[]{:T(128)}, s32[]{:T(128)}) while((s32[]{:T(128)}, f32[16,16]{1,0:T(8,128)S(1)}, f32[16,192,128]{2,1,0:T(8,128)}, f32[16,192,128]{2,1,0:T(8,128)S(1)}, ...), condition=%wide.region_3.4_spmd, body=%wide.region_0.3_spmd.sunk | while | flops 151437504 | bytes 857773 | solution.py:59
  710.2 0.4 fusion.55
  710.9 1.0 fusion.56
  712.6 1.0 fusion.56
  714.4 1.0 fusion.56
  716.1 1.0 fusion.56
  717.8 1.0 fusion.56
  719.6 1.0 fusion.56
  721.3 1.0 fusion.56
  723.0 1.0 fusion.56
  724.8 1.0 fusion.56
  726.5 1.0 fusion.56
  728.2 1.0 fusion.56
  730.0 1.0 fusion.56
  731.7 1.0 fusion.56
  733.4 1.0 fusion.56
  735.1 1.0 fusion.56
  736.9 1.0 fusion.56
  738.0 12.8 %all-reduce.2 = (f32[256]{0:T(256)S(1)}, f32[256]{0:T(256)S(1)}) all-reduce(f32[256]{0:T(256)S(1)} %get-tuple-element.216, f32[256]{0:T(256)S(1)} %get-tuple-element.215), channel_id=1, replica_groups=mesh['grp_0'=4,'grp_1'=2,'dev_0'=4,'dev_1'=4,'dev_2'=2] {'grp_0'}, use_global_device_ids=true, to_apply=%region_9.10 | all-reduce | flops 512 | bytes 4096 | tf_op jit(solution)/shard_map/psum | solution.py:20
  750.8 3.4 all-reduce.4
  754.2 6.1 all-reduce.1
  760.2 6.3 all-reduce
  766.5 5.0 all-reduce.3
  771.6 0.6 subtract_multiply_fusion
  772.6 1.9 broadcast_multiply_fusion
  774.5 1.4 reshape.47
  775.9 0.9 copy-done.2
  776.8 20.1 %while.28 = (s32[]{:T(128)}, f32[256,128]{1,0:T(8,128)S(1)}, f32[16,192,128]{2,1,0:T(8,128)S(1)}, f32[256,128]{1,0:T(8,128)S(1)}, f32[16,192,1]{1,2,0:T(1,128)S(1)}, /*index=5*/s32[]{:T(128)}, s32[]{:T(128)}) while((s32[]{:T(128)}, f32[256,128]{1,0:T(8,128)S(1)}, f32[16,192,128]{2,1,0:T(8,128)S(1)}, f32[256,128]{1,0:T(8,128)S(1)}, ...), condition=%wide.region_18.19_spmd.clone, body=%wide.region_16.18_spmd.clone.sunk | while | flops 151502848 | bytes 987499 | solution.py:85
  777.3 0.8 convolution_add_fusion.2
  778.5 0.8 convolution_add_fusion.2
  779.3 0.5 fusion.60
  779.8 0.8 convolution_add_fusion.2
  780.6 0.5 fusion.60
  781.0 0.8 convolution_add_fusion.2
  781.9 0.5 fusion.60
  782.3 0.8 convolution_add_fusion.2
  783.1 0.5 fusion.60
  783.6 0.8 convolution_add_fusion.2
  784.4 0.5 fusion.60
  784.8 0.8 convolution_add_fusion.2
  785.6 0.5 fusion.60
  786.1 0.8 convolution_add_fusion.2
  786.9 0.5 fusion.60
  787.4 0.8 convolution_add_fusion.2
  788.2 0.5 fusion.60
  788.6 0.8 convolution_add_fusion.2
  789.4 0.5 fusion.60
  789.9 0.8 convolution_add_fusion.2
  790.7 0.5 fusion.60
  791.1 0.8 convolution_add_fusion.2
  791.9 0.5 fusion.60
  792.4 0.8 convolution_add_fusion.2
  793.2 0.5 fusion.60
  793.7 0.8 convolution_add_fusion.2
  794.5 0.5 fusion.60
  794.9 0.8 convolution_add_fusion.2
  795.7 0.5 fusion.60
  796.2 0.8 convolution_add_fusion.2
  797.6 239.9 %all-reduce.7.cloned.1.call-done = f32[256,12,128]{2,1,0:T(8,128)} async-done(((f32[256,12,128]{2,1,0:T(8,128)}), f32[256,12,128]{2,1,0:T(8,128)}) %all-reduce.7.cloned.1.call-update) | async-done | bytes 1572880 | tf_op jit(solution)/shard_map/psum | solution.py:87
  1037.6 0.7 constant_dynamic-slice_fusion
  1038.3 0.6 copy.15
  (133 shorter events, 12.3 us)
Async XLA Ops:
  7.2 701.4 %all-gather.2.cloned.1.call-start = ((), (), s32[]{:S(2)}) async-start(), calls=%async_computation | async-start | bytes 2105344 | tf_op jit(solution)/shard_map/all_gather | solution.py:40
  8.5 1029.0 %all-reduce.7.cloned.1.call-start = ((), (), s32[]{:S(2)}) async-start(), calls=%async_computation.1 | async-start | bytes 4194304 | tf_op jit(solution)/shard_map/psum | solution.py:87
  8.6 701.5 %copy-start = (f32[1,256,128]{2,1,0:T(8,128)S(1)}, f32[1,256,128]{2,1,0:T(8,128)}, u32[]{:S(2)}) copy-start(f32[1,256,128]{2,1,0:T(8,128)} %param.8) | copy-start | bytes 393220
  710.2 27.8 %copy-start.1 = (s32[256]{0:T(256)S(1)}, s32[256]{0:T(256)}, u32[]{:S(2)}) copy-start(s32[256]{0:T(256)} %param.9) | copy-start | bytes 3076
  775.9 0.9 copy-start.2
  797.0 241.9 %copy-start.3 = (f32[256,128]{1,0:T(8,128)}, f32[256,128]{1,0:T(8,128)S(1)}, u32[]{:S(2)}) copy-start(f32[256,128]{1,0:T(8,128)S(1)} %get-tuple-element.136) | copy-start | bytes 393220
Sparse Core Ops, SparseCore 0:
  9.9 698.6 all-gather.1
  776.1 261.4 all-reduce.6
where the time goes:
time: 1050 us
  waiting for transfers between devices  940 us (90%)
  matrix products  42.8 us (4%)
  blocking collectives  33.6 us (3%)
  between operations  15.9 us (2%)
    all_gather x1, waiting for transfers between devices, shards(): gathered = lax.all_gather(queries, GRP_DEV, axis=0, tiled=True)  700 us
    psum x1, waiting for transfers between devices, shards(): summed = lax.psum(query_terms, GRP_DEV)  240 us
    psum x5, blocking collectives, one_axis_at_a_time(): return functools.reduce(lax.psum, axes, shard)  33.6 us
  transfers between devices with their start and end apart: 2, of which 2 were waited for; matrix products, arithmetic and copies ran while one was open for 2% of the time, Pallas kernels for 0%

commit v1 on v0

v1 whole, which is shorter than its diff:
```python
import itertools

import jax
import jax.numpy as jnp
from jax import lax
from jax.experimental import pallas as pl
from jax.experimental.pallas import tpu as pltpu
from jax.sharding import Mesh
from jax.sharding import PartitionSpec as P

AXES = ("za", "co", "y", "x", "zb")
SIZES = dict(za=4, co=2, y=4, x=4, zb=2)
QUERY_AXES = ("za", "y", "zb")
QN = 32
XN = 4
TOK = 12
ROWS = QN * TOK
PT = 256
W = 128
NQ = 256

cap_value = 4.0
sharpness_divisor = 0.25
logit_scale = 8.0
z_weight = 0.001
f32 = jnp.float32
bf16 = jnp.bfloat16


def iota(shape, dim):
    return lax.broadcasted_iota(jnp.int32, shape, dim)


def parts(x):
    high = x.astype(bf16)
    return high, (x - high.astype(f32)).astype(bf16)


def product(a, b, dims, a_axis, b_axis):
    left = jnp.concatenate([a[0], a[0], a[1]], axis=a_axis)
    right = jnp.concatenate([b[0], b[1], b[0]], axis=b_axis)
    return lax.dot_general(left, right, (dims, ((), ())), preferred_element_type=f32)


def spread_matrix():
    row, lane = iota((ROWS, 128), 0), iota((ROWS, 128), 1)
    first = (lane & 31) * TOK
    return ((row >= first) & (row < first + TOK) & (lane < 64)).astype(f32)


def page_terms(q_parts, pages, whi_ref, wlo_ref, ut_ref, tot_ref):
    for s, page_ref in enumerate(pages):
        page = page_ref[0]
        scores = product(parts(page), q_parts, ((1,), (0,)), 1, 0)
        tangent = jnp.tanh(scores * (1.0 / cap_value))
        grid = jnp.exp(tangent * (cap_value / sharpness_divisor))
        tot_ref[s : s + 1, :] = jnp.sum(grid, axis=0, keepdims=True)
        weights = parts(grid * (1.0 - tangent * tangent))
        whi_ref[s] = weights[0]
        wlo_ref[s] = weights[1]
        ut_ref[s] = product(parts(page.T), weights, ((1,), (0,)), 1, 0)


def own_side_kernel(q_ref, p0, p1, p2, p3, whi_ref, wlo_ref, ut_ref, tot_ref, qt_ref, rows_ref):
    for k in range(QN):
        rows_ref[k * TOK : (k + 1) * TOK, :] = q_ref[k]
    qt = rows_ref[...].T
    qt_ref[...] = qt
    page_terms(parts(qt), (p0, p1, p2, p3), whi_ref, wlo_ref, ut_ref, tot_ref)


def is_positive(me_ref, positive_ref):
    me = me_ref[0]
    base = me & 0b00100110
    index, lane = iota((NQ, 128), 0), iota((NQ, 128), 1)
    k = lane & 31
    query = ((k >> 3) << 6) + (((k >> 1) & 3) << 3) + (k & 1) + base
    chosen = jnp.dot(
        positive_ref[...].astype(f32), (index == query).astype(f32), precision=lax.Precision.HIGHEST,
        preferred_element_type=f32,
    )
    row = iota((8, 128), 0)
    x = (((me >> 1) & 3) - (row & 3)) & 3
    co = ((me >> 5) & 1) ^ (row >> 2)
    page = (me & 0b11011001) + (x << 1) + (co << 5)
    return page.astype(f32) == chosen


def other_side_kernel(
    me_ref, positive_ref, qt_ref, tot_a_ref, p0, p1, p2, p3,
    whi_ref, wlo_ref, ut_ref, tot_ref, logits_ref, stats_ref,
):
    page_terms(parts(qt_ref[...]), (p0, p1, p2, p3), whi_ref, wlo_ref, ut_ref, tot_ref.at[4:8])
    tot_ref[0:4, :] = tot_a_ref[...]
    smooth = sharpness_divisor * jnp.log(tot_ref[...])
    logits = (logit_scale / TOK) * jnp.dot(
        smooth, spread_matrix(), precision=lax.Precision.HIGHEST, preferred_element_type=f32
    )
    logits_ref[...] = logits
    lane = iota((8, 128), 1)
    matched = jnp.where(is_positive(me_ref, positive_ref), logits, 0.0)
    local = jnp.where(lane < 32, jnp.exp(logits), jnp.where(lane < 64, matched, 0.0))
    summed = jnp.sum(local, axis=0, keepdims=True)
    stats_ref[...] = jnp.broadcast_to(summed[None], stats_ref.shape)


def page_gradients(whi_ref, wlo_ref, qt, factors, out_ref):
    for s in range(XN):
        scaled = parts(qt * factors[s : s + 1, :])
        out_ref[s * PT : (s + 1) * PT, :] = product(
            (whi_ref[s], wlo_ref[s]), scaled, ((1,), (1,)), 1, 1
        )


def coefficient_kernel(
    me_ref, positive_ref, stats_ref, logits_ref, tot_ref, qt_ref, whi_ref, wlo_ref,
    out_ref, factors_ref,
):
    stats = jnp.sum(stats_ref[...], axis=0)
    lane = iota((1, 128), 1)
    totals = jnp.where(lane < 32, stats, 1.0)
    log_totals = jnp.log(totals)
    terms = jnp.where(
        lane < 32, log_totals + z_weight * log_totals * log_totals, jnp.where(lane < 64, -stats, 0.0)
    )
    loss = jnp.sum(terms, axis=1, keepdims=True) * (1.0 / NQ)
    out_ref[XN * PT :, :] = jnp.broadcast_to(loss, (8, 128))
    chosen = is_positive(me_ref, positive_ref).astype(f32)
    exponential = jnp.where(iota((8, 128), 1) < 32, jnp.exp(logits_ref[...]), 0.0)
    coefficients = (
        (1.0 + 2.0 * z_weight * log_totals) * exponential / totals - chosen
    ) * (1.0 / NQ)
    coefficients = jnp.where(iota((8, 128), 1) < 32, coefficients, 0.0)
    rows = lax.dot_general(
        coefficients, spread_matrix(), (((1,), (1,)), ((), ())), precision=lax.Precision.HIGHEST,
        preferred_element_type=f32,
    )
    factors = rows * (logit_scale / TOK) / tot_ref[...]
    factors_ref[...] = factors
    page_gradients(whi_ref, wlo_ref, qt_ref[...], factors[4:8], out_ref)


def gradient_kernel(factors_ref, qt_ref, whi_ref, wlo_ref, ut_a_ref, ut_b_ref, out_ref, dq_ref, rows_ref):
    factors = factors_ref[...]
    page_gradients(whi_ref, wlo_ref, qt_ref[...], factors[0:4], out_ref)
    total = jnp.zeros((W, ROWS), f32)
    for s in range(XN):
        total = total + ut_a_ref[s] * factors[s : s + 1, :]
        total = total + ut_b_ref[s] * factors[4 + s : 5 + s, :]
    rows_ref[...] = total.T
    for k in range(QN):
        dq_ref[k] = rows_ref[k * TOK : (k + 1) * TOK, :]


def pair_kernel(mine_ref, loss_ref, theirs_ref, o0, o1, o2, o3):
    loss = loss_ref[...] + theirs_ref[XN * PT :, :]
    for s, out in enumerate((o0, o1, o2, o3)):
        rows = slice(s * PT, (s + 1) * PT)
        out[0:PT, :] = mine_ref[rows, :] + theirs_ref[rows, :]
        out[PT:, :] = loss


def final_kernel(r0, r1, r2, r3, dq_ref, page_ref, loss_ref, slope_ref):
    total = (r0[...] + r2[...]) + (r1[...] + r3[...])
    page_ref[0] = total[0:PT]
    loss_ref[...] = total[PT:]
    slope_ref[0] = jnp.sum(dq_ref[...], axis=0)


def call(kernel, out, scratch=(), scalars=0):
    vmem = pl.BlockSpec(memory_space=pltpu.VMEM)

    def run(*args):
        specs = [pl.BlockSpec(memory_space=pltpu.SMEM)] * scalars + [vmem] * (len(args) - scalars)
        return pl.pallas_call(
            kernel,
            out_shape=[jax.ShapeDtypeStruct(s, d) for s, d in out],
            in_specs=specs,
            out_specs=[vmem] * len(out),
            scratch_shapes=list(scratch),
            compiler_params=pltpu.CompilerParams(vmem_limit_bytes=48 * 1024 * 1024),
        )(*args)

    return run


def moved(value, axis, step):
    n = SIZES[axis]
    return lax.ppermute(value, axis, [(i, (i + step) % n) for i in range(n)])


def shards(queries, pages, positive):
    me = lax.axis_index(AXES).astype(jnp.int32).reshape(1)
    positive = positive.reshape(1, NQ)
    own = [pages] + [moved(pages, "x", s) for s in range(1, XN)]
    spread = jnp.broadcast_to(queries, (QN, TOK, W))
    block = lax.all_to_all(spread, QUERY_AXES, 0, 0, tiled=True)
    other = [moved(page, "co", 1) for page in own]

    halves = [((XN, PT, ROWS), bf16), ((XN, PT, ROWS), bf16), ((XN, W, ROWS), f32)]
    whi_a, wlo_a, ut_a, tot_a, qt = call(
        own_side_kernel, halves + [((XN, ROWS), f32), ((W, ROWS), f32)],
        [pltpu.VMEM((ROWS, W), f32)],
    )(block, *own)
    whi_b, wlo_b, ut_b, tot, logits, stats = call(
        other_side_kernel,
        halves + [((2 * XN, ROWS), f32), ((8, 128), f32), ((QN, 1, 128), f32)],
        scalars=1,
    )(me, positive, qt, tot_a, *other)
    stats = lax.all_to_all(stats, QUERY_AXES, 0, 0, tiled=True)
    theirs, factors = call(
        coefficient_kernel, [((XN * PT + 8, W), f32), ((2 * XN, ROWS), f32)], scalars=1
    )(me, positive, stats, logits, tot, qt, whi_b, wlo_b)
    loss_rows = theirs[XN * PT :]
    theirs = moved(theirs, "co", 1)
    mine, dq = call(
        gradient_kernel, [((XN * PT, W), f32), ((QN, TOK, W), f32)], [pltpu.VMEM((ROWS, W), f32)]
    )(factors, qt, whi_a, wlo_a, ut_a, ut_b)
    sums = call(pair_kernel, [((PT + 8, W), f32)] * XN)(mine, loss_rows, theirs)
    sums = [sums[0]] + [moved(sums[s], "x", -s) for s in range(1, XN)]
    dq = lax.all_to_all(dq, QUERY_AXES, 0, 0, tiled=True)
    page_grad, loss, slope = call(
        final_kernel, [((1, PT, W), f32), ((8, 128), f32), ((1, TOK, W), f32)]
    )(*sums, dq)
    return loss[0, 0], slope, page_grad


def solution(mesh):
    finer = Mesh(mesh.devices.reshape(tuple(SIZES[a] for a in AXES)), AXES)
    placed = (P(AXES, None, None), P(AXES, None, None), P())
    return jax.shard_map(
        shards,
        mesh=finer,
        in_specs=placed,
        out_specs=(P(), P(AXES, None, None), P(AXES, None, None)),
        check_vma=False,
    )
```

time: 1050 us -> 71.6 us (0.07)
  waiting for transfers between devices: 940 us -> 10.5 us
  matrix products: 42.8 us -> 0 us
  starting transfers between devices: 0.08 us -> 31.6 us
  blocking collectives: 33.6 us -> 17.7 us
  between operations: 15.9 us -> 0.75 us
    all_gather x1 -> x0, waiting for transfers between devices: 700 us -> none  [shards(): gathered = lax.all_gather(queries, GRP_DEV, axis=0, tiled=True)]
    psum x1 -> x0, waiting for transfers between devices: 240 us -> none  [shards(): summed = lax.psum(query_terms, GRP_DEV)]
    dot_general x64 -> x0, matrix products: 42.8 us -> none  [the longest x16 16.1 us: evaluate_loss_and_slopes(): jnp.dot(slopes, page_rows, precision=highest, preferred_element_type=jnp....]
    psum x5 -> x0, blocking collectives: 33.6 us -> none  [one_axis_at_a_time(): return functools.reduce(lax.psum, axes, shard)]
    all_to_all x0 -> x1, blocking collectives: none -> 17.7 us  [shards(): stats = lax.all_to_all(stats, QUERY_AXES, 0, 0, tiled=True)]
    all_to_all x0 -> x2, starting transfers between devices: none -> 16 us  [the longest x1 12.2 us: shards(): block = lax.all_to_all(spread, QUERY_AXES, 0, 0, tiled=True)]
    ppermute x0 -> x11, starting transfers between devices: none -> 15.5 us  [moved(): return lax.ppermute(value, axis, [(i, (i + step) % n) for i in range(n)])]
  transfers between devices with their start and end apart: 2 -> 13, of which waited for: 2 -> 2; matrix products, arithmetic and copies ran while one was open for 2% -> 0% of each run, Pallas kernels for 0% -> 5%
where the time goes in v1:
time: 71.6 us; the launch traced here: 71.2 us
  starting transfers between devices  31.6 us (44%)
  blocking collectives  17.7 us (25%)
  waiting for transfers between devices  10.5 us (15%)
  Pallas kernels  7.54 us (11%)
  local copies, waits for them, and re-layouts  3.2 us (4%)
  between operations  0.75 us (1%)
    all_to_all x1, blocking collectives, shards(): stats = lax.all_to_all(stats, QUERY_AXES, 0, 0, tiled=True)  17.7 us
    ppermute x11, starting transfers between devices, moved(): return lax.ppermute(value, axis, [(i, (i + step) % n) for i in range(n)])  15.5 us
    all_to_all x1, starting transfers between devices, shards(): block = lax.all_to_all(spread, QUERY_AXES, 0, 0, tiled=True)  12.2 us
    all_to_all x1, waiting for transfers between devices, shards(): dq = lax.all_to_all(dq, QUERY_AXES, 0, 0, tiled=True)  10.1 us
    pallas_call x6, Pallas kernels, run(): pl.pallas_call(kernel, out_shape=[jax.ShapeDtypeStruct(s, d) for s, d in...  7.54 us
    all_to_all x1, starting transfers between devices, shards(): dq = lax.all_to_all(dq, QUERY_AXES, 0, 0, tiled=True)  3.87 us
    unnamed x6, local copies, waits for them, and re-layouts  1.97 us
  transfers between devices with their start and end apart: 13, of which 2 were waited for; matrix products, arithmetic and copies ran while one was open for 0% of the time, Pallas kernels for 5%

profile of v1, /device:TPU:1, one launch (start us, length us, event | category | flops | bytes accessed | tf_op | source)
XLA Modules:
  0.0 71.2 jit_solution(435141158784858793)
XLA Ops:
  0.6 0.7 copy.9
  1.3 0.7 %broadcast_in_dim.8 = f32[32,12,128]{2,1,0:T(8,128)} broadcast(f32[12,128]{1,0:T(8,128)S(1)} %bitcast.8), dimensions={1,2} | broadcast | bytes 202752 | tf_op jit(solution)/shard_map/broadcast_in_dim | solution.py:196
  2.0 0.0 copy-start
  2.0 12.2 %all-to-all-start = ((f32[32,12,128]{2,1,0:T(8,128)}), f32[32,12,128]{2,1,0:T(8,128)S(1)}, u32[]{:S(2)}, u32[]{:S(2)}) async-start(f32[32,12,128]{2,1,0:T(8,128)} %broadcast_in_dim.8), calls=%async_computation | async-start | bytes 524288 | tf_op jit(solution)/shard_map/all_to_all | solution.py:197
  14.2 0.0 copy-done
  14.2 2.6 %collective-permute-start.2 = (f32[1,256,128]{2,1,0:T(8,128)S(1)}, f32[1,256,128]{2,1,0:T(8,128)S(1)}, u32[]{:S(2)}, u32[]{:S(2)}) collective-permute-start(f32[1,256,128]{2,1,0:T(8,128)S(1)} %copy-done), channel_id=1, source_target_pairs={{0,6},{2,0},{4,2},{6,4},{1,7},{3,1},{5,3},{7,5},{8,14},{10,8},{12,... | collective-permute-start | bytes 393224 | tf_op jit(solution)/shard_map/ppermute | solution.py:189
  16.8 0.5 collective-permute-start.1
  17.3 0.6 collective-permute-start
  17.9 1.8 %collective-permute-start.3 = (f32[1,256,128]{2,1,0:T(8,128)S(1)}, f32[1,256,128]{2,1,0:T(8,128)S(1)}, u32[]{:S(2)}, u32[]{:S(2)}) collective-permute-start(f32[1,256,128]{2,1,0:T(8,128)S(1)} %copy-done), channel_id=1, source_target_pairs={{0,32},{32,0},{1,33},{33,1},{2,34},{34,2},{3,35},{35,3},{4,36},{36... | collective-permute-start | bytes 393224 | tf_op jit(solution)/shard_map/ppermute | solution.py:189
  19.7 0.0 collective-permute-done.2.p3
  19.7 3.6 %collective-permute-start.6 = (f32[1,256,128]{2,1,0:T(8,128)S(1)}, f32[1,256,128]{2,1,0:T(8,128)S(1)}, u32[]{:S(2)}, u32[]{:S(2)}) collective-permute-start(f32[1,256,128]{2,1,0:T(8,128)S(1)} %collective-permute-done.2.p3), channel_id=1, source_target_pairs={{0,32},{32,0},{1,33},{33,1},{2,34},{34,2},{3,35},{35,3},{4,36},{36... | collective-permute-start | bytes 393224 | tf_op jit(solution)/shard_map/ppermute | solution.py:189
  23.3 0.0 collective-permute-done.1.p2
  23.3 2.3 %collective-permute-start.5 = (f32[1,256,128]{2,1,0:T(8,128)S(1)}, f32[1,256,128]{2,1,0:T(8,128)S(1)}, u32[]{:S(2)}, u32[]{:S(2)}) collective-permute-start(f32[1,256,128]{2,1,0:T(8,128)S(1)} %collective-permute-done.1.p2), channel_id=1, source_target_pairs={{0,32},{32,0},{1,33},{33,1},{2,34},{34,2},{3,35},{35,3},{4,36},{36... | collective-permute-start | bytes 393224 | tf_op jit(solution)/shard_map/ppermute | solution.py:189
  25.6 0.3 collective-permute-done.p1
  26.0 1.0 %collective-permute-start.4 = (f32[1,256,128]{2,1,0:T(8,128)S(1)}, f32[1,256,128]{2,1,0:T(8,128)S(1)}, u32[]{:S(2)}, u32[]{:S(2)}) collective-permute-start(f32[1,256,128]{2,1,0:T(8,128)S(1)} %collective-permute-done.p1), channel_id=1, source_target_pairs={{0,32},{32,0},{1,33},{33,1},{2,34},{34,2},{3,35},{35,3},{4,36},{36... | collective-permute-start | bytes 393224 | tf_op jit(solution)/shard_map/ppermute | solution.py:189
  27.0 0.0 all-to-all-done.q_ref
  27.0 2.0 %shard_map.58 = (bf16[4,256,384]{2,1,0:T(8,128)(2,1)S(1)}, bf16[4,256,384]{2,1,0:T(8,128)(2,1)S(1)}, f32[4,128,384]{2,1,0:T(8,128)S(1)}, f32[4,384]{1,0:T(4,128)S(1)}, f32[128,384]{1,0:T(8,128)S(1)}) custom-call(f32[32,12,128]{2,1,0:T(8,128)S(1)} %all-to-all-done.q_ref, f32[1,256,128]{2,1,0:T(8,128)S(1)} %copy-done, ...), custom_call_target="tpu_custom_call" | custom-call | tf_op jit(solution)/shard_map/pallas_call | solution.py:175
  29.0 0.0 collective-permute-done.3.p0
  29.0 0.0 collective-permute-done.6.p3
  29.0 0.0 collective-permute-done.5.p2
  29.0 0.0 collective-permute-done.4.p1
  29.1 0.0 copy-start.1
  29.1 0.7 copy-done.1
  29.7 2.0 %shard_map.59 = (bf16[4,256,384]{2,1,0:T(8,128)(2,1)S(1)}, bf16[4,256,384]{2,1,0:T(8,128)(2,1)S(1)}, f32[4,128,384]{2,1,0:T(8,128)S(1)}, f32[8,384]{1,0:T(8,128)...) custom-call(s32[1]{0:T(128)} %bitcast.me_ref, s32[1,256]{1,0:T(1,128)S(1)} %bitcast.6, ...), custom_call_target="tpu_custom_call" | custom-call | tf_op jit(solution)/shard_map/pallas_call | solution.py:175
  31.8 17.7 %all_to_all.15.stats_ref = f32[32,1,128]{2,1,0:T(1,128)S(1)} all-to-all(f32[32,1,128]{2,1,0:T(1,128)S(1)} %get-tuple-element.27), channel_id=1, replica_groups=mesh['za'=4,'co'=2,'y'=4,'x'=4,'zb'=2] {'za','y','zb'}, dimensions={0} | all-to-all | bytes 32768 | tf_op jit(solution)/shard_map/all_to_all | solution.py:210
  49.4 1.3 %shard_map.60 = (f32[1032,128]{1,0:T(8,128)S(1)}, f32[8,384]{1,0:T(8,128)S(1)}) custom-call(s32[1]{0:T(128)} %bitcast.me_ref, s32[1,256]{1,0:T(1,128)S(1)} %bitcast.7, f32[32,1,128]{2,1,0:T(1,128)S(1)} %all_to_all.15.stats_ref, f32[8,128]{1,0:T(8,128)S(1)} %get-tuple-element.28.logits_ref, f32[8,384]{1,0:T(8,128)S(1)} %get-tuple-element.29.tot_ref, ...), custom_call_target="tpu_custom_call" | custom-call | tf_op jit(solution)/shard_map/pallas_call | solution.py:175
  50.7 1.5 %collective-permute-start.7 = (f32[1032,128]{1,0:T(8,128)S(1)}, f32[1032,128]{1,0:T(8,128)S(1)}, u32[]{:S(2)}, u32[]{:S(2)}) collective-permute-start(f32[1032,128]{1,0:T(8,128)S(1)} %get-tuple-element.38), channel_id=1, source_target_pairs={{0,32},{32,0},{1,33},{33,1},{2,34},{34,2},{3,35},{35,3},{4,36},{36... | collective-permute-start | bytes 1585160 | tf_op jit(solution)/shard_map/ppermute | solution.py:189
  52.2 1.5 %shard_map.61 = (f32[1024,128]{1,0:T(8,128)S(1)}, f32[32,12,128]{2,1,0:T(8,128)}) custom-call(f32[8,384]{1,0:T(8,128)S(1)} %get-tuple-element.32.factors_ref, f32[128,384]{1,0:T(8,128)S(1)} %get-tuple-element.25.qt_ref, bf16[4,256,384]{2,1,0:T(8,128)(2,1)S(1)} %get-tuple-element.33.whi_ref, bf16[4,256,384]{2,1,0:T(8,128)(2,1)S(1)} %get-tuple-element.34.wlo_ref, ...), custom_call_target="tpu_custom_call" | custom-call | tf_op jit(solution)/shard_map/pallas_call | solution.py:175
  53.7 3.9 %all-to-all-start.2 = ((f32[32,12,128]{2,1,0:T(8,128)}), f32[32,12,128]{2,1,0:T(8,128)S(1)}, u32[]{:S(2)}, u32[]{:S(2)}) async-start(f32[32,12,128]{2,1,0:T(8,128)} %get-tuple-element.43), calls=%async_computation.2 | async-start | bytes 524288 | tf_op jit(solution)/shard_map/all_to_all | solution.py:221
  57.6 0.0 collective-permute-done.7.theirs_ref
  57.6 0.1 shard_map.62
  57.7 0.4 collective-permute-start.8
  58.1 0.5 collective-permute-start.9
  58.6 0.7 collective-permute-start.10
  59.2 10.1 %all-to-all-done.2.dq_ref = f32[32,12,128]{2,1,0:T(8,128)S(1)} async-done(((f32[32,12,128]{2,1,0:T(8,128)}), f32[32,12,128]{2,1,0:T(8,128)S(1)}, u32[]{:S(2)}, u32[]{:S(2)}) %all-to-all-start.2) | async-done | bytes 196640 | tf_op jit(solution)/shard_map/all_to_all | solution.py:221
  69.4 0.0 collective-permute-done.8.r1
  69.4 0.0 collective-permute-done.9.r2
  69.4 0.0 collective-permute-done.10.r3
  69.4 0.7 shard_map.63
  70.1 0.5 slice.7
  70.6 0.6 copy.6
  (1 shorter events, 0.0 us)
Async XLA Ops:
  2.0 12.2 %copy-start = (f32[1,256,128]{2,1,0:T(8,128)S(1)}, f32[1,256,128]{2,1,0:T(8,128)}, u32[]{:S(2)}) copy-start(f32[1,256,128]{2,1,0:T(8,128)} %p0.1) | copy-start | bytes 393220
  2.0 25.0 %all-to-all-start = ((f32[32,12,128]{2,1,0:T(8,128)}), f32[32,12,128]{2,1,0:T(8,128)S(1)}, u32[]{:S(2)}, u32[]{:S(2)}) async-start(f32[32,12,128]{2,1,0:T(8,128)} %broadcast_in_dim.8), calls=%async_computation | async-start | bytes 524288 | tf_op jit(solution)/shard_map/all_to_all | solution.py:197
  14.2 5.5 %collective-permute-start.2 = (f32[1,256,128]{2,1,0:T(8,128)S(1)}, f32[1,256,128]{2,1,0:T(8,128)S(1)}, u32[]{:S(2)}, u32[]{:S(2)}) collective-permute-start(f32[1,256,128]{2,1,0:T(8,128)S(1)} %copy-done), channel_id=1, source_target_pairs={{0,6},{2,0},{4,2},{6,4},{1,7},{3,1},{5,3},{7,5},{8,14},{10,8},{12,... | collective-permute-start | bytes 393224 | tf_op jit(solution)/shard_map/ppermute | solution.py:189
  16.8 6.5 %collective-permute-start.1 = (f32[1,256,128]{2,1,0:T(8,128)S(1)}, f32[1,256,128]{2,1,0:T(8,128)S(1)}, u32[]{:S(2)}, u32[]{:S(2)}) collective-permute-start(f32[1,256,128]{2,1,0:T(8,128)S(1)} %copy-done), channel_id=1, source_target_pairs={{0,4},{2,6},{4,0},{6,2},{1,5},{3,7},{5,1},{7,3},{8,12},{10,14},{12... | collective-permute-start | bytes 393224 | tf_op jit(solution)/shard_map/ppermute | solution.py:189
  17.3 8.7 %collective-permute-start = (f32[1,256,128]{2,1,0:T(8,128)S(1)}, f32[1,256,128]{2,1,0:T(8,128)S(1)}, u32[]{:S(2)}, u32[]{:S(2)}) collective-permute-start(f32[1,256,128]{2,1,0:T(8,128)S(1)} %copy-done), channel_id=1, source_target_pairs={{0,2},{2,4},{4,6},{6,0},{1,3},{3,5},{5,7},{7,1},{8,10},{10,12},{12... | collective-permute-start | bytes 393224 | tf_op jit(solution)/shard_map/ppermute | solution.py:189
  17.9 11.1 %collective-permute-start.3 = (f32[1,256,128]{2,1,0:T(8,128)S(1)}, f32[1,256,128]{2,1,0:T(8,128)S(1)}, u32[]{:S(2)}, u32[]{:S(2)}) collective-permute-start(f32[1,256,128]{2,1,0:T(8,128)S(1)} %copy-done), channel_id=1, source_target_pairs={{0,32},{32,0},{1,33},{33,1},{2,34},{34,2},{3,35},{35,3},{4,36},{36... | collective-permute-start | bytes 393224 | tf_op jit(solution)/shard_map/ppermute | solution.py:189
  19.7 9.3 %collective-permute-start.6 = (f32[1,256,128]{2,1,0:T(8,128)S(1)}, f32[1,256,128]{2,1,0:T(8,128)S(1)}, u32[]{:S(2)}, u32[]{:S(2)}) collective-permute-start(f32[1,256,128]{2,1,0:T(8,128)S(1)} %collective-permute-done.2.p3), channel_id=1, source_target_pairs={{0,32},{32,0},{1,33},{33,1},{2,34},{34,2},{3,35},{35,3},{4,36},{36... | collective-permute-start | bytes 393224 | tf_op jit(solution)/shard_map/ppermute | solution.py:189
  23.3 5.7 %collective-permute-start.5 = (f32[1,256,128]{2,1,0:T(8,128)S(1)}, f32[1,256,128]{2,1,0:T(8,128)S(1)}, u32[]{:S(2)}, u32[]{:S(2)}) collective-permute-start(f32[1,256,128]{2,1,0:T(8,128)S(1)} %collective-permute-done.1.p2), channel_id=1, source_target_pairs={{0,32},{32,0},{1,33},{33,1},{2,34},{34,2},{3,35},{35,3},{4,36},{36... | collective-permute-start | bytes 393224 | tf_op jit(solution)/shard_map/ppermute | solution.py:189
  26.0 3.1 %collective-permute-start.4 = (f32[1,256,128]{2,1,0:T(8,128)S(1)}, f32[1,256,128]{2,1,0:T(8,128)S(1)}, u32[]{:S(2)}, u32[]{:S(2)}) collective-permute-start(f32[1,256,128]{2,1,0:T(8,128)S(1)} %collective-permute-done.p1), channel_id=1, source_target_pairs={{0,32},{32,0},{1,33},{33,1},{2,34},{34,2},{3,35},{35,3},{4,36},{36... | collective-permute-start | bytes 393224 | tf_op jit(solution)/shard_map/ppermute | solution.py:189
  29.1 0.7 copy-start.1
  50.7 6.9 %collective-permute-start.7 = (f32[1032,128]{1,0:T(8,128)S(1)}, f32[1032,128]{1,0:T(8,128)S(1)}, u32[]{:S(2)}, u32[]{:S(2)}) collective-permute-start(f32[1032,128]{1,0:T(8,128)S(1)} %get-tuple-element.38), channel_id=1, source_target_pairs={{0,32},{32,0},{1,33},{33,1},{2,34},{34,2},{3,35},{35,3},{4,36},{36... | collective-permute-start | bytes 1585160 | tf_op jit(solution)/shard_map/ppermute | solution.py:189
  53.7 15.6 %all-to-all-start.2 = ((f32[32,12,128]{2,1,0:T(8,128)}), f32[32,12,128]{2,1,0:T(8,128)S(1)}, u32[]{:S(2)}, u32[]{:S(2)}) async-start(f32[32,12,128]{2,1,0:T(8,128)} %get-tuple-element.43), calls=%async_computation.2 | async-start | bytes 524288 | tf_op jit(solution)/shard_map/all_to_all | solution.py:221
  57.7 11.7 %collective-permute-start.8 = (f32[264,128]{1,0:T(8,128)S(1)}, f32[264,128]{1,0:T(8,128)S(1)}, u32[]{:S(2)}, u32[]{:S(2)}) collective-permute-start(f32[264,128]{1,0:T(8,128)S(1)} %get-tuple-element.40), channel_id=1, source_target_pairs={{0,6},{2,0},{4,2},{6,4},{1,7},{3,1},{5,3},{7,5},{8,14},{10,8},{12,... | collective-permute-start | bytes 405512 | tf_op jit(solution)/shard_map/ppermute | solution.py:189
  58.1 11.3 %collective-permute-start.9 = (f32[264,128]{1,0:T(8,128)S(1)}, f32[264,128]{1,0:T(8,128)S(1)}, u32[]{:S(2)}, u32[]{:S(2)}) collective-permute-start(f32[264,128]{1,0:T(8,128)S(1)} %get-tuple-element.41), channel_id=1, source_target_pairs={{0,4},{2,6},{4,0},{6,2},{1,5},{3,7},{5,1},{7,3},{8,12},{10,14},{12... | collective-permute-start | bytes 405512 | tf_op jit(solution)/shard_map/ppermute | solution.py:189
  58.6 10.8 %collective-permute-start.10 = (f32[264,128]{1,0:T(8,128)S(1)}, f32[264,128]{1,0:T(8,128)S(1)}, u32[]{:S(2)}, u32[]{:S(2)}) collective-permute-start(f32[264,128]{1,0:T(8,128)S(1)} %get-tuple-element.42), channel_id=1, source_target_pairs={{0,2},{2,4},{4,6},{6,0},{1,3},{3,5},{5,7},{7,1},{8,10},{10,12},{12... | collective-permute-start | bytes 405512 | tf_op jit(solution)/shard_map/ppermute | solution.py:189

commit v2 on v1

v2 whole, which is shorter than its diff:
```python
import itertools

import jax
import jax.numpy as jnp
from jax import lax
from jax.experimental import pallas as pl
from jax.experimental.pallas import tpu as pltpu
from jax.sharding import Mesh
from jax.sharding import PartitionSpec as P

AXES = ("za", "co", "y", "x", "zb")
SIZES = dict(za=4, co=2, y=4, x=4, zb=2)
QUERY_AXES = ("za", "y", "zb")
QN = 32
XN = 4
TOK = 12
ROWS = QN * TOK
PT = 256
W = 128
NQ = 256

cap_value = 4.0
sharpness_divisor = 0.25
logit_scale = 8.0
z_weight = 0.001
PREPARE_FLOPS = 5_000_000_000
f32 = jnp.float32
bf16 = jnp.bfloat16


def iota(shape, dim):
    return lax.broadcasted_iota(jnp.int32, shape, dim)


def parts(x):
    high = x.astype(bf16)
    return high, (x - high.astype(f32)).astype(bf16)


def product(a, b, dims, a_axis, b_axis):
    left = jnp.concatenate([a[0], a[0], a[1]], axis=a_axis)
    right = jnp.concatenate([b[0], b[1], b[0]], axis=b_axis)
    return lax.dot_general(left, right, (dims, ((), ())), preferred_element_type=f32)


def spread_matrix():
    row, lane = iota((ROWS, 128), 0), iota((ROWS, 128), 1)
    first = (lane & 31) * TOK
    return ((row >= first) & (row < first + TOK) & (lane < 64)).astype(f32)


def prepare_kernel(p0, p1, p2, p3, hi_ref, lo_ref):
    for s, page_ref in enumerate((p0, p1, p2, p3)):
        hi_ref[s], lo_ref[s] = parts(page_ref[0])


def spread_kernel(q_ref, out_ref, rows_ref):
    for i in range(TOK):
        rows_ref[i : i + 1, :] = q_ref[i]
    out_ref[...] = jnp.broadcast_to(rows_ref[...][None], (QN, TOK, W))


def is_positive(me_ref, positive_ref):
    me = me_ref[0]
    base = me & 0b00100110
    index, lane = iota((NQ, 128), 0), iota((NQ, 128), 1)
    k = lane & 31
    query = ((k >> 3) << 6) + (((k >> 1) & 3) << 3) + (k & 1) + base
    chosen = jnp.dot(
        positive_ref[...].astype(f32), (index == query).astype(f32), precision=lax.Precision.HIGHEST,
        preferred_element_type=f32,
    )
    row = iota((8, 128), 0)
    x = (((me >> 1) & 3) - (row & 3)) & 3
    co = ((me >> 5) & 1) ^ (row >> 2)
    page = (me & 0b11011001) + (x << 1) + (co << 5)
    return page.astype(f32) == chosen


def chosen_kernel(me_ref, positive_ref, chosen_ref):
    chosen_ref[...] = is_positive(me_ref, positive_ref).astype(f32)


def score_kernel(
    q_ref, chosen_ref, hi_a, lo_a, hi_b, lo_b,
    whi_ref, wlo_ref, tot_ref, qt_ref, logits_ref, stats_ref, rows_ref,
):
    for k in range(QN):
        rows_ref[k * TOK : (k + 1) * TOK, :] = q_ref[k]
    qt = rows_ref[...].T
    qt_ref[...] = qt
    q_parts = parts(qt)
    for s in range(2 * XN):
        hi, lo = (hi_a, lo_a) if s < XN else (hi_b, lo_b)
        scores = product((hi[s % XN], lo[s % XN]), q_parts, ((1,), (0,)), 1, 0)
        tangent = jnp.tanh(scores * (1.0 / cap_value))
        grid = jnp.exp(tangent * (cap_value / sharpness_divisor))
        tot_ref[s : s + 1, :] = jnp.sum(grid, axis=0, keepdims=True)
        whi_ref[s], wlo_ref[s] = parts(grid * (1.0 - tangent * tangent))
    smooth = sharpness_divisor * jnp.log(tot_ref[...])
    logits = (logit_scale / TOK) * jnp.dot(
        smooth, spread_matrix(), precision=lax.Precision.HIGHEST, preferred_element_type=f32
    )
    logits_ref[...] = logits
    lane = iota((8, 128), 1)
    matched = jnp.where(chosen_ref[...] > 0.5, logits, 0.0)
    local = jnp.where(lane < 32, jnp.exp(logits), jnp.where(lane < 64, matched, 0.0))
    summed = jnp.sum(local, axis=0, keepdims=True)
    stats_ref[...] = jnp.broadcast_to(summed[None], stats_ref.shape)


def by_row(values):
    return lax.dot_general(
        jnp.where(iota((8, 128), 1) < 32, values, 0.0), spread_matrix(), (((1,), (1,)), ((), ())),
        precision=lax.Precision.HIGHEST, preferred_element_type=f32,
    )


def query_sums_kernel(
    logits_ref, chosen_ref, tot_ref, whi_ref, wlo_ref, hi_a, lo_a, hi_b, lo_b, out_ref, rows_ref
):
    scale = (logit_scale / TOK) / tot_ref[...]
    weighted = by_row(jnp.exp(logits_ref[...])) * scale
    matched = by_row(chosen_ref[...]) * scale
    totals = [jnp.zeros((W, ROWS), f32)] * 2
    for s in range(2 * XN):
        hi, lo = (hi_a, lo_a) if s < XN else (hi_b, lo_b)
        turned = [half[s % XN].astype(f32).T.astype(bf16) for half in (hi, lo)]
        terms = product(turned, (whi_ref[s], wlo_ref[s]), ((1,), (0,)), 1, 0)
        totals = [t + terms * f[s : s + 1, :] for t, f in zip(totals, (weighted, matched))]
    for start, total in zip((0, TOK), totals):
        rows_ref[...] = total.T
        for k in range(QN):
            out_ref[k, start : start + TOK, :] = rows_ref[k * TOK : (k + 1) * TOK, :]


def page_gradients(whi_ref, wlo_ref, qt, factors, first, out_ref):
    for s in range(XN):
        scaled = parts(qt * factors[first + s : first + s + 1, :])
        out_ref[s * PT : (s + 1) * PT, :] = product(
            (whi_ref[first + s], wlo_ref[first + s]), scaled, ((1,), (1,)), 1, 1
        )


def coefficient_kernel(
    stats_ref, logits_ref, chosen_ref, tot_ref, qt_ref, whi_ref, wlo_ref,
    out_ref, factors_ref, owner_ref,
):
    stats = jnp.sum(stats_ref[...], axis=0)
    lane = iota((1, 128), 1)
    totals = jnp.where(lane < 32, stats, 1.0)
    log_totals = jnp.log(totals)
    terms = jnp.where(
        lane < 32, log_totals + z_weight * log_totals * log_totals, jnp.where(lane < 64, -stats, 0.0)
    )
    loss = jnp.sum(terms, axis=1, keepdims=True) * (1.0 / NQ)
    out_ref[XN * PT :, :] = jnp.broadcast_to(loss, (8, 128))
    slope = 1.0 + 2.0 * z_weight * log_totals
    owner_ref[...] = slope / totals * (1.0 / NQ)
    coefficients = (slope * jnp.exp(logits_ref[...]) / totals - chosen_ref[...]) * (1.0 / NQ)
    factors = by_row(coefficients) * (logit_scale / TOK) / tot_ref[...]
    factors_ref[...] = factors
    page_gradients(whi_ref, wlo_ref, qt_ref[...], factors, XN, out_ref)


def own_gradient_kernel(factors_ref, qt_ref, whi_ref, wlo_ref, out_ref):
    page_gradients(whi_ref, wlo_ref, qt_ref[...], factors_ref[...], 0, out_ref)


def pair_kernel(mine_ref, loss_ref, theirs_ref, o0, o1, o2, o3):
    loss = loss_ref[...] + theirs_ref[XN * PT :, :]
    for s, out in enumerate((o0, o1, o2, o3)):
        rows = slice(s * PT, (s + 1) * PT)
        out[0:PT, :] = mine_ref[rows, :] + theirs_ref[rows, :]
        out[PT:, :] = loss


def final_kernel(me_ref, owner_ref, r0, r1, r2, r3, sums_ref, page_ref, loss_ref, slope_ref):
    total = (r0[...] + r2[...]) + (r1[...] + r3[...])
    page_ref[0] = total[0:PT]
    loss_ref[...] = total[PT : PT + 1, 0:1]
    me = me_ref[0]
    k = ((me >> 6) << 3) + (((me >> 3) & 3) << 1) + (me & 1)
    mine = jnp.where(iota((1, 128), 1) == k, owner_ref[...], 0.0)
    weight = jnp.sum(mine, axis=1, keepdims=True)
    sums = jnp.sum(sums_ref[...], axis=0)
    slope = sums[0:TOK] * weight - sums[TOK:] * (1.0 / NQ)
    for i in range(TOK):
        slope_ref[i] = slope[i : i + 1, :]


def call(kernel, out, scratch=(), scalars=0, flops=None):
    vmem = pl.BlockSpec(memory_space=pltpu.VMEM)

    def run(*args):
        specs = [pl.BlockSpec(memory_space=pltpu.SMEM)] * scalars + [vmem] * (len(args) - scalars)
        return pl.pallas_call(
            kernel,
            out_shape=[jax.ShapeDtypeStruct(s, d) for s, d in out],
            in_specs=specs,
            out_specs=[vmem] * len(out),
            scratch_shapes=list(scratch),
            compiler_params=pltpu.CompilerParams(vmem_limit_bytes=16 * 1024 * 1024),
            cost_estimate=flops and pl.CostEstimate(flops=flops, transcendentals=0, bytes_accessed=0),
        )(*args)

    return run


def moved(value, axis, step):
    n = SIZES[axis]
    return lax.ppermute(value, axis, [(i, (i + step) % n) for i in range(n)])


def shards(queries, pages, positive):
    me = lax.axis_index(AXES).astype(jnp.int32).reshape(1)
    positive = positive.reshape(1, NQ)
    own = [pages] + [moved(pages, "x", s) for s in range(1, XN)]
    other = [moved(page, "co", 1) for page in own]
    (spread,) = call(spread_kernel, [((QN, TOK, W), f32)], [pltpu.VMEM((TOK, W), f32)])(
        queries.transpose(1, 0, 2)
    )
    block = lax.all_to_all(spread, QUERY_AXES, 0, 0, tiled=True)

    prepare = call(prepare_kernel, [((XN, PT, W), bf16)] * 2, flops=PREPARE_FLOPS)
    hi_a, lo_a = prepare(*own)
    hi_b, lo_b = prepare(*other)
    (chosen,) = call(chosen_kernel, [((8, 128), f32)], scalars=1)(me, positive)
    weights = ((2 * XN, PT, ROWS), bf16)
    whi, wlo, tot, qt, logits, stats = call(
        score_kernel,
        [weights, weights, ((2 * XN, ROWS), f32), ((W, ROWS), f32), ((8, 128), f32), ((QN, 1, 128), f32)],
        [pltpu.VMEM((ROWS, W), f32)],
    )(block, chosen, hi_a, lo_a, hi_b, lo_b)
    stats = lax.all_to_all(stats, QUERY_AXES, 0, 0, tiled=True)
    (sums,) = call(query_sums_kernel, [((QN, 2 * TOK, W), f32)], [pltpu.VMEM((ROWS, W), f32)])(
        logits, chosen, tot, whi, wlo, hi_a, lo_a, hi_b, lo_b
    )
    sums = lax.all_to_all(sums, QUERY_AXES, 0, 0, tiled=True)
    theirs, factors, owner = call(
        coefficient_kernel, [((XN * PT + 8, W), f32), ((2 * XN, ROWS), f32), ((1, 128), f32)]
    )(stats, logits, chosen, tot, qt, whi, wlo)
    loss_rows = theirs[XN * PT :]
    theirs = moved(theirs, "co", 1)
    (mine,) = call(own_gradient_kernel, [((XN * PT, W), f32)])(factors, qt, whi, wlo)
    blocks = call(pair_kernel, [((PT + 8, W), f32)] * XN)(mine, loss_rows, theirs)
    blocks = [blocks[0]] + [moved(blocks[s], "x", -s) for s in range(1, XN)]
    page_grad, loss, slope = call(
        final_kernel, [((1, PT, W), f32), ((1, 1), f32), ((TOK, 1, W), f32)], scalars=1
    )(me, owner, *blocks, sums)
    return loss.reshape(()), slope.transpose(1, 0, 2), page_grad


def solution(mesh):
    finer = Mesh(mesh.devices.reshape(tuple(SIZES[a] for a in AXES)), AXES)
    placed = (P(AXES, None, None), P(AXES, None, None), P())
    return jax.shard_map(
        shards,
        mesh=finer,
        in_specs=placed,
        out_specs=(P(), P(AXES, None, None), P(AXES, None, None)),
        check_vma=False,
    )
```

time: 71.6 us -> 80.1 us (1.12)
  blocking collectives: 17.7 us -> 0 us
  local copies, waits for them, and re-layouts: 3.2 us -> 17.8 us
  waiting for transfers between devices: 10.5 us -> 17.1 us
  starting transfers between devices: 31.6 us -> 35.6 us
    all_to_all x1 -> x0, blocking collectives: 17.7 us -> none  [shards(): stats = lax.all_to_all(stats, QUERY_AXES, 0, 0, tiled=True)]
    unnamed x6 -> x54, local copies, waits for them, and re-layouts: 1.97 us -> 17.8 us
    ppermute x11, waiting for transfers between devices: 0.35 us -> 9.24 us  [moved(): return lax.ppermute(value, axis, [(i, (i + step) % n) for i in range(n)])]
    all_to_all x1 -> x2, starting transfers between devices: 3.87 us -> 11.8 us  [the longest x1 6.84 us: shards(): sums = lax.all_to_all(sums, QUERY_AXES, 0, 0, tiled=True)]
    all_to_all x1 -> x2, waiting for transfers between devices: 10.1 us -> 2.39 us  [the longest x1 2.39 us: shards(): stats = lax.all_to_all(stats, QUERY_AXES, 0, 0, tiled=True)]
    all_to_all x1, waiting for transfers between devices: 0.01 us -> 5.45 us  [shards(): block = lax.all_to_all(spread, QUERY_AXES, 0, 0, tiled=True)]
    ppermute x11, starting transfers between devices: 15.5 us -> 12.5 us  [moved(): return lax.ppermute(value, axis, [(i, (i + step) % n) for i in range(n)])]
    all_to_all x1, starting transfers between devices: 12.2 us -> 11.2 us  [shards(): block = lax.all_to_all(spread, QUERY_AXES, 0, 0, tiled=True)]
  transfers between devices with their start and end apart: 13 -> 14, of which waited for: 2 -> 6; matrix products, arithmetic and copies ran while one was open for 0% -> 0% of each run, Pallas kernels for 5% -> 6%
where the time goes in v2:
time: 80.1 us; the launch traced here: 79.3 us
  starting transfers between devices  35.6 us (44%)
  local copies, waits for them, and re-layouts  17.8 us (22%)
  waiting for transfers between devices  17.1 us (21%)
  Pallas kernels  8.08 us (10%)
  between operations  0.85 us (1%)
    unnamed x54, local copies, waits for them, and re-layouts  17.8 us
    ppermute x11, starting transfers between devices, moved(): return lax.ppermute(value, axis, [(i, (i + step) % n) for i in range(n)])  12.5 us
    all_to_all x1, starting transfers between devices, shards(): block = lax.all_to_all(spread, QUERY_AXES, 0, 0, tiled=True)  11.2 us
    ppermute x11, waiting for transfers between devices, moved(): return lax.ppermute(value, axis, [(i, (i + step) % n) for i in range(n)])  9.24 us
    pallas_call x10, Pallas kernels, run(): pl.pallas_call(kernel, out_shape=[jax.ShapeDtypeStruct(s, d) for s, d in...  8.08 us
    all_to_all x1, starting transfers between devices, shards(): sums = lax.all_to_all(sums, QUERY_AXES, 0, 0, tiled=True)  6.84 us
    all_to_all x1, waiting for transfers between devices, shards(): block = lax.all_to_all(spread, QUERY_AXES, 0, 0, tiled=True)  5.45 us
    all_to_all x1, starting transfers between devices, shards(): stats = lax.all_to_all(stats, QUERY_AXES, 0, 0, tiled=True)  4.99 us
  transfers between devices with their start and end apart: 14, of which 6 were waited for; matrix products, arithmetic and copies ran while one was open for 0% of the time, Pallas kernels for 6%

profile of v2, /device:TPU:1, one launch (start us, length us, event | category | flops | bytes accessed | tf_op | source)
XLA Modules:
  0.0 79.3 jit_solution(9766861695959530723)
XLA Ops:
  0.6 3.4 %collective-permute-start.2 = (f32[1,256,128]{2,1,0:T(8,128)}, f32[1,256,128]{2,1,0:T(8,128)S(1)}, u32[]{:S(2)}, u32[]{:S(2)}) collective-permute-start(f32[1,256,128]{2,1,0:T(8,128)} %p0.1), channel_id=1, source_target_pairs={{0,6},{2,0},{4,2},{6,4},{1,7},{3,1},{5,3},{7,5},{8,14},{10,8},{12,... | collective-permute-start | bytes 393224 | tf_op jit(solution)/shard_map/ppermute | solution.py:212
  4.0 0.5 collective-permute-start.1
  4.5 0.6 collective-permute-start
  5.1 1.5 %collective-permute-start.3 = (f32[1,256,128]{2,1,0:T(8,128)}, f32[1,256,128]{2,1,0:T(8,128)S(1)}, u32[]{:S(2)}, u32[]{:S(2)}) collective-permute-start(f32[1,256,128]{2,1,0:T(8,128)} %p0.1), channel_id=1, source_target_pairs={{0,32},{32,0},{1,33},{33,1},{2,34},{34,2},{3,35},{35,3},{4,36},{36... | collective-permute-start | bytes 393224 | tf_op jit(solution)/shard_map/ppermute | solution.py:212
  6.7 0.7 copy-done.22
  7.3 0.7 shard_map.58
  8.1 11.2 %all-to-all-start = ((f32[32,12,128]{2,1,0:T(8,128)}), f32[32,12,128]{2,1,0:T(8,128)S(1)}, u32[]{:S(2)}, u32[]{:S(2)}) async-start(f32[32,12,128]{2,1,0:T(8,128)} %shard_map.58), calls=%async_computation | async-start | bytes 524288 | tf_op jit(solution)/shard_map/all_to_all | solution.py:223
  19.3 0.0 copy-start.23
  19.3 0.7 copy-done.23
  20.0 0.2 shard_map.59.chosen_ref
  20.2 0.0 copy-start.16
  20.2 0.0 collective-permute-done.2.p3
  20.2 0.4 collective-permute-start.6
  20.5 0.0 collective-permute-done.1.p2
  20.6 0.2 collective-permute-start.5
  20.8 0.0 collective-permute-done.p1
  20.8 0.3 collective-permute-start.4
  21.1 0.9 %copy-done.26 = f32[1,256,128]{2,1,0:T(8,128)S(1)} copy-done((f32[1,256,128]{2,1,0:T(8,128)S(1)}, f32[1,256,128]{2,1,0:T(8,128)}, u32[]{:S(2)}) %copy-start.26) | copy-done | bytes 131096
  22.0 0.1 shard_map.60
  22.0 0.7 copy-done.1
  22.7 0.7 copy-done.4
  23.5 0.0 collective-permute-done.3.p0
  23.5 0.0 collective-permute-done.6.p3
  23.5 0.0 collective-permute-done.5.p2
  23.5 0.0 collective-permute-done.4.p1
  23.5 0.1 shard_map.61
  23.5 0.7 copy-done.7
  24.2 0.7 copy-done.10
  25.0 5.4 %all-to-all-done.q_ref = f32[32,12,128]{2,1,0:T(8,128)S(1)} async-done(((f32[32,12,128]{2,1,0:T(8,128)}), f32[32,12,128]{2,1,0:T(8,128)S(1)}, u32[]{:S(2)}, u32[]{:S(2)}) %all-to-all-start) | async-done | bytes 196640 | tf_op jit(solution)/shard_map/all_to_all | solution.py:223
  30.4 0.9 %copy-done.2 = bf16[4,256,128]{2,1,0:T(8,128)(2,1)S(1)} copy-done((bf16[4,256,128]{2,1,0:T(8,128)(2,1)S(1)}, bf16[4,256,128]{2,1,0:T(8,128)(2,1)}, u32[]{:S(2)}) %copy-start.2) | copy-done | bytes 262168
  31.4 0.9 %copy-done.5 = bf16[4,256,128]{2,1,0:T(8,128)(2,1)S(1)} copy-done((bf16[4,256,128]{2,1,0:T(8,128)(2,1)S(1)}, bf16[4,256,128]{2,1,0:T(8,128)(2,1)}, u32[]{:S(2)}) %copy-start.5) | copy-done | bytes 262168
  32.3 0.9 %copy-done.8 = bf16[4,256,128]{2,1,0:T(8,128)(2,1)S(1)} copy-done((bf16[4,256,128]{2,1,0:T(8,128)(2,1)S(1)}, bf16[4,256,128]{2,1,0:T(8,128)(2,1)}, u32[]{:S(2)}) %copy-start.8) | copy-done | bytes 262168
  33.3 0.9 %copy-done.11 = bf16[4,256,128]{2,1,0:T(8,128)(2,1)S(1)} copy-done((bf16[4,256,128]{2,1,0:T(8,128)(2,1)S(1)}, bf16[4,256,128]{2,1,0:T(8,128)(2,1)}, u32[]{:S(2)}) %copy-start.11) | copy-done | bytes 262168
  34.2 2.8 %shard_map.62 = (bf16[8,256,384]{2,1,0:T(8,128)(2,1)S(1)}, bf16[8,256,384]{2,1,0:T(8,128)(2,1)S(1)}, f32[8,384]{1,0:T(8,128)S(1)}, f32[128,384]{1,0:T(8,128)S(1)...) custom-call(f32[32,12,128]{2,1,0:T(8,128)S(1)} %all-to-all-done.q_ref, f32[8,128]{1,0:T(8,128)S(1)} %shard_map.59.chosen_ref, ...), custom_call_target="tpu_custom_call" | custom-call | tf_op jit(solution)/shard_map/pallas_call | solution.py:197
  37.0 0.7 copy-done.13
  37.7 5.0 %all-to-all-start.1 = ((f32[32,1,128]{2,1,0:T(1,128)}), f32[32,1,128]{2,1,0:T(1,128)S(1)}, u32[]{:S(2)}, u32[]{:S(2)}) async-start(f32[32,1,128]{2,1,0:T(1,128)} %get-tuple-element.27), calls=%async_computation.1 | async-start | bytes 32768 | tf_op jit(solution)/shard_map/all_to_all | solution.py:235
  42.7 0.9 %copy-done.3 = bf16[4,256,128]{2,1,0:T(8,128)(2,1)S(1)} copy-done((bf16[4,256,128]{2,1,0:T(8,128)(2,1)S(1)}, bf16[4,256,128]{2,1,0:T(8,128)(2,1)}, u32[]{:S(2)}) %copy-start.3) | copy-done | bytes 262168
  43.6 0.9 %copy-done.6 = bf16[4,256,128]{2,1,0:T(8,128)(2,1)S(1)} copy-done((bf16[4,256,128]{2,1,0:T(8,128)(2,1)S(1)}, bf16[4,256,128]{2,1,0:T(8,128)(2,1)}, u32[]{:S(2)}) %copy-start.6) | copy-done | bytes 262168
  44.6 0.9 %copy-done.9 = bf16[4,256,128]{2,1,0:T(8,128)(2,1)S(1)} copy-done((bf16[4,256,128]{2,1,0:T(8,128)(2,1)S(1)}, bf16[4,256,128]{2,1,0:T(8,128)(2,1)}, u32[]{:S(2)}) %copy-start.9) | copy-done | bytes 262168
  45.5 0.9 %copy-done.12 = bf16[4,256,128]{2,1,0:T(8,128)(2,1)S(1)} copy-done((bf16[4,256,128]{2,1,0:T(8,128)(2,1)S(1)}, bf16[4,256,128]{2,1,0:T(8,128)(2,1)}, u32[]{:S(2)}) %copy-start.12) | copy-done | bytes 262168
  46.5 1.6 %shard_map.66 = f32[32,24,128]{2,1,0:T(8,128)S(1)} custom-call(f32[8,128]{1,0:T(8,128)S(1)} %get-tuple-element.28.logits_ref, f32[8,128]{1,0:T(8,128)S(1)} %shard_map.59.chosen_ref, f32[8,384]{1,0:T(8,128)S(1)} %get-tuple-element.29.tot_ref, bf16[8,256,384]{2,1,0:T(8,128)(2,1)S(1)} %get-tuple-element.31.whi_ref, ...), custom_call_target="tpu_custom_call" | custom-call | tf_op jit(solution)/shard_map/pallas_call | solution.py:197
  48.1 0.8 copy-done
  48.8 2.4 %all-to-all-done.1.stats_ref = f32[32,1,128]{2,1,0:T(1,128)S(1)} async-done(((f32[32,1,128]{2,1,0:T(1,128)}), f32[32,1,128]{2,1,0:T(1,128)S(1)}, u32[]{:S(2)}, u32[]{:S(2)}) %all-to-all-start.1) | async-done | bytes 16416 | tf_op jit(solution)/shard_map/all_to_all | solution.py:235
  51.2 6.8 %all-to-all-start.2 = ((f32[32,24,128]{2,1,0:T(8,128)}), f32[32,24,128]{2,1,0:T(8,128)S(1)}, u32[]{:S(2)}, u32[]{:S(2)}) async-start(f32[32,24,128]{2,1,0:T(8,128)} %copy-done), calls=%async_computation.2 | async-start | bytes 786432 | tf_op jit(solution)/shard_map/all_to_all | solution.py:239
  58.1 0.0 copy-start.14
  58.1 0.9 %copy-done.14 = f32[128,384]{1,0:T(8,128)S(1)} copy-done((f32[128,384]{1,0:T(8,128)S(1)}, f32[128,384]{1,0:T(8,128)}, u32[]{:S(2)}) %copy-start.14) | copy-done | bytes 196632
  59.0 0.7 copy-done.17
  59.7 0.7 copy-done.19
  60.4 0.7 copy-done.21
  61.1 1.2 %shard_map.63 = (f32[1032,128]{1,0:T(8,128)S(1)}, f32[8,384]{1,0:T(8,128)S(1)}, f32[1,128]{1,0:T(1,128)S(1)}) custom-call(f32[32,1,128]{2,1,0:T(1,128)S(1)} %all-to-all-done.1.stats_ref, f32[8,128]{1,0:T(8,128)S(1)} %copy-done.21, f32[8,128]{1,0:T(8,128)S(1)} %copy-done.17, f32[8,384]{1,0:T(8,128)S(1)} %copy-done.19, f32[128,384]{1,0:T(8,128)S(1)} %copy-done.14, ...), custom_call_target="tpu_custom_call" | custom-call | tf_op jit(solution)/shard_map/pallas_call | solution.py:197
  62.3 0.0 copy-start.24
  62.3 2.2 %collective-permute-start.7 = (f32[1032,128]{1,0:T(8,128)S(1)}, f32[1032,128]{1,0:T(8,128)S(1)}, u32[]{:S(2)}, u32[]{:S(2)}) collective-permute-start(f32[1032,128]{1,0:T(8,128)S(1)} %get-tuple-element.35), channel_id=1, source_target_pairs={{0,32},{32,0},{1,33},{33,1},{2,34},{34,2},{3,35},{35,3},{4,36},{36... | collective-permute-start | bytes 1585160 | tf_op jit(solution)/shard_map/ppermute | solution.py:212
  64.5 0.8 shard_map.64.mine_ref
  65.3 0.7 collective-permute-done.7.theirs_ref
  66.0 0.1 shard_map.65
  66.1 2.1 %collective-permute-start.8 = (f32[264,128]{1,0:T(8,128)S(1)}, f32[264,128]{1,0:T(8,128)S(1)}, u32[]{:S(2)}, u32[]{:S(2)}) collective-permute-start(f32[264,128]{1,0:T(8,128)S(1)} %get-tuple-element.37), channel_id=1, source_target_pairs={{0,6},{2,0},{4,2},{6,4},{1,7},{3,1},{5,3},{7,5},{8,14},{10,8},{12,... | collective-permute-start | bytes 405512 | tf_op jit(solution)/shard_map/ppermute | solution.py:212
  68.2 1.2 %collective-permute-start.9 = (f32[264,128]{1,0:T(8,128)S(1)}, f32[264,128]{1,0:T(8,128)S(1)}, u32[]{:S(2)}, u32[]{:S(2)}) collective-permute-start(f32[264,128]{1,0:T(8,128)S(1)} %get-tuple-element.38), channel_id=1, source_target_pairs={{0,4},{2,6},{4,0},{6,2},{1,5},{3,7},{5,1},{7,3},{8,12},{10,14},{12... | collective-permute-start | bytes 405512 | tf_op jit(solution)/shard_map/ppermute | solution.py:212
  69.5 0.0 collective-permute-start.10
  69.5 1.6 %collective-permute-done.8.r1 = f32[264,128]{1,0:T(8,128)S(1)} collective-permute-done((f32[264,128]{1,0:T(8,128)S(1)}, f32[264,128]{1,0:T(8,128)S(1)}, u32[]{:S(2)}, u32[]{:S(2)}) %collective-permute-start.8) | collective-permute-done | bytes 135200 | tf_op jit(solution)/shard_map/ppermute | solution.py:212
  71.1 3.1 %collective-permute-done.9.r2 = f32[264,128]{1,0:T(8,128)S(1)} collective-permute-done((f32[264,128]{1,0:T(8,128)S(1)}, f32[264,128]{1,0:T(8,128)S(1)}, u32[]{:S(2)}, u32[]{:S(2)}) %collective-permute-start.9) | collective-permute-done | bytes 135200 | tf_op jit(solution)/shard_map/ppermute | solution.py:212
  74.2 3.7 %collective-permute-done.10.r3 = f32[264,128]{1,0:T(8,128)S(1)} collective-permute-done((f32[264,128]{1,0:T(8,128)S(1)}, f32[264,128]{1,0:T(8,128)S(1)}, u32[]{:S(2)}, u32[]{:S(2)}) %collective-permute-start.10) | collective-permute-done | bytes 135200 | tf_op jit(solution)/shard_map/ppermute | solution.py:212
  78.0 0.0 all-to-all-done.2.sums_ref
  78.0 0.7 copy-done.25
  78.6 0.7 shard_map.67
  (29 shorter events, 0.1 us)
Async XLA Ops:
  0.6 19.5 %collective-permute-start.2 = (f32[1,256,128]{2,1,0:T(8,128)}, f32[1,256,128]{2,1,0:T(8,128)S(1)}, u32[]{:S(2)}, u32[]{:S(2)}) collective-permute-start(f32[1,256,128]{2,1,0:T(8,128)} %p0.1), channel_id=1, source_target_pairs={{0,6},{2,0},{4,2},{6,4},{1,7},{3,1},{5,3},{7,5},{8,14},{10,8},{12,... | collective-permute-start | bytes 393224 | tf_op jit(solution)/shard_map/ppermute | solution.py:212
  4.0 16.5 %collective-permute-start.1 = (f32[1,256,128]{2,1,0:T(8,128)}, f32[1,256,128]{2,1,0:T(8,128)S(1)}, u32[]{:S(2)}, u32[]{:S(2)}) collective-permute-start(f32[1,256,128]{2,1,0:T(8,128)} %p0.1), channel_id=1, source_target_pairs={{0,4},{2,6},{4,0},{6,2},{1,5},{3,7},{5,1},{7,3},{8,12},{10,14},{12... | collective-permute-start | bytes 393224 | tf_op jit(solution)/shard_map/ppermute | solution.py:212
  4.5 16.2 %collective-permute-start = (f32[1,256,128]{2,1,0:T(8,128)}, f32[1,256,128]{2,1,0:T(8,128)S(1)}, u32[]{:S(2)}, u32[]{:S(2)}) collective-permute-start(f32[1,256,128]{2,1,0:T(8,128)} %p0.1), channel_id=1, source_target_pairs={{0,2},{2,4},{4,6},{6,0},{1,3},{3,5},{5,7},{7,1},{8,10},{10,12},{12... | collective-permute-start | bytes 393224 | tf_op jit(solution)/shard_map/ppermute | solution.py:212
  5.1 18.3 %collective-permute-start.3 = (f32[1,256,128]{2,1,0:T(8,128)}, f32[1,256,128]{2,1,0:T(8,128)S(1)}, u32[]{:S(2)}, u32[]{:S(2)}) collective-permute-start(f32[1,256,128]{2,1,0:T(8,128)} %p0.1), channel_id=1, source_target_pairs={{0,32},{32,0},{1,33},{33,1},{2,34},{34,2},{3,35},{35,3},{4,36},{36... | collective-permute-start | bytes 393224 | tf_op jit(solution)/shard_map/ppermute | solution.py:212
  6.7 0.7 copy-start.22
  8.1 22.3 %all-to-all-start = ((f32[32,12,128]{2,1,0:T(8,128)}), f32[32,12,128]{2,1,0:T(8,128)S(1)}, u32[]{:S(2)}, u32[]{:S(2)}) async-start(f32[32,12,128]{2,1,0:T(8,128)} %shard_map.58), calls=%async_computation | async-start | bytes 524288 | tf_op jit(solution)/shard_map/all_to_all | solution.py:223
  19.3 0.7 copy-start.23
  20.2 22.5 %copy-start.16 = (f32[8,128]{1,0:T(8,128)}, f32[8,128]{1,0:T(8,128)S(1)}, u32[]{:S(2)}) copy-start(f32[8,128]{1,0:T(8,128)S(1)} %shard_map.59.chosen_ref) | copy-start | bytes 12292
  20.2 3.3 %collective-permute-start.6 = (f32[1,256,128]{2,1,0:T(8,128)S(1)}, f32[1,256,128]{2,1,0:T(8,128)S(1)}, u32[]{:S(2)}, u32[]{:S(2)}) collective-permute-start(f32[1,256,128]{2,1,0:T(8,128)S(1)} %collective-permute-done.2.p3), channel_id=1, source_target_pairs={{0,32},{32,0},{1,33},{33,1},{2,34},{34,2},{3,35},{35,3},{4,36},{36... | collective-permute-start | bytes 393224 | tf_op jit(solution)/shard_map/ppermute | solution.py:212
  20.6 2.9 %collective-permute-start.5 = (f32[1,256,128]{2,1,0:T(8,128)S(1)}, f32[1,256,128]{2,1,0:T(8,128)S(1)}, u32[]{:S(2)}, u32[]{:S(2)}) collective-permute-start(f32[1,256,128]{2,1,0:T(8,128)S(1)} %collective-permute-done.1.p2), channel_id=1, source_target_pairs={{0,32},{32,0},{1,33},{33,1},{2,34},{34,2},{3,35},{35,3},{4,36},{36... | collective-permute-start | bytes 393224 | tf_op jit(solution)/shard_map/ppermute | solution.py:212
  20.8 2.7 %collective-permute-start.4 = (f32[1,256,128]{2,1,0:T(8,128)S(1)}, f32[1,256,128]{2,1,0:T(8,128)S(1)}, u32[]{:S(2)}, u32[]{:S(2)}) collective-permute-start(f32[1,256,128]{2,1,0:T(8,128)S(1)} %collective-permute-done.p1), channel_id=1, source_target_pairs={{0,32},{32,0},{1,33},{33,1},{2,34},{34,2},{3,35},{35,3},{4,36},{36... | collective-permute-start | bytes 393224 | tf_op jit(solution)/shard_map/ppermute | solution.py:212
  21.1 0.9 %copy-start.26 = (f32[1,256,128]{2,1,0:T(8,128)S(1)}, f32[1,256,128]{2,1,0:T(8,128)}, u32[]{:S(2)}) copy-start(f32[1,256,128]{2,1,0:T(8,128)} %p0.1) | copy-start | bytes 393220
  22.0 0.7 copy-start.1
  22.7 0.7 copy-start.4
  23.5 0.7 copy-start.7
  24.2 0.7 copy-start.10
  30.4 1.0 %copy-start.2 = (bf16[4,256,128]{2,1,0:T(8,128)(2,1)S(1)}, bf16[4,256,128]{2,1,0:T(8,128)(2,1)}, u32[]{:S(2)}) copy-start(bf16[4,256,128]{2,1,0:T(8,128)(2,1)} %copy-done.1) | copy-start | bytes 786436
  31.3 0.9 %copy-start.5 = (bf16[4,256,128]{2,1,0:T(8,128)(2,1)S(1)}, bf16[4,256,128]{2,1,0:T(8,128)(2,1)}, u32[]{:S(2)}) copy-start(bf16[4,256,128]{2,1,0:T(8,128)(2,1)} %copy-done.4) | copy-start | bytes 786436
  32.3 0.9 %copy-start.8 = (bf16[4,256,128]{2,1,0:T(8,128)(2,1)S(1)}, bf16[4,256,128]{2,1,0:T(8,128)(2,1)}, u32[]{:S(2)}) copy-start(bf16[4,256,128]{2,1,0:T(8,128)(2,1)} %copy-done.7) | copy-start | bytes 786436
  33.3 0.9 %copy-start.11 = (bf16[4,256,128]{2,1,0:T(8,128)(2,1)S(1)}, bf16[4,256,128]{2,1,0:T(8,128)(2,1)}, u32[]{:S(2)}) copy-start(bf16[4,256,128]{2,1,0:T(8,128)(2,1)} %copy-done.10) | copy-start | bytes 786436
  37.0 0.7 copy-start.13
  37.7 10.4 %copy-start.18 = (f32[8,384]{1,0:T(8,128)}, f32[8,384]{1,0:T(8,128)S(1)}, u32[]{:S(2)}) copy-start(f32[8,384]{1,0:T(8,128)S(1)} %get-tuple-element.29.tot_ref) | copy-start | bytes 36868
  37.7 10.4 %copy-start.20 = (f32[8,128]{1,0:T(8,128)}, f32[8,128]{1,0:T(8,128)S(1)}, u32[]{:S(2)}) copy-start(f32[8,128]{1,0:T(8,128)S(1)} %get-tuple-element.28.logits_ref) | copy-start | bytes 12292
  37.7 13.6 %all-to-all-start.1 = ((f32[32,1,128]{2,1,0:T(1,128)}), f32[32,1,128]{2,1,0:T(1,128)S(1)}, u32[]{:S(2)}, u32[]{:S(2)}) async-start(f32[32,1,128]{2,1,0:T(1,128)} %get-tuple-element.27), calls=%async_computation.1 | async-start | bytes 32768 | tf_op jit(solution)/shard_map/all_to_all | solution.py:235
  42.7 1.0 %copy-start.3 = (bf16[4,256,128]{2,1,0:T(8,128)(2,1)S(1)}, bf16[4,256,128]{2,1,0:T(8,128)(2,1)}, u32[]{:S(2)}) copy-start(bf16[4,256,128]{2,1,0:T(8,128)(2,1)} %copy-done.1) | copy-start | bytes 786436
  43.6 0.9 %copy-start.6 = (bf16[4,256,128]{2,1,0:T(8,128)(2,1)S(1)}, bf16[4,256,128]{2,1,0:T(8,128)(2,1)}, u32[]{:S(2)}) copy-start(bf16[4,256,128]{2,1,0:T(8,128)(2,1)} %copy-done.4) | copy-start | bytes 786436
  44.6 0.9 %copy-start.9 = (bf16[4,256,128]{2,1,0:T(8,128)(2,1)S(1)}, bf16[4,256,128]{2,1,0:T(8,128)(2,1)}, u32[]{:S(2)}) copy-start(bf16[4,256,128]{2,1,0:T(8,128)(2,1)} %copy-done.7) | copy-start | bytes 786436
  45.5 0.9 %copy-start.12 = (bf16[4,256,128]{2,1,0:T(8,128)(2,1)S(1)}, bf16[4,256,128]{2,1,0:T(8,128)(2,1)}, u32[]{:S(2)}) copy-start(bf16[4,256,128]{2,1,0:T(8,128)(2,1)} %copy-done.10) | copy-start | bytes 786436
  48.1 0.8 copy-start
  51.2 26.7 %all-to-all-start.2 = ((f32[32,24,128]{2,1,0:T(8,128)}), f32[32,24,128]{2,1,0:T(8,128)S(1)}, u32[]{:S(2)}, u32[]{:S(2)}) async-start(f32[32,24,128]{2,1,0:T(8,128)} %copy-done), calls=%async_computation.2 | async-start | bytes 786432 | tf_op jit(solution)/shard_map/all_to_all | solution.py:239
  58.1 0.9 %copy-start.14 = (f32[128,384]{1,0:T(8,128)S(1)}, f32[128,384]{1,0:T(8,128)}, u32[]{:S(2)}) copy-start(f32[128,384]{1,0:T(8,128)} %copy-done.13) | copy-start | bytes 589828
  59.0 0.7 copy-start.17
  59.7 0.7 copy-start.19
  60.4 0.7 copy-start.21
  61.1 3.4 %copy-start.15 = (f32[128,384]{1,0:T(8,128)S(1)}, f32[128,384]{1,0:T(8,128)}, u32[]{:S(2)}) copy-start(f32[128,384]{1,0:T(8,128)} %copy-done.13) | copy-start | bytes 589828
  62.3 3.0 %copy-start.24 = (f32[1,128]{1,0:T(1,128)}, f32[1,128]{1,0:T(1,128)S(1)}, u32[]{:S(2)}) copy-start(f32[1,128]{1,0:T(1,128)S(1)} %get-tuple-element.33.owner_ref) | copy-start | bytes 1540
  62.3 3.8 %collective-permute-start.7 = (f32[1032,128]{1,0:T(8,128)S(1)}, f32[1032,128]{1,0:T(8,128)S(1)}, u32[]{:S(2)}, u32[]{:S(2)}) collective-permute-start(f32[1032,128]{1,0:T(8,128)S(1)} %get-tuple-element.35), channel_id=1, source_target_pairs={{0,32},{32,0},{1,33},{33,1},{2,34},{34,2},{3,35},{35,3},{4,36},{36... | collective-permute-start | bytes 1585160 | tf_op jit(solution)/shard_map/ppermute | solution.py:212
  66.1 5.0 %collective-permute-start.8 = (f32[264,128]{1,0:T(8,128)S(1)}, f32[264,128]{1,0:T(8,128)S(1)}, u32[]{:S(2)}, u32[]{:S(2)}) collective-permute-start(f32[264,128]{1,0:T(8,128)S(1)} %get-tuple-element.37), channel_id=1, source_target_pairs={{0,6},{2,0},{4,2},{6,4},{1,7},{3,1},{5,3},{7,5},{8,14},{10,8},{12,... | collective-permute-start | bytes 405512 | tf_op jit(solution)/shard_map/ppermute | solution.py:212
  68.2 6.0 %collective-permute-start.9 = (f32[264,128]{1,0:T(8,128)S(1)}, f32[264,128]{1,0:T(8,128)S(1)}, u32[]{:S(2)}, u32[]{:S(2)}) collective-permute-start(f32[264,128]{1,0:T(8,128)S(1)} %get-tuple-element.38), channel_id=1, source_target_pairs={{0,4},{2,6},{4,0},{6,2},{1,5},{3,7},{5,1},{7,3},{8,12},{10,14},{12... | collective-permute-start | bytes 405512 | tf_op jit(solution)/shard_map/ppermute | solution.py:212
  69.5 8.5 %collective-permute-start.10 = (f32[264,128]{1,0:T(8,128)S(1)}, f32[264,128]{1,0:T(8,128)S(1)}, u32[]{:S(2)}, u32[]{:S(2)}) collective-permute-start(f32[264,128]{1,0:T(8,128)S(1)} %get-tuple-element.39), channel_id=1, source_target_pairs={{0,2},{2,4},{4,6},{6,0},{1,3},{3,5},{5,7},{7,1},{8,10},{10,12},{12... | collective-permute-start | bytes 405512 | tf_op jit(solution)/shard_map/ppermute | solution.py:212
  78.0 0.7 copy-start.25

commit v3 on v2

v3 whole, which is shorter than its diff:
```python
import itertools

import jax
import jax.numpy as jnp
from jax import lax
from jax.experimental import pallas as pl
from jax.experimental.pallas import tpu as pltpu
from jax.sharding import Mesh
from jax.sharding import PartitionSpec as P

AXES = ("za", "co", "y", "x", "zb")
SIZES = dict(za=4, co=2, y=4, x=4, zb=2)
QUERY_AXES = ("za", "y", "zb")
QN = 32
XN = 4
TOK = 12
ROWS = QN * TOK
PT = 256
W = 128
NQ = 256

cap_value = 4.0
sharpness_divisor = 0.25
logit_scale = 8.0
z_weight = 0.001
PIECE = 2 * TOK + 1
f32 = jnp.float32
bf16 = jnp.bfloat16


def iota(shape, dim):
    return lax.broadcasted_iota(jnp.int32, shape, dim)


def parts(x):
    high = x.astype(bf16)
    return high, (x - high.astype(f32)).astype(bf16)


def product(a, b, dims, a_axis, b_axis):
    left = jnp.concatenate([a[0], a[0], a[1]], axis=a_axis)
    right = jnp.concatenate([b[0], b[1], b[0]], axis=b_axis)
    return lax.dot_general(left, right, (dims, ((), ())), preferred_element_type=f32)


def spread_matrix():
    row, lane = iota((ROWS, 128), 0), iota((ROWS, 128), 1)
    first = (lane & 31) * TOK
    return ((row >= first) & (row < first + TOK) & (lane < 64)).astype(f32)


def is_positive(me_ref, positive_ref):
    me = me_ref[0]
    base = me & 0b00100110
    index, lane = iota((NQ, 128), 0), iota((NQ, 128), 1)
    k = lane & 31
    query = ((k >> 3) << 6) + (((k >> 1) & 3) << 3) + (k & 1) + base
    chosen = jnp.dot(
        positive_ref[...].astype(f32), (index == query).astype(f32), precision=lax.Precision.HIGHEST,
        preferred_element_type=f32,
    )
    row = iota((8, 128), 0)
    x = (((me >> 1) & 3) - (row & 3)) & 3
    co = ((me >> 5) & 1) ^ (row >> 2)
    page = (me & 0b11011001) + (x << 1) + (co << 5)
    return page.astype(f32) == chosen


def by_row(values):
    return lax.dot_general(
        jnp.where(iota((8, 128), 1) < 32, values, 0.0), spread_matrix(), (((1,), (1,)), ((), ())),
        precision=lax.Precision.HIGHEST, preferred_element_type=f32,
    )


def score_kernel(
    me_ref, own_hbm, positive_hbm, q_ref, p1, p2, p3, p4, p5, p6, p7,
    whi_ref, wlo_ref, qt_ref, logits_ref, scale_ref, chosen_ref, sums_ref,
    tot_ref, rows_ref, p0, positive_ref, own_sem, positive_sem,
):
    own_copy = pltpu.make_async_copy(own_hbm, p0, own_sem)
    positive_copy = pltpu.make_async_copy(positive_hbm, positive_ref, positive_sem)
    own_copy.start()
    positive_copy.start()
    qt = q_ref[...].T
    qt_ref[...] = qt
    q_parts = parts(qt)
    pages = (p0, p1, p2, p3, p4, p5, p6, p7)
    for s, page_ref in [*enumerate(pages)][1:] + [(0, p0)]:
        if s == 0:
            own_copy.wait()
        scores = product(parts(page_ref[0]), q_parts, ((1,), (0,)), 1, 0)
        tangent = jnp.tanh(scores * (1.0 / cap_value))
        grid = jnp.exp(tangent * (cap_value / sharpness_divisor))
        tot_ref[s : s + 1, :] = jnp.sum(grid, axis=0, keepdims=True)
        whi_ref[s], wlo_ref[s] = parts(grid * (1.0 - tangent * tangent))
    smooth = sharpness_divisor * jnp.log(tot_ref[...])
    logits = (logit_scale / TOK) * jnp.dot(
        smooth, spread_matrix(), precision=lax.Precision.HIGHEST, preferred_element_type=f32
    )
    logits_ref[...] = logits
    positive_copy.wait()
    chosen = is_positive(me_ref, positive_ref)
    chosen_ref[...] = chosen.astype(f32)
    scale = (logit_scale / TOK) / tot_ref[...]
    scale_ref[...] = scale
    lane = iota((8, 128), 1)
    exponential = jnp.exp(logits)
    matched = jnp.where(chosen, logits, 0.0)
    local = jnp.where(lane < 32, exponential, jnp.where(lane < 64, matched, 0.0))
    stats = jnp.sum(local, axis=0, keepdims=True)

    weighted = by_row(exponential) * scale
    matched = by_row(chosen.astype(f32)) * scale
    totals = [jnp.zeros((W, ROWS), f32)] * 2
    for s, page_ref in enumerate(pages):
        terms = product(parts(page_ref[0].T), (whi_ref[s], wlo_ref[s]), ((1,), (0,)), 1, 0)
        totals = [t + terms * f[s : s + 1, :] for t, f in zip(totals, (weighted, matched))]
    for start, total in zip((0, TOK), totals):
        rows_ref[...] = total.T
        for k in range(QN):
            first = k * PIECE + start
            sums_ref[first : first + TOK, :] = rows_ref[k * TOK : (k + 1) * TOK, :]
    for k in range(QN):
        sums_ref[k * PIECE + 2 * TOK : (k + 1) * PIECE, :] = stats


def page_gradients(whi_ref, wlo_ref, qt, factors, first, out_ref):
    for s in range(XN):
        scaled = parts(qt * factors[first + s : first + s + 1, :])
        out_ref[s * PT : (s + 1) * PT, :] = product(
            (whi_ref[first + s], wlo_ref[first + s]), scaled, ((1,), (1,)), 1, 1
        )


def coefficient_kernel(
    sums_ref, logits_ref, chosen_ref, scale_ref, qt_ref, whi_ref, wlo_ref,
    out_ref, factors_ref, owner_ref,
):
    stats = jnp.zeros((1, 128), f32)
    for k in range(QN):
        stats = stats + sums_ref[k * PIECE + 2 * TOK : (k + 1) * PIECE, :]
    lane = iota((1, 128), 1)
    totals = jnp.where(lane < 32, stats, 1.0)
    log_totals = jnp.log(totals)
    terms = jnp.where(
        lane < 32, log_totals + z_weight * log_totals * log_totals, jnp.where(lane < 64, -stats, 0.0)
    )
    loss = jnp.sum(terms, axis=1, keepdims=True) * (1.0 / NQ)
    out_ref[XN * PT :, :] = jnp.broadcast_to(loss, (8, 128))
    slope = 1.0 + 2.0 * z_weight * log_totals
    owner_ref[...] = slope / totals * (1.0 / NQ)
    coefficients = (slope * jnp.exp(logits_ref[...]) / totals - chosen_ref[...]) * (1.0 / NQ)
    factors = by_row(coefficients) * scale_ref[...]
    factors_ref[...] = factors
    page_gradients(whi_ref, wlo_ref, qt_ref[...], factors, XN, out_ref)


def own_gradient_kernel(factors_ref, qt_ref, whi_ref, wlo_ref, out_ref):
    page_gradients(whi_ref, wlo_ref, qt_ref[...], factors_ref[...], 0, out_ref)


def pair_kernel(mine_ref, loss_ref, theirs_ref, o0, o1, o2, o3):
    loss = loss_ref[...] + theirs_ref[XN * PT :, :]
    for s, out in enumerate((o0, o1, o2, o3)):
        rows = slice(s * PT, (s + 1) * PT)
        out[0:PT, :] = mine_ref[rows, :] + theirs_ref[rows, :]
        out[PT:, :] = loss


def final_kernel(me_ref, owner_ref, r0, r1, r2, r3, sums_ref, page_ref, loss_ref, slope_ref):
    total = (r0[...] + r2[...]) + (r1[...] + r3[...])
    page_ref[0] = total[0:PT]
    loss_ref[...] = total[PT : PT + 1, 0:1]
    me = me_ref[0]
    k = ((me >> 6) << 3) + (((me >> 3) & 3) << 1) + (me & 1)
    mine = jnp.where(iota((1, 128), 1) == k, owner_ref[...], 0.0)
    weight = jnp.sum(mine, axis=1, keepdims=True)
    sums = jnp.zeros((2 * TOK, W), f32)
    for k in range(QN):
        sums = sums + sums_ref[k * PIECE : k * PIECE + 2 * TOK, :]
    slope = sums[0:TOK] * weight - sums[TOK:] * (1.0 / NQ)
    for i in range(TOK):
        slope_ref[i] = slope[i : i + 1, :]


def call(kernel, out, scratch=(), scalars=0, anywhere=0):
    vmem = pl.BlockSpec(memory_space=pltpu.VMEM)

    def run(*args):
        specs = [pl.BlockSpec(memory_space=pltpu.SMEM)] * scalars
        specs += [pl.BlockSpec(memory_space=pltpu.HBM)] * anywhere
        specs += [vmem] * (len(args) - scalars - anywhere)
        return pl.pallas_call(
            kernel,
            out_shape=[jax.ShapeDtypeStruct(s, d) for s, d in out],
            in_specs=specs,
            out_specs=[vmem] * len(out),
            scratch_shapes=list(scratch),
            compiler_params=pltpu.CompilerParams(vmem_limit_bytes=16 * 1024 * 1024),
        )(*args)

    return run


def moved(value, axis, step):
    n = SIZES[axis]
    return lax.ppermute(value, axis, [(i, (i + step) % n) for i in range(n)])


def shards(queries, pages, positive):
    me = lax.axis_index(AXES).astype(jnp.int32).reshape(1)
    positive = positive.reshape(1, NQ)
    rows = lax.optimization_barrier(queries.transpose(1, 0, 2))
    spread = jnp.broadcast_to(rows, (QN, TOK, 1, W))
    block = lax.all_to_all(spread, QUERY_AXES, 0, 0, tiled=True).reshape(ROWS, W)
    own = [pages] + [moved(pages, "x", s) for s in range(1, XN)]
    other = [moved(page, "co", 1) for page in own]

    weights, block_scalars = ((2 * XN, PT, ROWS), bf16), ((8, 128), f32)
    whi, wlo, qt, logits, scale, chosen, sums = call(
        score_kernel,
        [weights, weights, ((W, ROWS), f32), block_scalars, ((2 * XN, ROWS), f32), block_scalars,
         ((QN * PIECE, W), f32)],
        [pltpu.VMEM((2 * XN, ROWS), f32), pltpu.VMEM((ROWS, W), f32), pltpu.VMEM((1, PT, W), f32),
         pltpu.VMEM((1, NQ), jnp.int32), pltpu.SemaphoreType.DMA, pltpu.SemaphoreType.DMA],
        scalars=1, anywhere=2,
    )(me, pages, positive, block, *own[1:], *other)
    sums = lax.all_to_all(sums.reshape(QN, PIECE, 1, W), QUERY_AXES, 0, 0, tiled=True)
    sums = sums.reshape(QN * PIECE, W)
    theirs, factors, owner = call(
        coefficient_kernel, [((XN * PT + 8, W), f32), ((2 * XN, ROWS), f32), ((1, 128), f32)]
    )(sums, logits, chosen, scale, qt, whi, wlo)
    loss_rows = theirs[XN * PT :]
    theirs = moved(theirs, "co", 1)
    (mine,) = call(own_gradient_kernel, [((XN * PT, W), f32)])(factors, qt, whi, wlo)
    blocks = call(pair_kernel, [((PT + 8, W), f32)] * XN)(mine, loss_rows, theirs)
    blocks = [blocks[0]] + [moved(blocks[s], "x", -s) for s in range(1, XN)]
    page_grad, loss, slope = call(
        final_kernel, [((1, PT, W), f32), ((1, 1), f32), ((TOK, 1, W), f32)], scalars=1
    )(me, owner, *blocks, sums)
    return loss.reshape(()), slope.transpose(1, 0, 2), page_grad


def solution(mesh):
    finer = Mesh(mesh.devices.reshape(tuple(SIZES[a] for a in AXES)), AXES)
    placed = (P(AXES, None, None), P(AXES, None, None), P())
    return jax.shard_map(
        shards,
        mesh=finer,
        in_specs=placed,
        out_specs=(P(), P(AXES, None, None), P(AXES, None, None)),
        check_vma=False,
    )
```

time: 80.1 us -> 73.4 us (0.916)
  blocking collectives: 0 us -> 22.3 us
  local copies, waits for them, and re-layouts: 17.8 us -> 3.07 us
  starting transfers between devices: 35.6 us -> 29.1 us
  waiting for transfers between devices: 17.1 us -> 10.8 us
  Pallas kernels: 8.08 us -> 7.18 us
    all_to_all x0 -> x1, blocking collectives: none -> 22.3 us  [shards(): lax.all_to_all(sums.reshape(QN, PIECE, 1, W), QUERY_AXES, 0, 0, tiled=True)]
    unnamed x54 -> x5, local copies, waits for them, and re-layouts: 17.8 us -> 2.28 us
    all_to_all x3 -> x1, starting transfers between devices: 23 us -> 12 us  [shards(): lax.all_to_all(spread, QUERY_AXES, 0, 0, tiled=True).reshape(ROWS, W)]
    all_to_all x3 -> x1, waiting for transfers between devices: 7.84 us -> 0.01 us  [shards(): lax.all_to_all(spread, QUERY_AXES, 0, 0, tiled=True).reshape(ROWS, W)]
    ppermute x11, starting transfers between devices: 12.5 us -> 17.1 us  [moved(): return lax.ppermute(value, axis, [(i, (i + step) % n) for i in range(n)])]
    ppermute x11, waiting for transfers between devices: 9.24 us -> 10.8 us  [moved(): return lax.ppermute(value, axis, [(i, (i + step) % n) for i in range(n)])]
    pallas_call x10 -> x5, Pallas kernels: 8.08 us -> 7.18 us  [run(): pl.pallas_call(kernel, out_shape=[jax.ShapeDtypeStruct(s, d) for s, d in...]
  transfers between devices with their start and end apart: 14 -> 12, of which waited for: 6 -> 6; matrix products, arithmetic and copies ran while one was open for 0% -> 0% of each run, Pallas kernels for 6% -> 1%
where the time goes in v3:
time: 73.4 us; the launch traced here: 73.1 us
  starting transfers between devices  29.1 us (40%)
  blocking collectives  22.3 us (30%)
  waiting for transfers between devices  10.8 us (15%)
  Pallas kernels  7.18 us (10%)
  local copies, waits for them, and re-layouts  3.07 us (4%)
    all_to_all x1, blocking collectives, shards(): lax.all_to_all(sums.reshape(QN, PIECE, 1, W), QUERY_AXES, 0, 0, tiled=True)  22.3 us
    ppermute x11, starting transfers between devices, moved(): return lax.ppermute(value, axis, [(i, (i + step) % n) for i in range(n)])  17.1 us
    all_to_all x1, starting transfers between devices, shards(): lax.all_to_all(spread, QUERY_AXES, 0, 0, tiled=True).reshape(ROWS, W)  12 us
    ppermute x11, waiting for transfers between devices, moved(): return lax.ppermute(value, axis, [(i, (i + step) % n) for i in range(n)])  10.8 us
    pallas_call x5, Pallas kernels, run(): pl.pallas_call(kernel, out_shape=[jax.ShapeDtypeStruct(s, d) for s, d in...  7.18 us
    unnamed x5, local copies, waits for them, and re-layouts  2.28 us
  transfers between devices with their start and end apart: 12, of which 6 were waited for; matrix products, arithmetic and copies ran while one was open for 0% of the time, Pallas kernels for 1%

profile of v3, /device:TPU:1, one launch (start us, length us, event | category | flops | bytes accessed | tf_op | source)
XLA Modules:
  0.0 73.1 jit_solution(12296488441736176610)
XLA Ops:
  0.6 0.7 copy.9
  1.3 0.8 %broadcast_in_dim.3 = f32[32,12,1,128]{3,2,1,0:T(1,128)} broadcast(f32[12,128]{1,0:T(8,128)S(1)} %bitcast.16), dimensions={1,3} | broadcast | bytes 202752 | tf_op jit(solution)/shard_map/broadcast_in_dim | solution.py:215
  2.1 12.0 %all-to-all-start = ((f32[32,12,1,128]{3,2,1,0:T(1,128)}), f32[32,12,1,128]{3,2,1,0:T(1,128)S(1)}, u32[]{:S(2)}, u32[]{:S(2)}) async-start(f32[32,12,1,128]{3,2,1,0:T(1,128)} %broadcast_in_dim.3), calls=%async_computation | async-start | bytes 393216 | tf_op jit(solution)/shard_map/all_to_all | solution.py:216
  14.2 2.6 %collective-permute-start.2 = (f32[1,256,128]{2,1,0:T(8,128)}, f32[1,256,128]{2,1,0:T(8,128)S(1)}, u32[]{:S(2)}, u32[]{:S(2)}) collective-permute-start(f32[1,256,128]{2,1,0:T(8,128)} %own_hbm.1), channel_id=1, source_target_pairs={{0,6},{2,0},{4,2},{6,4},{1,7},{3,1},{5,3},{7,5},{8,14},{10,8},{12,... | collective-permute-start | bytes 393224 | tf_op jit(solution)/shard_map/ppermute | solution.py:208
  16.7 0.5 collective-permute-start.1
  17.2 0.6 collective-permute-start
  17.8 1.8 %collective-permute-start.3 = (f32[1,256,128]{2,1,0:T(8,128)}, f32[1,256,128]{2,1,0:T(8,128)S(1)}, u32[]{:S(2)}, u32[]{:S(2)}) collective-permute-start(f32[1,256,128]{2,1,0:T(8,128)} %own_hbm.1), channel_id=1, source_target_pairs={{0,32},{32,0},{1,33},{33,1},{2,34},{34,2},{3,35},{35,3},{4,36},{36... | collective-permute-start | bytes 393224 | tf_op jit(solution)/shard_map/ppermute | solution.py:208
  19.6 0.0 collective-permute-done.2.p3
  19.6 3.9 %collective-permute-start.6 = (f32[1,256,128]{2,1,0:T(8,128)S(1)}, f32[1,256,128]{2,1,0:T(8,128)S(1)}, u32[]{:S(2)}, u32[]{:S(2)}) collective-permute-start(f32[1,256,128]{2,1,0:T(8,128)S(1)} %collective-permute-done.2.p3), channel_id=1, source_target_pairs={{0,32},{32,0},{1,33},{33,1},{2,34},{34,2},{3,35},{35,3},{4,36},{36... | collective-permute-start | bytes 393224 | tf_op jit(solution)/shard_map/ppermute | solution.py:208
  23.6 0.0 collective-permute-done.1.p2
  23.6 2.2 %collective-permute-start.5 = (f32[1,256,128]{2,1,0:T(8,128)S(1)}, f32[1,256,128]{2,1,0:T(8,128)S(1)}, u32[]{:S(2)}, u32[]{:S(2)}) collective-permute-start(f32[1,256,128]{2,1,0:T(8,128)S(1)} %collective-permute-done.1.p2), channel_id=1, source_target_pairs={{0,32},{32,0},{1,33},{33,1},{2,34},{34,2},{3,35},{35,3},{4,36},{36... | collective-permute-start | bytes 393224 | tf_op jit(solution)/shard_map/ppermute | solution.py:208
  25.8 0.3 collective-permute-done.p1
  26.1 1.0 %collective-permute-start.4 = (f32[1,256,128]{2,1,0:T(8,128)S(1)}, f32[1,256,128]{2,1,0:T(8,128)S(1)}, u32[]{:S(2)}, u32[]{:S(2)}) collective-permute-start(f32[1,256,128]{2,1,0:T(8,128)S(1)} %collective-permute-done.p1), channel_id=1, source_target_pairs={{0,32},{32,0},{1,33},{33,1},{2,34},{34,2},{3,35},{35,3},{4,36},{36... | collective-permute-start | bytes 393224 | tf_op jit(solution)/shard_map/ppermute | solution.py:208
  27.2 0.0 collective-permute-done.3.p4
  27.2 0.0 collective-permute-done.6.p7
  27.2 0.0 collective-permute-done.5.p6
  27.2 1.0 %collective-permute-done.4.p5 = f32[1,256,128]{2,1,0:T(8,128)S(1)} collective-permute-done((f32[1,256,128]{2,1,0:T(8,128)S(1)}, f32[1,256,128]{2,1,0:T(8,128)S(1)}, u32[]{:S(2)}, u32[]{:S(2)}) %collective-permute-start.4) | collective-permute-done | bytes 131104 | tf_op jit(solution)/shard_map/ppermute | solution.py:208
  28.1 0.0 all-to-all-done
  28.1 0.0 copy-start
  28.1 0.9 %copy-done = f32[1,256,128]{2,1,0:T(8,128)S(1)} copy-done((f32[1,256,128]{2,1,0:T(8,128)S(1)}, f32[1,256,128]{2,1,0:T(8,128)}, u32[]{:S(2)}) %copy-start) | copy-done | bytes 131096
  29.0 0.0 copy-start.1
  29.1 0.7 copy-done.1
  29.7 4.4 %shard_map.58 = (bf16[8,256,384]{2,1,0:T(8,128)(2,1)S(1)}, bf16[8,256,384]{2,1,0:T(8,128)(2,1)S(1)}, f32[128,384]{1,0:T(8,128)S(1)}, f32[8,128]{1,0:T(8,128)S(1)...) custom-call(s32[1]{0:T(128)} %bitcast.me_ref, f32[1,256,128]{2,1,0:T(8,128)S(1)} %copy-done, ...), custom_call_target="tpu_custom_call" | custom-call | tf_op jit(solution)/shard_map/pallas_call | solution.py:194
  34.2 22.3 %all_to_all.10 = f32[32,25,1,128]{3,2,1,0:T(1,128)S(1)} all-to-all(f32[32,25,1,128]{3,2,1,0:T(1,128)S(1)} %bitcast.14), channel_id=1, replica_groups=mesh['za'=4,'co'=2,'y'=4,'x'=4,'zb'=2] {'za','y','zb'}, dimensions={0} | all-to-all | bytes 819200 | tf_op jit(solution)/shard_map/all_to_all | solution.py:229
  56.4 1.2 %shard_map.59 = (f32[1032,128]{1,0:T(8,128)S(1)}, f32[8,384]{1,0:T(8,128)S(1)}, f32[1,128]{1,0:T(1,128)S(1)}) custom-call(f32[800,128]{1,0:T(8,128)S(1)} %bitcast.11, f32[8,128]{1,0:T(8,128)S(1)} %get-tuple-element.21.logits_ref, f32[8,128]{1,0:T(8,128)S(1)} %get-tuple-element.22.chosen_ref, f32[8,384]{1,0:T(8,128)S(1)} %get-tuple-element.23.scale_ref, ...), custom_call_target="tpu_custom_call" | custom-call | tf_op jit(solution)/shard_map/pallas_call | solution.py:194
  57.6 2.9 %collective-permute-start.7 = (f32[1032,128]{1,0:T(8,128)S(1)}, f32[1032,128]{1,0:T(8,128)S(1)}, u32[]{:S(2)}, u32[]{:S(2)}) collective-permute-start(f32[1032,128]{1,0:T(8,128)S(1)} %get-tuple-element.29), channel_id=1, source_target_pairs={{0,32},{32,0},{1,33},{33,1},{2,34},{34,2},{3,35},{35,3},{4,36},{36... | collective-permute-start | bytes 1585160 | tf_op jit(solution)/shard_map/ppermute | solution.py:208
  60.5 0.8 %shard_map.60.mine_ref = f32[1024,128]{1,0:T(8,128)S(1)} custom-call(f32[8,384]{1,0:T(8,128)S(1)} %get-tuple-element.28.factors_ref, f32[128,384]{1,0:T(8,128)S(1)} %get-tuple-element.24.qt_ref, bf16[8,256,384]{2,1,0:T(8,128)(2,1)S(1)} %get-tuple-element.25.whi_ref, bf16[8,256,384]{2,1,0:T(8,128)(2,1)S(1)} %get-tuple-element.26.wlo_ref), custom_call_target="tpu_custom_call" | custom-call | tf_op jit(solution)/shard_map/pallas_call | solution.py:194
  61.3 0.7 %collective-permute-done.7.theirs_ref = f32[1032,128]{1,0:T(8,128)S(1)} collective-permute-done((f32[1032,128]{1,0:T(8,128)S(1)}, f32[1032,128]{1,0:T(8,128)S(1)}, u32[]{:S(2)}, u32[]{:S(2)}) %collective-permute-start.7) | collective-permute-done | bytes 528416 | tf_op jit(solution)/shard_map/ppermute | solution.py:208
  62.0 0.1 shard_map.61
  62.1 0.4 collective-permute-start.8
  62.5 0.5 collective-permute-start.9
  63.0 0.7 collective-permute-start.10
  63.6 3.3 %collective-permute-done.8.r1 = f32[264,128]{1,0:T(8,128)S(1)} collective-permute-done((f32[264,128]{1,0:T(8,128)S(1)}, f32[264,128]{1,0:T(8,128)S(1)}, u32[]{:S(2)}, u32[]{:S(2)}) %collective-permute-start.8) | collective-permute-done | bytes 135200 | tf_op jit(solution)/shard_map/ppermute | solution.py:208
  67.0 1.5 %collective-permute-done.9.r2 = f32[264,128]{1,0:T(8,128)S(1)} collective-permute-done((f32[264,128]{1,0:T(8,128)S(1)}, f32[264,128]{1,0:T(8,128)S(1)}, u32[]{:S(2)}, u32[]{:S(2)}) %collective-permute-start.9) | collective-permute-done | bytes 135200 | tf_op jit(solution)/shard_map/ppermute | solution.py:208
  68.4 3.9 %collective-permute-done.10.r3 = f32[264,128]{1,0:T(8,128)S(1)} collective-permute-done((f32[264,128]{1,0:T(8,128)S(1)}, f32[264,128]{1,0:T(8,128)S(1)}, u32[]{:S(2)}, u32[]{:S(2)}) %collective-permute-start.10) | collective-permute-done | bytes 135200 | tf_op jit(solution)/shard_map/ppermute | solution.py:208
  72.4 0.7 shard_map.62
  (1 shorter events, 0.0 us)
Async XLA Ops:
  2.1 26.0 %all-to-all-start = ((f32[32,12,1,128]{3,2,1,0:T(1,128)}), f32[32,12,1,128]{3,2,1,0:T(1,128)S(1)}, u32[]{:S(2)}, u32[]{:S(2)}) async-start(f32[32,12,1,128]{3,2,1,0:T(1,128)} %broadcast_in_dim.3), calls=%async_computation | async-start | bytes 393216 | tf_op jit(solution)/shard_map/all_to_all | solution.py:216
  14.2 5.5 %collective-permute-start.2 = (f32[1,256,128]{2,1,0:T(8,128)}, f32[1,256,128]{2,1,0:T(8,128)S(1)}, u32[]{:S(2)}, u32[]{:S(2)}) collective-permute-start(f32[1,256,128]{2,1,0:T(8,128)} %own_hbm.1), channel_id=1, source_target_pairs={{0,6},{2,0},{4,2},{6,4},{1,7},{3,1},{5,3},{7,5},{8,14},{10,8},{12,... | collective-permute-start | bytes 393224 | tf_op jit(solution)/shard_map/ppermute | solution.py:208
  16.7 6.8 %collective-permute-start.1 = (f32[1,256,128]{2,1,0:T(8,128)}, f32[1,256,128]{2,1,0:T(8,128)S(1)}, u32[]{:S(2)}, u32[]{:S(2)}) collective-permute-start(f32[1,256,128]{2,1,0:T(8,128)} %own_hbm.1), channel_id=1, source_target_pairs={{0,4},{2,6},{4,0},{6,2},{1,5},{3,7},{5,1},{7,3},{8,12},{10,14},{12... | collective-permute-start | bytes 393224 | tf_op jit(solution)/shard_map/ppermute | solution.py:208
  17.2 8.9 %collective-permute-start = (f32[1,256,128]{2,1,0:T(8,128)}, f32[1,256,128]{2,1,0:T(8,128)S(1)}, u32[]{:S(2)}, u32[]{:S(2)}) collective-permute-start(f32[1,256,128]{2,1,0:T(8,128)} %own_hbm.1), channel_id=1, source_target_pairs={{0,2},{2,4},{4,6},{6,0},{1,3},{3,5},{5,7},{7,1},{8,10},{10,12},{12... | collective-permute-start | bytes 393224 | tf_op jit(solution)/shard_map/ppermute | solution.py:208
  17.8 9.3 %collective-permute-start.3 = (f32[1,256,128]{2,1,0:T(8,128)}, f32[1,256,128]{2,1,0:T(8,128)S(1)}, u32[]{:S(2)}, u32[]{:S(2)}) collective-permute-start(f32[1,256,128]{2,1,0:T(8,128)} %own_hbm.1), channel_id=1, source_target_pairs={{0,32},{32,0},{1,33},{33,1},{2,34},{34,2},{3,35},{35,3},{4,36},{36... | collective-permute-start | bytes 393224 | tf_op jit(solution)/shard_map/ppermute | solution.py:208
  19.6 7.5 %collective-permute-start.6 = (f32[1,256,128]{2,1,0:T(8,128)S(1)}, f32[1,256,128]{2,1,0:T(8,128)S(1)}, u32[]{:S(2)}, u32[]{:S(2)}) collective-permute-start(f32[1,256,128]{2,1,0:T(8,128)S(1)} %collective-permute-done.2.p3), channel_id=1, source_target_pairs={{0,32},{32,0},{1,33},{33,1},{2,34},{34,2},{3,35},{35,3},{4,36},{36... | collective-permute-start | bytes 393224 | tf_op jit(solution)/shard_map/ppermute | solution.py:208
  23.6 3.6 %collective-permute-start.5 = (f32[1,256,128]{2,1,0:T(8,128)S(1)}, f32[1,256,128]{2,1,0:T(8,128)S(1)}, u32[]{:S(2)}, u32[]{:S(2)}) collective-permute-start(f32[1,256,128]{2,1,0:T(8,128)S(1)} %collective-permute-done.1.p2), channel_id=1, source_target_pairs={{0,32},{32,0},{1,33},{33,1},{2,34},{34,2},{3,35},{35,3},{4,36},{36... | collective-permute-start | bytes 393224 | tf_op jit(solution)/shard_map/ppermute | solution.py:208
  26.1 2.0 %collective-permute-start.4 = (f32[1,256,128]{2,1,0:T(8,128)S(1)}, f32[1,256,128]{2,1,0:T(8,128)S(1)}, u32[]{:S(2)}, u32[]{:S(2)}) collective-permute-start(f32[1,256,128]{2,1,0:T(8,128)S(1)} %collective-permute-done.p1), channel_id=1, source_target_pairs={{0,32},{32,0},{1,33},{33,1},{2,34},{34,2},{3,35},{35,3},{4,36},{36... | collective-permute-start | bytes 393224 | tf_op jit(solution)/shard_map/ppermute | solution.py:208
  28.1 0.9 %copy-start = (f32[1,256,128]{2,1,0:T(8,128)S(1)}, f32[1,256,128]{2,1,0:T(8,128)}, u32[]{:S(2)}) copy-start(f32[1,256,128]{2,1,0:T(8,128)} %own_hbm.1) | copy-start | bytes 393220
  29.0 0.7 copy-start.1
  57.6 4.4 %collective-permute-start.7 = (f32[1032,128]{1,0:T(8,128)S(1)}, f32[1032,128]{1,0:T(8,128)S(1)}, u32[]{:S(2)}, u32[]{:S(2)}) collective-permute-start(f32[1032,128]{1,0:T(8,128)S(1)} %get-tuple-element.29), channel_id=1, source_target_pairs={{0,32},{32,0},{1,33},{33,1},{2,34},{34,2},{3,35},{35,3},{4,36},{36... | collective-permute-start | bytes 1585160 | tf_op jit(solution)/shard_map/ppermute | solution.py:208
  62.1 4.9 %collective-permute-start.8 = (f32[264,128]{1,0:T(8,128)S(1)}, f32[264,128]{1,0:T(8,128)S(1)}, u32[]{:S(2)}, u32[]{:S(2)}) collective-permute-start(f32[264,128]{1,0:T(8,128)S(1)} %get-tuple-element.31), channel_id=1, source_target_pairs={{0,6},{2,0},{4,2},{6,4},{1,7},{3,1},{5,3},{7,5},{8,14},{10,8},{12,... | collective-permute-start | bytes 405512 | tf_op jit(solution)/shard_map/ppermute | solution.py:208
  62.5 6.0 %collective-permute-start.9 = (f32[264,128]{1,0:T(8,128)S(1)}, f32[264,128]{1,0:T(8,128)S(1)}, u32[]{:S(2)}, u32[]{:S(2)}) collective-permute-start(f32[264,128]{1,0:T(8,128)S(1)} %get-tuple-element.32), channel_id=1, source_target_pairs={{0,4},{2,6},{4,0},{6,2},{1,5},{3,7},{5,1},{7,3},{8,12},{10,14},{12... | collective-permute-start | bytes 405512 | tf_op jit(solution)/shard_map/ppermute | solution.py:208
  63.0 9.4 %collective-permute-start.10 = (f32[264,128]{1,0:T(8,128)S(1)}, f32[264,128]{1,0:T(8,128)S(1)}, u32[]{:S(2)}, u32[]{:S(2)}) collective-permute-start(f32[264,128]{1,0:T(8,128)S(1)} %get-tuple-element.33), channel_id=1, source_target_pairs={{0,2},{2,4},{4,6},{6,0},{1,3},{3,5},{5,7},{7,1},{8,10},{10,12},{12... | collective-permute-start | bytes 405512 | tf_op jit(solution)/shard_map/ppermute | solution.py:208

commit v4 on v3

v4 whole, which is shorter than its diff:
```python
import jax
import jax.numpy as jnp
from jax import lax
from jax.experimental import pallas as pl
from jax.experimental.pallas import tpu as pltpu
from jax.sharding import Mesh
from jax.sharding import PartitionSpec as P

DEVICES = 256
CO, X = (5, 1), (1, 3)
QN = 32
QUERY_TURN = 0
STATS_TURN = 16
XN = 4
TOK = 12
ROWS = QN * TOK
PT = 256
W = 128
NQ = 256

cap_value = 4.0
sharpness_divisor = 0.25
logit_scale = 8.0
z_weight = 0.001
f32 = jnp.float32
bf16 = jnp.bfloat16


def offset_of(member):
    return ((member >> 3) << 6) + (((member >> 1) & 3) << 3) + (member & 1)


def groups(turn):
    members = [offset_of((k - turn) % QN) for k in range(QN)]
    return [[(co << 5) + (x << 1) + m for m in members] for co in range(2) for x in range(XN)]


def exchange(value, turn):
    return lax.all_to_all(value, "d", 0, 0, axis_index_groups=groups(turn), tiled=True)


def iota(shape, dim):
    return lax.broadcasted_iota(jnp.int32, shape, dim)


def parts(x):
    high = x.astype(bf16)
    return high, (x - high.astype(f32)).astype(bf16)


def product(a, b, dims):
    terms = [
        lax.dot_general(left, right, (dims, ((), ())), preferred_element_type=f32)
        for left, right in ((a[0], b[0]), (a[0], b[1]), (a[1], b[0]))
    ]
    return terms[0] + (terms[1] + terms[2])


def spread_matrix():
    row, lane = iota((ROWS, 128), 0), iota((ROWS, 128), 1)
    first = (lane & 31) * TOK
    return ((row >= first) & (row < first + TOK) & (lane < 64)).astype(f32)


def spread_kernel(q_hbm, out_ref, query_ref, rows_ref, sem):
    copy = pltpu.make_async_copy(q_hbm, query_ref, sem)
    copy.start()
    copy.wait()
    for i in range(TOK):
        rows_ref[i : i + 1, :] = query_ref[i]
        rows_ref[TOK + i : TOK + i + 1, :] = query_ref[i]
    twice = rows_ref[...]
    for k in range(QN // 2):
        out_ref[2 * k * TOK : 2 * (k + 1) * TOK, :] = twice


def is_positive(me_ref, positive_ref):
    me = me_ref[0]
    base = me & 0b00100110
    index, lane = iota((NQ, 128), 0), iota((NQ, 128), 1)
    query = offset_of((lane - QUERY_TURN) & (QN - 1)) + base
    chosen = jnp.dot(
        positive_ref[...].astype(f32), (index == query).astype(f32), precision=lax.Precision.HIGHEST,
        preferred_element_type=f32,
    )
    row = iota((8, 128), 0)
    x = (((me >> 1) & 3) - (row & 3)) & 3
    co = ((me >> 5) & 1) ^ (row >> 2)
    page = (me & 0b11011001) + (x << 1) + (co << 5)
    return page.astype(f32) == chosen


def by_row(values):
    return lax.dot_general(
        jnp.where(iota((8, 128), 1) < 32, values, 0.0), spread_matrix(), (((1,), (1,)), ((), ())),
        precision=lax.Precision.HIGHEST, preferred_element_type=f32,
    )


def score_kernel(
    me_ref, own_hbm, positive_hbm, q_ref, p1, p2, p3, p4, p5, p6, p7,
    whi_ref, wlo_ref, qt_ref, logits_ref, scale_ref, chosen_ref, ut_ref, stats_ref,
    tot_ref, p0, positive_ref, own_sem, positive_sem,
):
    own_copy = pltpu.make_async_copy(own_hbm, p0, own_sem)
    positive_copy = pltpu.make_async_copy(positive_hbm, positive_ref, positive_sem)
    own_copy.start()
    positive_copy.start()
    qt = q_ref[...].T
    qt_ref[...] = qt
    q_parts = parts(qt)
    pages = (p0, p1, p2, p3, p4, p5, p6, p7)
    for s, page_ref in [*enumerate(pages)][1:] + [(0, p0)]:
        if s == 0:
            own_copy.wait()
        scores = product(parts(page_ref[0]), q_parts, ((1,), (0,)))
        tangent = jnp.tanh(scores * (1.0 / cap_value))
        grid = jnp.exp(tangent * (cap_value / sharpness_divisor))
        tot_ref[s : s + 1, :] = jnp.sum(grid, axis=0, keepdims=True)
        whi_ref[s], wlo_ref[s] = parts(grid * (1.0 - tangent * tangent))
    smooth = sharpness_divisor * jnp.log(tot_ref[...])
    logits = (logit_scale / TOK) * jnp.dot(
        smooth, spread_matrix(), precision=lax.Precision.HIGHEST, preferred_element_type=f32
    )
    logits_ref[...] = logits
    positive_copy.wait()
    chosen = is_positive(me_ref, positive_ref)
    chosen_ref[...] = chosen.astype(f32)
    scale = (logit_scale / TOK) / tot_ref[...]
    scale_ref[...] = scale
    lane = iota((8, 128), 1)
    exponential = jnp.exp(logits)
    matched = jnp.where(chosen, logits, 0.0)
    local = jnp.where(lane < 32, exponential, jnp.where(lane < 64, matched, 0.0))
    stats = jnp.sum(local, axis=0, keepdims=True)

    stats_ref[...] = jnp.broadcast_to(stats[None], stats_ref.shape)
    for s, page_ref in enumerate(pages):
        ut_ref[s] = product(parts(page_ref[0].T), (whi_ref[s], wlo_ref[s]), ((1,), (0,)))


def page_gradients(whi_ref, wlo_ref, qt, factors, first, out_ref):
    for s in range(XN):
        scaled = parts(qt * factors[first + s : first + s + 1, :])
        out_ref[s * PT : (s + 1) * PT, :] = product(
            (whi_ref[first + s], wlo_ref[first + s]), scaled, ((1,), (1,))
        )


def coefficient_kernel(
    stats_ref, logits_ref, chosen_ref, scale_ref, qt_ref, whi_ref, wlo_ref, out_ref, factors_ref
):
    stats = jnp.sum(stats_ref[...], axis=0)
    lane = iota((1, 128), 1)
    totals = jnp.where(lane < 32, stats, 1.0)
    log_totals = jnp.log(totals)
    terms = jnp.where(
        lane < 32, log_totals + z_weight * log_totals * log_totals, jnp.where(lane < 64, -stats, 0.0)
    )
    loss = jnp.sum(terms, axis=1, keepdims=True) * (1.0 / NQ)
    out_ref[XN * PT :, :] = jnp.broadcast_to(loss, (8, 128))
    slope = 1.0 + 2.0 * z_weight * log_totals
    coefficients = (slope * jnp.exp(logits_ref[...]) / totals - chosen_ref[...]) * (1.0 / NQ)
    factors = by_row(coefficients) * scale_ref[...]
    factors_ref[...] = factors
    page_gradients(whi_ref, wlo_ref, qt_ref[...], factors, XN, out_ref)


def own_gradient_kernel(factors_ref, qt_ref, whi_ref, wlo_ref, ut_ref, out_ref, dq_ref):
    factors = factors_ref[...]
    total = jnp.zeros((W, ROWS), f32)
    for s in range(2 * XN):
        total = total + ut_ref[s] * factors[s : s + 1, :]
    dq_ref[...] = total.T
    page_gradients(whi_ref, wlo_ref, qt_ref[...], factors, 0, out_ref)


def pair_kernel(mine_ref, loss_ref, theirs_ref, o0, o1, o2, o3):
    loss = loss_ref[...] + theirs_ref[XN * PT :, :]
    for s, out in enumerate((o0, o1, o2, o3)):
        rows = slice(s * PT, (s + 1) * PT)
        out[0:PT, :] = mine_ref[rows, :] + theirs_ref[rows, :]
        out[PT:, :] = loss


def final_kernel(r0, r1, r2, r3, dq_ref, page_ref, loss_ref, slope_ref):
    total = (r0[...] + r2[...]) + (r1[...] + r3[...])
    page_ref[0] = total[0:PT]
    loss_ref[...] = total[PT : PT + 1, 0:1]
    slope = jnp.zeros((TOK, W), f32)
    for k in range(QN):
        slope = slope + dq_ref[k * TOK : (k + 1) * TOK, :]
    for i in range(TOK):
        slope_ref[i] = slope[i : i + 1, :]


def call(kernel, out, scratch=(), scalars=0, anywhere=0):
    vmem = pl.BlockSpec(memory_space=pltpu.VMEM)

    def run(*args):
        args = [
            pltpu.with_memory_space_constraint(a, pltpu.HBM) if scalars <= i < scalars + anywhere else a
            for i, a in enumerate(args)
        ]
        specs = [pl.BlockSpec(memory_space=pltpu.SMEM)] * scalars
        specs += [pl.BlockSpec(memory_space=pltpu.HBM)] * anywhere
        specs += [vmem] * (len(args) - scalars - anywhere)
        return pl.pallas_call(
            kernel,
            out_shape=[jax.ShapeDtypeStruct(s, d) for s, d in out],
            in_specs=specs,
            out_specs=[vmem] * len(out),
            scratch_shapes=list(scratch),
            compiler_params=pltpu.CompilerParams(vmem_limit_bytes=16 * 1024 * 1024),
        )(*args)

    return run


def moved(value, axis, step):
    bit, mask = axis
    pairs = [
        (i, (i & ~(mask << bit)) | ((((i >> bit) + step) & mask) << bit)) for i in range(DEVICES)
    ]
    return lax.ppermute(value, "d", pairs)


def shards(queries, pages, positive):
    me = lax.axis_index("d").astype(jnp.int32).reshape(1)
    positive = positive.reshape(1, NQ)
    (spread,) = call(
        spread_kernel, [((ROWS, W), f32)],
        [pltpu.VMEM((TOK, 1, W), f32), pltpu.VMEM((2 * TOK, W), f32), pltpu.SemaphoreType.DMA],
        anywhere=1,
    )(queries.transpose(1, 0, 2))
    block = exchange(spread.reshape(QN, TOK, 1, W), QUERY_TURN).reshape(ROWS, W)
    own = [pages] + [moved(pages, X, s) for s in range(1, XN)]
    other = [moved(page, CO, 1) for page in own]

    weights, block_scalars = ((2 * XN, PT, ROWS), bf16), ((8, 128), f32)
    whi, wlo, qt, logits, scale, chosen, ut, stats = call(
        score_kernel,
        [weights, weights, ((W, ROWS), f32), block_scalars, ((2 * XN, ROWS), f32), block_scalars,
         ((2 * XN, W, ROWS), f32), ((QN, 1, W), f32)],
        [pltpu.VMEM((2 * XN, ROWS), f32), pltpu.VMEM((1, PT, W), f32),
         pltpu.VMEM((1, NQ), jnp.int32), pltpu.SemaphoreType.DMA, pltpu.SemaphoreType.DMA],
        scalars=1, anywhere=2,
    )(me, pages, positive, block, *own[1:], *other)
    stats = exchange(stats, STATS_TURN)
    theirs, factors = call(
        coefficient_kernel, [((XN * PT + 8, W), f32), ((2 * XN, ROWS), f32)]
    )(stats, logits, chosen, scale, qt, whi, wlo)
    loss_rows = theirs[XN * PT :]
    theirs = moved(theirs, CO, 1)
    mine, dq = call(own_gradient_kernel, [((XN * PT, W), f32), ((ROWS, W), f32)])(
        factors, qt, whi, wlo, ut
    )
    blocks = call(pair_kernel, [((PT + 8, W), f32)] * XN)(mine, loss_rows, theirs)
    blocks = [blocks[0]] + [moved(blocks[s], X, -s) for s in range(1, XN)]
    dq = exchange(dq.reshape(QN, TOK, 1, W), QUERY_TURN)
    page_grad, loss, slope = call(
        final_kernel, [((1, PT, W), f32), ((1, 1), f32), ((TOK, 1, W), f32)]
    )(*blocks, dq.reshape(ROWS, W))
    return loss.reshape(()), slope.transpose(1, 0, 2), page_grad


def solution(mesh):
    flat = Mesh(mesh.devices.reshape(DEVICES), ("d",))
    placed = (P("d", None, None), P("d", None, None), P())
    return jax.shard_map(
        shards,
        mesh=flat,
        in_specs=placed,
        out_specs=(P(), P("d", None, None), P("d", None, None)),
        check_vma=False,
    )
```

time: 73.4 us -> 68 us (0.926)
  blocking collectives: 22.3 us -> 13 us
  starting transfers between devices: 29.1 us -> 35.4 us
  local copies, waits for them, and re-layouts: 3.07 us -> 0.01 us
  Pallas kernels: 7.18 us -> 8.5 us
  waiting for transfers between devices: 10.8 us -> 10 us
    ppermute x11, waiting for transfers between devices: 10.8 us -> 1.47 us  [moved(): return lax.ppermute(value, 'd', pairs)]
    all_to_all x1, blocking collectives: 22.3 us -> 13 us  [exchange(): lax.all_to_all(value, 'd', 0, 0, axis_index_groups=groups(turn), tiled=True)]
    all_to_all x1 -> x2, waiting for transfers between devices: 0.01 us -> 8.57 us  [exchange(): lax.all_to_all(value, 'd', 0, 0, axis_index_groups=groups(turn), tiled=True)]
    all_to_all x1 -> x2, starting transfers between devices: 12 us -> 19.3 us  [exchange(): lax.all_to_all(value, 'd', 0, 0, axis_index_groups=groups(turn), tiled=True)]
    unnamed x5 -> x0, local copies, waits for them, and re-layouts: 2.28 us -> none
    pallas_call x5 -> x6, Pallas kernels: 7.18 us -> 8.5 us  [run(): pl.pallas_call(kernel, out_shape=[jax.ShapeDtypeStruct(s, d) for s, d in...]
    ppermute x11, starting transfers between devices: 17.1 us -> 16.1 us  [moved(): return lax.ppermute(value, 'd', pairs)]
    broadcast_in_dim x1 -> x0, local copies, waits for them, and re-layouts: 0.79 us -> none  [shards(): spread = jnp.broadcast_to(rows, (QN, TOK, 1, W))]
  transfers between devices with their start and end apart: 12 -> 13, of which waited for: 6 -> 4; matrix products, arithmetic and copies ran while one was open for 0% -> 0% of each run, Pallas kernels for 1% -> 2%
where the time goes in v4:
time: 68 us; the launch traced here: 67.6 us
  starting transfers between devices  35.4 us (52%)
  blocking collectives  13 us (19%)
  waiting for transfers between devices  10 us (15%)
  Pallas kernels  8.5 us (12%)
  between operations  0.71 us (1%)
    all_to_all x2, starting transfers between devices, exchange(): lax.all_to_all(value, 'd', 0, 0, axis_index_groups=groups(turn), tiled=True)  19.3 us
    ppermute x11, starting transfers between devices, moved(): return lax.ppermute(value, 'd', pairs)  16.1 us
    all_to_all x1, blocking collectives, exchange(): lax.all_to_all(value, 'd', 0, 0, axis_index_groups=groups(turn), tiled=True)  13 us
    all_to_all x2, waiting for transfers between devices, exchange(): lax.all_to_all(value, 'd', 0, 0, axis_index_groups=groups(turn), tiled=True)  8.57 us
    pallas_call x6, Pallas kernels, run(): pl.pallas_call(kernel, out_shape=[jax.ShapeDtypeStruct(s, d) for s, d in...  8.5 us
    ppermute x11, waiting for transfers between devices, moved(): return lax.ppermute(value, 'd', pairs)  1.47 us
  transfers between devices with their start and end apart: 13, of which 4 were waited for; matrix products, arithmetic and copies ran while one was open for 0% of the time, Pallas kernels for 2%

profile of v4, /device:TPU:1, one launch (start us, length us, event | category | flops | bytes accessed | tf_op | source)
XLA Modules:
  0.0 67.6 jit_solution(13834642409329410114)
XLA Ops:
  0.6 1.4 %shard_map.58 = f32[384,128]{1,0:T(8,128)} custom-call(f32[12,1,128]{2,1,0:T(1,128)} %bitcast.11), custom_call_target="tpu_custom_call" | custom-call | tf_op jit(solution)/shard_map/pallas_call | solution.py:208
  2.0 12.0 %all-to-all-start = ((f32[32,12,1,128]{3,2,1,0:T(1,128)}), f32[32,12,1,128]{3,2,1,0:T(1,128)S(1)}, u32[]{:S(2)}, u32[]{:S(2)}) async-start(f32[32,12,1,128]{3,2,1,0:T(1,128)} %bitcast.3), calls=%async_computation | async-start | bytes 393216 | tf_op jit(solution)/shard_map/all_to_all | solution.py:39
  14.1 2.6 %collective-permute-start.2 = (f32[1,256,128]{2,1,0:T(8,128)}, f32[1,256,128]{2,1,0:T(8,128)S(1)}, u32[]{:S(2)}, u32[]{:S(2)}) collective-permute-start(f32[1,256,128]{2,1,0:T(8,128)} %own_hbm.1), channel_id=1, source_target_pairs={{0,6},{1,7},{2,0},{3,1},{4,2},{5,3},{6,4},{7,5},{8,14},{9,15},{10,... | collective-permute-start | bytes 393224 | tf_op jit(solution)/shard_map/ppermute | solution.py:225
  16.6 0.5 collective-permute-start.1
  17.2 0.6 collective-permute-start
  17.8 1.8 %collective-permute-start.3 = (f32[1,256,128]{2,1,0:T(8,128)}, f32[1,256,128]{2,1,0:T(8,128)S(1)}, u32[]{:S(2)}, u32[]{:S(2)}) collective-permute-start(f32[1,256,128]{2,1,0:T(8,128)} %own_hbm.1), channel_id=1, source_target_pairs={{0,32},{1,33},{2,34},{3,35},{4,36},{5,37},{6,38},{7,39},{8,40},{9,... | collective-permute-start | bytes 393224 | tf_op jit(solution)/shard_map/ppermute | solution.py:225
  19.6 0.0 collective-permute-done.2.p3
  19.6 3.9 %collective-permute-start.6 = (f32[1,256,128]{2,1,0:T(8,128)S(1)}, f32[1,256,128]{2,1,0:T(8,128)S(1)}, u32[]{:S(2)}, u32[]{:S(2)}) collective-permute-start(f32[1,256,128]{2,1,0:T(8,128)S(1)} %collective-permute-done.2.p3), channel_id=1, source_target_pairs={{0,32},{1,33},{2,34},{3,35},{4,36},{5,37},{6,38},{7,39},{8,40},{9,... | collective-permute-start | bytes 393224 | tf_op jit(solution)/shard_map/ppermute | solution.py:225
  23.5 0.0 collective-permute-done.1.p2
  23.5 2.2 %collective-permute-start.5 = (f32[1,256,128]{2,1,0:T(8,128)S(1)}, f32[1,256,128]{2,1,0:T(8,128)S(1)}, u32[]{:S(2)}, u32[]{:S(2)}) collective-permute-start(f32[1,256,128]{2,1,0:T(8,128)S(1)} %collective-permute-done.1.p2), channel_id=1, source_target_pairs={{0,32},{1,33},{2,34},{3,35},{4,36},{5,37},{6,38},{7,39},{8,40},{9,... | collective-permute-start | bytes 393224 | tf_op jit(solution)/shard_map/ppermute | solution.py:225
  25.7 0.3 collective-permute-done.p1
  26.0 1.0 %collective-permute-start.4 = (f32[1,256,128]{2,1,0:T(8,128)S(1)}, f32[1,256,128]{2,1,0:T(8,128)S(1)}, u32[]{:S(2)}, u32[]{:S(2)}) collective-permute-start(f32[1,256,128]{2,1,0:T(8,128)S(1)} %collective-permute-done.p1), channel_id=1, source_target_pairs={{0,32},{1,33},{2,34},{3,35},{4,36},{5,37},{6,38},{7,39},{8,40},{9,... | collective-permute-start | bytes 393224 | tf_op jit(solution)/shard_map/ppermute | solution.py:225
  27.1 0.0 collective-permute-done.3.p4
  27.1 0.0 collective-permute-done.6.p7
  27.1 0.0 collective-permute-done.5.p6
  27.1 1.0 %collective-permute-done.4.p5 = f32[1,256,128]{2,1,0:T(8,128)S(1)} collective-permute-done((f32[1,256,128]{2,1,0:T(8,128)S(1)}, f32[1,256,128]{2,1,0:T(8,128)S(1)}, u32[]{:S(2)}, u32[]{:S(2)}) %collective-permute-start.4) | collective-permute-done | bytes 131104 | tf_op jit(solution)/shard_map/ppermute | solution.py:225
  28.1 0.0 all-to-all-done
  28.1 3.7 %shard_map.59 = (bf16[8,256,384]{2,1,0:T(8,128)(2,1)S(1)}, bf16[8,256,384]{2,1,0:T(8,128)(2,1)S(1)}, f32[128,384]{1,0:T(8,128)S(1)}, f32[8,128]{1,0:T(8,128)S(1)...) custom-call(s32[1]{0:T(128)} %bitcast.me_ref, ...), custom_call_target="tpu_custom_call" | custom-call | tf_op jit(solution)/shard_map/pallas_call | solution.py:208
  31.7 13.0 %all_to_all.15.stats_ref = f32[32,1,128]{2,1,0:T(1,128)S(1)} all-to-all(f32[32,1,128]{2,1,0:T(1,128)S(1)} %get-tuple-element.22), channel_id=1, replica_groups={{128,129,136,137,144,145,152,153,192,193,200,201,208,209,216,217,0,1,8,..., dimensions={0} | all-to-all | bytes 32768 | tf_op jit(solution)/shard_map/all_to_all | solution.py:39
  44.7 1.2 %shard_map.60 = (f32[1032,128]{1,0:T(8,128)S(1)}, f32[8,384]{1,0:T(8,128)S(1)}) custom-call(f32[32,1,128]{2,1,0:T(1,128)S(1)} %all_to_all.15.stats_ref, f32[8,128]{1,0:T(8,128)S(1)} %get-tuple-element.23.logits_ref, f32[8,128]{1,0:T(8,128)S(1)} %get-tuple-element.24.chosen_ref, f32[8,384]{1,0:T(8,128)S(1)} %get-tuple-element.25.scale_ref, ...), custom_call_target="tpu_custom_call" | custom-call | tf_op jit(solution)/shard_map/pallas_call | solution.py:208
  45.9 1.9 %collective-permute-start.7 = (f32[1032,128]{1,0:T(8,128)S(1)}, f32[1032,128]{1,0:T(8,128)S(1)}, u32[]{:S(2)}, u32[]{:S(2)}) collective-permute-start(f32[1032,128]{1,0:T(8,128)S(1)} %get-tuple-element.32), channel_id=1, source_target_pairs={{0,32},{1,33},{2,34},{3,35},{4,36},{5,37},{6,38},{7,39},{8,40},{9,... | collective-permute-start | bytes 1585160 | tf_op jit(solution)/shard_map/ppermute | solution.py:225
  47.8 1.5 %shard_map.61 = (f32[1024,128]{1,0:T(8,128)S(1)}, f32[384,128]{1,0:T(8,128)}) custom-call(f32[8,384]{1,0:T(8,128)S(1)} %get-tuple-element.29.factors_ref, f32[128,384]{1,0:T(8,128)S(1)} %get-tuple-element.26.qt_ref, bf16[8,256,384]{2,1,0:T(8,128)(2,1)S(1)} %get-tuple-element.27.whi_ref, bf16[8,256,384]{2,1,0:T(8,128)(2,1)S(1)} %get-tuple-element.28.wlo_ref, ...), custom_call_target="tpu_custom_call" | custom-call | tf_op jit(solution)/shard_map/pallas_call | solution.py:208
  49.3 7.3 %all-to-all-start.2 = ((f32[32,12,1,128]{3,2,1,0:T(1,128)}), f32[32,12,1,128]{3,2,1,0:T(1,128)S(1)}, u32[]{:S(2)}, u32[]{:S(2)}) async-start(f32[32,12,1,128]{3,2,1,0:T(1,128)} %bitcast.5), calls=%async_computation.2 | async-start | bytes 393216 | tf_op jit(solution)/shard_map/all_to_all | solution.py:39
  56.6 0.0 collective-permute-done.7.theirs_ref
  56.6 0.1 shard_map.62
  56.7 0.4 collective-permute-start.8
  57.0 0.5 collective-permute-start.9
  57.6 0.7 collective-permute-start.10
  58.2 8.6 %all-to-all-done.2 = f32[32,12,1,128]{3,2,1,0:T(1,128)S(1)} async-done(((f32[32,12,1,128]{3,2,1,0:T(1,128)}), f32[32,12,1,128]{3,2,1,0:T(1,128)S(1)}, u32[]{:S(2)}, u32[]{:S(2)}) %all-to-all-start.2) | async-done | bytes 196640 | tf_op jit(solution)/shard_map/all_to_all | solution.py:39
  66.8 0.0 collective-permute-done.8.r1
  66.8 0.0 collective-permute-done.9.r2
  66.8 0.1 collective-permute-done.10.r3
  66.9 0.7 %shard_map.63 = (f32[1,256,128]{2,1,0:T(8,128)}, f32[1,1]{1,0:T(1,128)}, f32[12,1,128]{2,1,0:T(1,128)}) custom-call(f32[264,128]{1,0:T(8,128)S(1)} %get-tuple-element.33.r0, f32[264,128]{1,0:T(8,128)S(1)} %collective-permute-done.8.r1, f32[264,128]{1,0:T(8,128)S(1)} %collective-permute-done.9.r2, f32[264,128]{1,0:T(8,128)S(1)} %collective-permute-done.10.r3, ...), custom_call_target="tpu_custom_call" | custom-call | tf_op jit(solution)/shard_map/pallas_call | solution.py:208
  (1 shorter events, 0.0 us)
Async XLA Ops:
  2.0 26.0 %all-to-all-start = ((f32[32,12,1,128]{3,2,1,0:T(1,128)}), f32[32,12,1,128]{3,2,1,0:T(1,128)S(1)}, u32[]{:S(2)}, u32[]{:S(2)}) async-start(f32[32,12,1,128]{3,2,1,0:T(1,128)} %bitcast.3), calls=%async_computation | async-start | bytes 393216 | tf_op jit(solution)/shard_map/all_to_all | solution.py:39
  14.1 5.5 %collective-permute-start.2 = (f32[1,256,128]{2,1,0:T(8,128)}, f32[1,256,128]{2,1,0:T(8,128)S(1)}, u32[]{:S(2)}, u32[]{:S(2)}) collective-permute-start(f32[1,256,128]{2,1,0:T(8,128)} %own_hbm.1), channel_id=1, source_target_pairs={{0,6},{1,7},{2,0},{3,1},{4,2},{5,3},{6,4},{7,5},{8,14},{9,15},{10,... | collective-permute-start | bytes 393224 | tf_op jit(solution)/shard_map/ppermute | solution.py:225
  16.6 6.8 %collective-permute-start.1 = (f32[1,256,128]{2,1,0:T(8,128)}, f32[1,256,128]{2,1,0:T(8,128)S(1)}, u32[]{:S(2)}, u32[]{:S(2)}) collective-permute-start(f32[1,256,128]{2,1,0:T(8,128)} %own_hbm.1), channel_id=1, source_target_pairs={{0,4},{1,5},{2,6},{3,7},{4,0},{5,1},{6,2},{7,3},{8,12},{9,13},{10,... | collective-permute-start | bytes 393224 | tf_op jit(solution)/shard_map/ppermute | solution.py:225
  17.2 8.9 %collective-permute-start = (f32[1,256,128]{2,1,0:T(8,128)}, f32[1,256,128]{2,1,0:T(8,128)S(1)}, u32[]{:S(2)}, u32[]{:S(2)}) collective-permute-start(f32[1,256,128]{2,1,0:T(8,128)} %own_hbm.1), channel_id=1, source_target_pairs={{0,2},{1,3},{2,4},{3,5},{4,6},{5,7},{6,0},{7,1},{8,10},{9,11},{10,... | collective-permute-start | bytes 393224 | tf_op jit(solution)/shard_map/ppermute | solution.py:225
  17.8 9.3 %collective-permute-start.3 = (f32[1,256,128]{2,1,0:T(8,128)}, f32[1,256,128]{2,1,0:T(8,128)S(1)}, u32[]{:S(2)}, u32[]{:S(2)}) collective-permute-start(f32[1,256,128]{2,1,0:T(8,128)} %own_hbm.1), channel_id=1, source_target_pairs={{0,32},{1,33},{2,34},{3,35},{4,36},{5,37},{6,38},{7,39},{8,40},{9,... | collective-permute-start | bytes 393224 | tf_op jit(solution)/shard_map/ppermute | solution.py:225
  19.6 7.5 %collective-permute-start.6 = (f32[1,256,128]{2,1,0:T(8,128)S(1)}, f32[1,256,128]{2,1,0:T(8,128)S(1)}, u32[]{:S(2)}, u32[]{:S(2)}) collective-permute-start(f32[1,256,128]{2,1,0:T(8,128)S(1)} %collective-permute-done.2.p3), channel_id=1, source_target_pairs={{0,32},{1,33},{2,34},{3,35},{4,36},{5,37},{6,38},{7,39},{8,40},{9,... | collective-permute-start | bytes 393224 | tf_op jit(solution)/shard_map/ppermute | solution.py:225
  23.5 3.6 %collective-permute-start.5 = (f32[1,256,128]{2,1,0:T(8,128)S(1)}, f32[1,256,128]{2,1,0:T(8,128)S(1)}, u32[]{:S(2)}, u32[]{:S(2)}) collective-permute-start(f32[1,256,128]{2,1,0:T(8,128)S(1)} %collective-permute-done.1.p2), channel_id=1, source_target_pairs={{0,32},{1,33},{2,34},{3,35},{4,36},{5,37},{6,38},{7,39},{8,40},{9,... | collective-permute-start | bytes 393224 | tf_op jit(solution)/shard_map/ppermute | solution.py:225
  26.0 2.0 %collective-permute-start.4 = (f32[1,256,128]{2,1,0:T(8,128)S(1)}, f32[1,256,128]{2,1,0:T(8,128)S(1)}, u32[]{:S(2)}, u32[]{:S(2)}) collective-permute-start(f32[1,256,128]{2,1,0:T(8,128)S(1)} %collective-permute-done.p1), channel_id=1, source_target_pairs={{0,32},{1,33},{2,34},{3,35},{4,36},{5,37},{6,38},{7,39},{8,40},{9,... | collective-permute-start | bytes 393224 | tf_op jit(solution)/shard_map/ppermute | solution.py:225
  45.9 10.7 %collective-permute-start.7 = (f32[1032,128]{1,0:T(8,128)S(1)}, f32[1032,128]{1,0:T(8,128)S(1)}, u32[]{:S(2)}, u32[]{:S(2)}) collective-permute-start(f32[1032,128]{1,0:T(8,128)S(1)} %get-tuple-element.32), channel_id=1, source_target_pairs={{0,32},{1,33},{2,34},{3,35},{4,36},{5,37},{6,38},{7,39},{8,40},{9,... | collective-permute-start | bytes 1585160 | tf_op jit(solution)/shard_map/ppermute | solution.py:225
  49.3 17.5 %all-to-all-start.2 = ((f32[32,12,1,128]{3,2,1,0:T(1,128)}), f32[32,12,1,128]{3,2,1,0:T(1,128)S(1)}, u32[]{:S(2)}, u32[]{:S(2)}) async-start(f32[32,12,1,128]{3,2,1,0:T(1,128)} %bitcast.5), calls=%async_computation.2 | async-start | bytes 393216 | tf_op jit(solution)/shard_map/all_to_all | solution.py:39
  56.7 10.1 %collective-permute-start.8 = (f32[264,128]{1,0:T(8,128)S(1)}, f32[264,128]{1,0:T(8,128)S(1)}, u32[]{:S(2)}, u32[]{:S(2)}) collective-permute-start(f32[264,128]{1,0:T(8,128)S(1)} %get-tuple-element.34), channel_id=1, source_target_pairs={{0,6},{1,7},{2,0},{3,1},{4,2},{5,3},{6,4},{7,5},{8,14},{9,15},{10,... | collective-permute-start | bytes 405512 | tf_op jit(solution)/shard_map/ppermute | solution.py:225
  57.0 9.8 %collective-permute-start.9 = (f32[264,128]{1,0:T(8,128)S(1)}, f32[264,128]{1,0:T(8,128)S(1)}, u32[]{:S(2)}, u32[]{:S(2)}) collective-permute-start(f32[264,128]{1,0:T(8,128)S(1)} %get-tuple-element.35), channel_id=1, source_target_pairs={{0,4},{1,5},{2,6},{3,7},{4,0},{5,1},{6,2},{7,3},{8,12},{9,13},{10,... | collective-permute-start | bytes 405512 | tf_op jit(solution)/shard_map/ppermute | solution.py:225
  57.6 9.4 %collective-permute-start.10 = (f32[264,128]{1,0:T(8,128)S(1)}, f32[264,128]{1,0:T(8,128)S(1)}, u32[]{:S(2)}, u32[]{:S(2)}) collective-permute-start(f32[264,128]{1,0:T(8,128)S(1)} %get-tuple-element.36), channel_id=1, source_target_pairs={{0,2},{1,3},{2,4},{3,5},{4,6},{5,7},{6,0},{7,1},{8,10},{9,11},{10,... | collective-permute-start | bytes 405512 | tf_op jit(solution)/shard_map/ppermute | solution.py:225

commit v5 on v4

--- a/solution.py
+++ b/solution.py
@@ -97,10 +97,21 @@
     )
 
 
-def score_kernel(
-    me_ref, own_hbm, positive_hbm, q_ref, p1, p2, p3, p4, p5, p6, p7,
-    whi_ref, wlo_ref, qt_ref, logits_ref, scale_ref, chosen_ref, ut_ref, stats_ref,
-    tot_ref, p0, positive_ref, own_sem, positive_sem,
+def page_terms(q_parts, page, s, whi_ref, wlo_ref, tot_ref):
+    scores = product(parts(page), q_parts, ((1,), (0,)))
+    tangent = jnp.tanh(scores * (1.0 / cap_value))
+    grid = jnp.exp(tangent * (cap_value / sharpness_divisor))
+    tot_ref[s : s + 1, :] = jnp.sum(grid, axis=0, keepdims=True)
+    whi_ref[s], wlo_ref[s] = parts(grid * (1.0 - tangent * tangent))
+
+
+def query_terms(page, s, whi_ref, wlo_ref, ut_ref):
+    ut_ref[s] = product(parts(page.T), (whi_ref[s], wlo_ref[s]), ((1,), (0,)))
+
+
+def own_score_kernel(
+    me_ref, own_hbm, positive_hbm, q_ref, p1, p2, p3,
+    whi_ref, wlo_ref, ut_ref, tot_ref, qt_ref, chosen_ref, p0, positive_ref, own_sem, positive_sem,
 ):
     own_copy = pltpu.make_async_copy(own_hbm, p0, own_sem)
     positive_copy = pltpu.make_async_copy(positive_hbm, positive_ref, positive_sem)
@@ -109,46 +120,52 @@
     qt = q_ref[...].T
     qt_ref[...] = qt
     q_parts = parts(qt)
-    pages = (p0, p1, p2, p3, p4, p5, p6, p7)
-    for s, page_ref in [*enumerate(pages)][1:] + [(0, p0)]:
-        if s == 0:
-            own_copy.wait()
-        scores = product(parts(page_ref[0]), q_parts, ((1,), (0,)))
-        tangent = jnp.tanh(scores * (1.0 / cap_value))
-        grid = jnp.exp(tangent * (cap_value / sharpness_divisor))
-        tot_ref[s : s + 1, :] = jnp.sum(grid, axis=0, keepdims=True)
-        whi_ref[s], wlo_ref[s] = parts(grid * (1.0 - tangent * tangent))
+    pages = (p0, p1, p2, p3)
+    for s in range(1, XN):
+        page_terms(q_parts, pages[s][0], s, whi_ref, wlo_ref, tot_ref)
+    own_copy.wait()
+    page_terms(q_parts, p0[0], 0, whi_ref, wlo_ref, tot_ref)
+    for s in range(XN):
+        query_terms(pages[s][0], s, whi_ref, wlo_ref, ut_ref)
+    positive_copy.wait()
+    chosen_ref[...] = is_positive(me_ref, positive_ref).astype(f32)
+
+
+def score_kernel(
+    qt_ref, tot_a_ref, chosen_ref, p0, p1, p2, p3,
+    whi_ref, wlo_ref, ut_ref, logits_ref, scale_ref, stats_ref, tot_ref,
+):
+    tot_ref[0:XN, :] = tot_a_ref[...]
+    q_parts = parts(qt_ref[...])
+    pages = (p0, p1, p2, p3)
+    for s in range(XN):
+        page_terms(q_parts, pages[s][0], s, whi_ref, wlo_ref, tot_ref.at[XN : 2 * XN])
     smooth = sharpness_divisor * jnp.log(tot_ref[...])
     logits = (logit_scale / TOK) * jnp.dot(
         smooth, spread_matrix(), precision=lax.Precision.HIGHEST, preferred_element_type=f32
     )
     logits_ref[...] = logits
-    positive_copy.wait()
-    chosen = is_positive(me_ref, positive_ref)
-    chosen_ref[...] = chosen.astype(f32)
-    scale = (logit_scale / TOK) / tot_ref[...]
-    scale_ref[...] = scale
+    scale_ref[...] = (logit_scale / TOK) / tot_ref[...]
     lane = iota((8, 128), 1)
-    exponential = jnp.exp(logits)
-    matched = jnp.where(chosen, logits, 0.0)
-    local = jnp.where(lane < 32, exponential, jnp.where(lane < 64, matched, 0.0))
+    matched = jnp.where(chosen_ref[...] > 0.5, logits, 0.0)
+    local = jnp.where(lane < 32, jnp.exp(logits), jnp.where(lane < 64, matched, 0.0))
     stats = jnp.sum(local, axis=0, keepdims=True)
-
     stats_ref[...] = jnp.broadcast_to(stats[None], stats_ref.shape)
-    for s, page_ref in enumerate(pages):
-        ut_ref[s] = product(parts(page_ref[0].T), (whi_ref[s], wlo_ref[s]), ((1,), (0,)))
+    for s in range(XN):
+        query_terms(pages[s][0], s, whi_ref, wlo_ref, ut_ref)
 
 
 def page_gradients(whi_ref, wlo_ref, qt, factors, first, out_ref):
     for s in range(XN):
         scaled = parts(qt * factors[first + s : first + s + 1, :])
         out_ref[s * PT : (s + 1) * PT, :] = product(
-            (whi_ref[first + s], wlo_ref[first + s]), scaled, ((1,), (1,))
+            (whi_ref[s], wlo_ref[s]), scaled, ((1,), (1,))
         )
 
 
 def coefficient_kernel(
-    stats_ref, logits_ref, chosen_ref, scale_ref, qt_ref, whi_ref, wlo_ref, out_ref, factors_ref
+    stats_ref, logits_ref, chosen_ref, scale_ref, qt_ref, whi_ref, wlo_ref, ut_a_ref, ut_b_ref,
+    out_ref, factors_ref, dq_ref,
 ):
     stats = jnp.sum(stats_ref[...], axis=0)
     lane = iota((1, 128), 1)
@@ -163,16 +180,16 @@
     coefficients = (slope * jnp.exp(logits_ref[...]) / totals - chosen_ref[...]) * (1.0 / NQ)
     factors = by_row(coefficients) * scale_ref[...]
     factors_ref[...] = factors
+    total = jnp.zeros((W, ROWS), f32)
+    for s in range(XN):
+        total = total + ut_a_ref[s] * factors[s : s + 1, :]
+        total = total + ut_b_ref[s] * factors[XN + s : XN + s + 1, :]
+    dq_ref[...] = total.T
     page_gradients(whi_ref, wlo_ref, qt_ref[...], factors, XN, out_ref)
 
 
-def own_gradient_kernel(factors_ref, qt_ref, whi_ref, wlo_ref, ut_ref, out_ref, dq_ref):
-    factors = factors_ref[...]
-    total = jnp.zeros((W, ROWS), f32)
-    for s in range(2 * XN):
-        total = total + ut_ref[s] * factors[s : s + 1, :]
-    dq_ref[...] = total.T
-    page_gradients(whi_ref, wlo_ref, qt_ref[...], factors, 0, out_ref)
+def own_gradient_kernel(factors_ref, qt_ref, whi_ref, wlo_ref, out_ref):
+    page_gradients(whi_ref, wlo_ref, qt_ref[...], factors_ref[...], 0, out_ref)
 
 
 def pair_kernel(mine_ref, loss_ref, theirs_ref, o0, o1, o2, o3):
@@ -237,24 +254,26 @@
     own = [pages] + [moved(pages, X, s) for s in range(1, XN)]
     other = [moved(page, CO, 1) for page in own]
 
-    weights, block_scalars = ((2 * XN, PT, ROWS), bf16), ((8, 128), f32)
-    whi, wlo, qt, logits, scale, chosen, ut, stats = call(
+    weights, terms = ((XN, PT, ROWS), bf16), ((XN, W, ROWS), f32)
+    whi_a, wlo_a, ut_a, tot_a, qt, chosen = call(
+        own_score_kernel,
+        [weights, weights, terms, ((XN, ROWS), f32), ((W, ROWS), f32), ((8, 128), f32)],
+        [pltpu.VMEM((1, PT, W), f32), pltpu.VMEM((1, NQ), jnp.int32),
+         pltpu.SemaphoreType.DMA, pltpu.SemaphoreType.DMA],
+        scalars=1, anywhere=2,
+    )(me, pages, positive, block, *own[1:])
+    whi_b, wlo_b, ut_b, logits, scale, stats = call(
         score_kernel,
-        [weights, weights, ((W, ROWS), f32), block_scalars, ((2 * XN, ROWS), f32), block_scalars,
-         ((2 * XN, W, ROWS), f32), ((QN, 1, W), f32)],
-        [pltpu.VMEM((2 * XN, ROWS), f32), pltpu.VMEM((1, PT, W), f32),
-         pltpu.VMEM((1, NQ), jnp.int32), pltpu.SemaphoreType.DMA, pltpu.SemaphoreType.DMA],
-        scalars=1, anywhere=2,
-    )(me, pages, positive, block, *own[1:], *other)
+        [weights, weights, terms, ((8, 128), f32), ((2 * XN, ROWS), f32), ((QN, 1, W), f32)],
+        [pltpu.VMEM((2 * XN, ROWS), f32)],
+    )(qt, tot_a, chosen, *other)
     stats = exchange(stats, STATS_TURN)
-    theirs, factors = call(
-        coefficient_kernel, [((XN * PT + 8, W), f32), ((2 * XN, ROWS), f32)]
-    )(stats, logits, chosen, scale, qt, whi, wlo)
+    theirs, factors, dq = call(
+        coefficient_kernel, [((XN * PT + 8, W), f32), ((2 * XN, ROWS), f32), ((ROWS, W), f32)]
+    )(stats, logits, chosen, scale, qt, whi_b, wlo_b, ut_a, ut_b)
     loss_rows = theirs[XN * PT :]
     theirs = moved(theirs, CO, 1)
-    mine, dq = call(own_gradient_kernel, [((XN * PT, W), f32), ((ROWS, W), f32)])(
-        factors, qt, whi, wlo, ut
-    )
+    (mine,) = call(own_gradient_kernel, [((XN * PT, W), f32)])(factors, qt, whi_a, wlo_a)
     blocks = call(pair_kernel, [((PT + 8, W), f32)] * XN)(mine, loss_rows, theirs)
     blocks = [blocks[0]] + [moved(blocks[s], X, -s) for s in range(1, XN)]
     dq = exchange(dq.reshape(QN, TOK, 1, W), QUERY_TURN)

time: 68 us -> 67.4 us (level)
  waiting for transfers between devices: 10 us -> 9.12 us
    all_to_all x2, waiting for transfers between devices: 8.57 us -> 7.47 us  [exchange(): lax.all_to_all(value, 'd', 0, 0, axis_index_groups=groups(turn), tiled=True)]
    pallas_call x6 -> x7, Pallas kernels: 8.5 us -> 9.05 us  [run(): pl.pallas_call(kernel, out_shape=[jax.ShapeDtypeStruct(s, d) for s, d in...]
  transfers between devices with their start and end apart: 13 -> 13, of which waited for: 4 -> 3; matrix products, arithmetic and copies ran while one was open for 0% -> 0% of each run, Pallas kernels for 2% -> 5%
where the time goes in v5:
time: 67.4 us; the launch traced here: 67.1 us
  starting transfers between devices  35.2 us (52%)
  blocking collectives  13 us (19%)
  waiting for transfers between devices  9.12 us (14%)
  Pallas kernels  9.05 us (13%)
  between operations  0.74 us (1%)
    all_to_all x2, starting transfers between devices, exchange(): lax.all_to_all(value, 'd', 0, 0, axis_index_groups=groups(turn), tiled=True)  19.4 us
    ppermute x11, starting transfers between devices, moved(): return lax.ppermute(value, 'd', pairs)  15.7 us
    all_to_all x1, blocking collectives, exchange(): lax.all_to_all(value, 'd', 0, 0, axis_index_groups=groups(turn), tiled=True)  13 us
    pallas_call x7, Pallas kernels, run(): pl.pallas_call(kernel, out_shape=[jax.ShapeDtypeStruct(s, d) for s, d in...  9.05 us
    all_to_all x2, waiting for transfers between devices, exchange(): lax.all_to_all(value, 'd', 0, 0, axis_index_groups=groups(turn), tiled=True)  7.47 us
    ppermute x11, waiting for transfers between devices, moved(): return lax.ppermute(value, 'd', pairs)  1.65 us
  transfers between devices with their start and end apart: 13, of which 3 were waited for; matrix products, arithmetic and copies ran while one was open for 0% of the time, Pallas kernels for 5%

profile of v5, /device:TPU:1, one launch (start us, length us, event | category | flops | bytes accessed | tf_op | source)
XLA Modules:
  0.0 67.1 jit_solution(3989500334789629642)
XLA Ops:
  0.6 1.4 %shard_map.58 = f32[384,128]{1,0:T(8,128)} custom-call(f32[12,1,128]{2,1,0:T(1,128)} %bitcast.11), custom_call_target="tpu_custom_call" | custom-call | tf_op jit(solution)/shard_map/pallas_call | solution.py:225
  2.0 0.0 copy-start
  2.0 12.2 %all-to-all-start = ((f32[32,12,1,128]{3,2,1,0:T(1,128)}), f32[32,12,1,128]{3,2,1,0:T(1,128)S(1)}, u32[]{:S(2)}, u32[]{:S(2)}) async-start(f32[32,12,1,128]{3,2,1,0:T(1,128)} %bitcast.3), calls=%async_computation | async-start | bytes 393216 | tf_op jit(solution)/shard_map/all_to_all | solution.py:39
  14.2 0.0 copy-done
  14.2 2.6 %collective-permute-start.2 = (f32[1,256,128]{2,1,0:T(8,128)S(1)}, f32[1,256,128]{2,1,0:T(8,128)S(1)}, u32[]{:S(2)}, u32[]{:S(2)}) collective-permute-start(f32[1,256,128]{2,1,0:T(8,128)S(1)} %copy-done), channel_id=1, source_target_pairs={{0,6},{1,7},{2,0},{3,1},{4,2},{5,3},{6,4},{7,5},{8,14},{9,15},{10,... | collective-permute-start | bytes 393224 | tf_op jit(solution)/shard_map/ppermute | solution.py:242
  16.8 0.5 collective-permute-start.1
  17.3 0.6 collective-permute-start
  17.9 1.8 %collective-permute-start.3 = (f32[1,256,128]{2,1,0:T(8,128)S(1)}, f32[1,256,128]{2,1,0:T(8,128)S(1)}, u32[]{:S(2)}, u32[]{:S(2)}) collective-permute-start(f32[1,256,128]{2,1,0:T(8,128)S(1)} %copy-done), channel_id=1, source_target_pairs={{0,32},{1,33},{2,34},{3,35},{4,36},{5,37},{6,38},{7,39},{8,40},{9,... | collective-permute-start | bytes 393224 | tf_op jit(solution)/shard_map/ppermute | solution.py:242
  19.7 0.0 collective-permute-done.2.p3
  19.7 3.6 %collective-permute-start.6 = (f32[1,256,128]{2,1,0:T(8,128)S(1)}, f32[1,256,128]{2,1,0:T(8,128)S(1)}, u32[]{:S(2)}, u32[]{:S(2)}) collective-permute-start(f32[1,256,128]{2,1,0:T(8,128)S(1)} %collective-permute-done.2.p3), channel_id=1, source_target_pairs={{0,32},{1,33},{2,34},{3,35},{4,36},{5,37},{6,38},{7,39},{8,40},{9,... | collective-permute-start | bytes 393224 | tf_op jit(solution)/shard_map/ppermute | solution.py:242
  23.3 0.0 collective-permute-done.1.p2
  23.3 2.3 %collective-permute-start.5 = (f32[1,256,128]{2,1,0:T(8,128)S(1)}, f32[1,256,128]{2,1,0:T(8,128)S(1)}, u32[]{:S(2)}, u32[]{:S(2)}) collective-permute-start(f32[1,256,128]{2,1,0:T(8,128)S(1)} %collective-permute-done.1.p2), channel_id=1, source_target_pairs={{0,32},{1,33},{2,34},{3,35},{4,36},{5,37},{6,38},{7,39},{8,40},{9,... | collective-permute-start | bytes 393224 | tf_op jit(solution)/shard_map/ppermute | solution.py:242
  25.6 0.3 collective-permute-done.p1
  26.0 1.0 %collective-permute-start.4 = (f32[1,256,128]{2,1,0:T(8,128)S(1)}, f32[1,256,128]{2,1,0:T(8,128)S(1)}, u32[]{:S(2)}, u32[]{:S(2)}) collective-permute-start(f32[1,256,128]{2,1,0:T(8,128)S(1)} %collective-permute-done.p1), channel_id=1, source_target_pairs={{0,32},{1,33},{2,34},{3,35},{4,36},{5,37},{6,38},{7,39},{8,40},{9,... | collective-permute-start | bytes 393224 | tf_op jit(solution)/shard_map/ppermute | solution.py:242
  27.0 0.0 all-to-all-done
  27.0 2.4 %shard_map.59 = (bf16[4,256,384]{2,1,0:T(8,128)(2,1)S(1)}, bf16[4,256,384]{2,1,0:T(8,128)(2,1)S(1)}, f32[4,128,384]{2,1,0:T(8,128)S(1)}, f32[4,384]{1,0:T(4,128)...) custom-call(s32[1]{0:T(128)} %bitcast.me_ref, f32[1,256,128]{2,1,0:T(8,128)} %own_hbm.1, s32[1,256]{1,0:T(1,128)} %bitcast.12, ...), custom_call_target="tpu_custom_call" | custom-call | tf_op jit(solution)/shard_map/pallas_call | solution.py:225
  29.4 0.0 collective-permute-done.3.p0
  29.4 0.0 collective-permute-done.6.p3
  29.4 0.0 collective-permute-done.5.p2
  29.4 0.0 collective-permute-done.4.p1
  29.5 1.8 %shard_map.60 = (bf16[4,256,384]{2,1,0:T(8,128)(2,1)S(1)}, bf16[4,256,384]{2,1,0:T(8,128)(2,1)S(1)}, f32[4,128,384]{2,1,0:T(8,128)S(1)}, f32[8,128]{1,0:T(8,128)...) custom-call(f32[128,384]{1,0:T(8,128)S(1)} %get-tuple-element.25.qt_ref, ...), custom_call_target="tpu_custom_call" | custom-call | tf_op jit(solution)/shard_map/pallas_call | solution.py:225
  31.3 13.0 %all_to_all.15.stats_ref = f32[32,1,128]{2,1,0:T(1,128)S(1)} all-to-all(f32[32,1,128]{2,1,0:T(1,128)S(1)} %get-tuple-element.28), channel_id=1, replica_groups={{128,129,136,137,144,145,152,153,192,193,200,201,208,209,216,217,0,1,8,..., dimensions={0} | all-to-all | bytes 32768 | tf_op jit(solution)/shard_map/all_to_all | solution.py:39
  44.3 1.9 %shard_map.61 = (f32[1032,128]{1,0:T(8,128)S(1)}, f32[8,384]{1,0:T(8,128)S(1)}, f32[384,128]{1,0:T(8,128)}) custom-call(f32[32,1,128]{2,1,0:T(1,128)S(1)} %all_to_all.15.stats_ref, f32[8,128]{1,0:T(8,128)S(1)} %get-tuple-element.29.logits_ref, f32[8,128]{1,0:T(8,128)S(1)} %get-tuple-element.27.chosen_ref, f32[8,384]{1,0:T(8,128)S(1)} %get-tuple-element.30.scale_ref, ...), custom_call_target="tpu_custom_call" | custom-call | tf_op jit(solution)/shard_map/pallas_call | solution.py:225
  46.2 1.4 %collective-permute-start.7 = (f32[1032,128]{1,0:T(8,128)S(1)}, f32[1032,128]{1,0:T(8,128)S(1)}, u32[]{:S(2)}, u32[]{:S(2)}) collective-permute-start(f32[1032,128]{1,0:T(8,128)S(1)} %get-tuple-element.38), channel_id=1, source_target_pairs={{0,32},{1,33},{2,34},{3,35},{4,36},{5,37},{6,38},{7,39},{8,40},{9,... | collective-permute-start | bytes 1585160 | tf_op jit(solution)/shard_map/ppermute | solution.py:242
  47.6 7.3 %all-to-all-start.2 = ((f32[32,12,1,128]{3,2,1,0:T(1,128)}), f32[32,12,1,128]{3,2,1,0:T(1,128)S(1)}, u32[]{:S(2)}, u32[]{:S(2)}) async-start(f32[32,12,1,128]{3,2,1,0:T(1,128)} %bitcast.5), calls=%async_computation.2 | async-start | bytes 393216 | tf_op jit(solution)/shard_map/all_to_all | solution.py:39
  54.9 0.8 %shard_map.62.mine_ref = f32[1024,128]{1,0:T(8,128)S(1)} custom-call(f32[8,384]{1,0:T(8,128)S(1)} %get-tuple-element.35.factors_ref, f32[128,384]{1,0:T(8,128)S(1)} %get-tuple-element.25.qt_ref, bf16[4,256,384]{2,1,0:T(8,128)(2,1)S(1)} %get-tuple-element.36.whi_ref, bf16[4,256,384]{2,1,0:T(8,128)(2,1)S(1)} %get-tuple-element.37.wlo_ref), custom_call_target="tpu_custom_call" | custom-call | tf_op jit(solution)/shard_map/pallas_call | solution.py:225
  55.7 0.0 collective-permute-done.7.theirs_ref
  55.7 0.1 shard_map.63
  55.8 0.7 %collective-permute-start.8 = (f32[264,128]{1,0:T(8,128)S(1)}, f32[264,128]{1,0:T(8,128)S(1)}, u32[]{:S(2)}, u32[]{:S(2)}) collective-permute-start(f32[264,128]{1,0:T(8,128)S(1)} %get-tuple-element.40), channel_id=1, source_target_pairs={{0,6},{1,7},{2,0},{3,1},{4,2},{5,3},{6,4},{7,5},{8,14},{9,15},{10,... | collective-permute-start | bytes 405512 | tf_op jit(solution)/shard_map/ppermute | solution.py:242
  56.5 0.5 collective-permute-start.9
  57.0 0.6 collective-permute-start.10
  57.6 7.5 %all-to-all-done.2 = f32[32,12,1,128]{3,2,1,0:T(1,128)S(1)} async-done(((f32[32,12,1,128]{3,2,1,0:T(1,128)}), f32[32,12,1,128]{3,2,1,0:T(1,128)S(1)}, u32[]{:S(2)}, u32[]{:S(2)}) %all-to-all-start.2) | async-done | bytes 196640 | tf_op jit(solution)/shard_map/all_to_all | solution.py:39
  65.1 0.0 collective-permute-done.8.r1
  65.1 0.0 collective-permute-done.9.r2
  65.1 1.3 %collective-permute-done.10.r3 = f32[264,128]{1,0:T(8,128)S(1)} collective-permute-done((f32[264,128]{1,0:T(8,128)S(1)}, f32[264,128]{1,0:T(8,128)S(1)}, u32[]{:S(2)}, u32[]{:S(2)}) %collective-permute-start.10) | collective-permute-done | bytes 135200 | tf_op jit(solution)/shard_map/ppermute | solution.py:242
  66.4 0.7 %shard_map.64 = (f32[1,256,128]{2,1,0:T(8,128)}, f32[1,1]{1,0:T(1,128)}, f32[12,1,128]{2,1,0:T(1,128)}) custom-call(f32[264,128]{1,0:T(8,128)S(1)} %get-tuple-element.39.r0, f32[264,128]{1,0:T(8,128)S(1)} %collective-permute-done.8.r1, f32[264,128]{1,0:T(8,128)S(1)} %collective-permute-done.9.r2, f32[264,128]{1,0:T(8,128)S(1)} %collective-permute-done.10.r3, ...), custom_call_target="tpu_custom_call" | custom-call | tf_op jit(solution)/shard_map/pallas_call | solution.py:225
  (1 shorter events, 0.0 us)
Async XLA Ops:
  2.0 12.2 %copy-start = (f32[1,256,128]{2,1,0:T(8,128)S(1)}, f32[1,256,128]{2,1,0:T(8,128)}, u32[]{:S(2)}) copy-start(f32[1,256,128]{2,1,0:T(8,128)} %own_hbm.1) | copy-start | bytes 393220
  2.0 25.0 %all-to-all-start = ((f32[32,12,1,128]{3,2,1,0:T(1,128)}), f32[32,12,1,128]{3,2,1,0:T(1,128)S(1)}, u32[]{:S(2)}, u32[]{:S(2)}) async-start(f32[32,12,1,128]{3,2,1,0:T(1,128)} %bitcast.3), calls=%async_computation | async-start | bytes 393216 | tf_op jit(solution)/shard_map/all_to_all | solution.py:39
  14.2 5.5 %collective-permute-start.2 = (f32[1,256,128]{2,1,0:T(8,128)S(1)}, f32[1,256,128]{2,1,0:T(8,128)S(1)}, u32[]{:S(2)}, u32[]{:S(2)}) collective-permute-start(f32[1,256,128]{2,1,0:T(8,128)S(1)} %copy-done), channel_id=1, source_target_pairs={{0,6},{1,7},{2,0},{3,1},{4,2},{5,3},{6,4},{7,5},{8,14},{9,15},{10,... | collective-permute-start | bytes 393224 | tf_op jit(solution)/shard_map/ppermute | solution.py:242
  16.8 6.5 %collective-permute-start.1 = (f32[1,256,128]{2,1,0:T(8,128)S(1)}, f32[1,256,128]{2,1,0:T(8,128)S(1)}, u32[]{:S(2)}, u32[]{:S(2)}) collective-permute-start(f32[1,256,128]{2,1,0:T(8,128)S(1)} %copy-done), channel_id=1, source_target_pairs={{0,4},{1,5},{2,6},{3,7},{4,0},{5,1},{6,2},{7,3},{8,12},{9,13},{10,... | collective-permute-start | bytes 393224 | tf_op jit(solution)/shard_map/ppermute | solution.py:242
  17.3 8.7 %collective-permute-start = (f32[1,256,128]{2,1,0:T(8,128)S(1)}, f32[1,256,128]{2,1,0:T(8,128)S(1)}, u32[]{:S(2)}, u32[]{:S(2)}) collective-permute-start(f32[1,256,128]{2,1,0:T(8,128)S(1)} %copy-done), channel_id=1, source_target_pairs={{0,2},{1,3},{2,4},{3,5},{4,6},{5,7},{6,0},{7,1},{8,10},{9,11},{10,... | collective-permute-start | bytes 393224 | tf_op jit(solution)/shard_map/ppermute | solution.py:242
  17.9 11.5 %collective-permute-start.3 = (f32[1,256,128]{2,1,0:T(8,128)S(1)}, f32[1,256,128]{2,1,0:T(8,128)S(1)}, u32[]{:S(2)}, u32[]{:S(2)}) collective-permute-start(f32[1,256,128]{2,1,0:T(8,128)S(1)} %copy-done), channel_id=1, source_target_pairs={{0,32},{1,33},{2,34},{3,35},{4,36},{5,37},{6,38},{7,39},{8,40},{9,... | collective-permute-start | bytes 393224 | tf_op jit(solution)/shard_map/ppermute | solution.py:242
  19.7 9.7 %collective-permute-start.6 = (f32[1,256,128]{2,1,0:T(8,128)S(1)}, f32[1,256,128]{2,1,0:T(8,128)S(1)}, u32[]{:S(2)}, u32[]{:S(2)}) collective-permute-start(f32[1,256,128]{2,1,0:T(8,128)S(1)} %collective-permute-done.2.p3), channel_id=1, source_target_pairs={{0,32},{1,33},{2,34},{3,35},{4,36},{5,37},{6,38},{7,39},{8,40},{9,... | collective-permute-start | bytes 393224 | tf_op jit(solution)/shard_map/ppermute | solution.py:242
  23.3 6.1 %collective-permute-start.5 = (f32[1,256,128]{2,1,0:T(8,128)S(1)}, f32[1,256,128]{2,1,0:T(8,128)S(1)}, u32[]{:S(2)}, u32[]{:S(2)}) collective-permute-start(f32[1,256,128]{2,1,0:T(8,128)S(1)} %collective-permute-done.1.p2), channel_id=1, source_target_pairs={{0,32},{1,33},{2,34},{3,35},{4,36},{5,37},{6,38},{7,39},{8,40},{9,... | collective-permute-start | bytes 393224 | tf_op jit(solution)/shard_map/ppermute | solution.py:242
  26.0 3.5 %collective-permute-start.4 = (f32[1,256,128]{2,1,0:T(8,128)S(1)}, f32[1,256,128]{2,1,0:T(8,128)S(1)}, u32[]{:S(2)}, u32[]{:S(2)}) collective-permute-start(f32[1,256,128]{2,1,0:T(8,128)S(1)} %collective-permute-done.p1), channel_id=1, source_target_pairs={{0,32},{1,33},{2,34},{3,35},{4,36},{5,37},{6,38},{7,39},{8,40},{9,... | collective-permute-start | bytes 393224 | tf_op jit(solution)/shard_map/ppermute | solution.py:242
  46.2 9.5 %collective-permute-start.7 = (f32[1032,128]{1,0:T(8,128)S(1)}, f32[1032,128]{1,0:T(8,128)S(1)}, u32[]{:S(2)}, u32[]{:S(2)}) collective-permute-start(f32[1032,128]{1,0:T(8,128)S(1)} %get-tuple-element.38), channel_id=1, source_target_pairs={{0,32},{1,33},{2,34},{3,35},{4,36},{5,37},{6,38},{7,39},{8,40},{9,... | collective-permute-start | bytes 1585160 | tf_op jit(solution)/shard_map/ppermute | solution.py:242
  47.6 17.5 %all-to-all-start.2 = ((f32[32,12,1,128]{3,2,1,0:T(1,128)}), f32[32,12,1,128]{3,2,1,0:T(1,128)S(1)}, u32[]{:S(2)}, u32[]{:S(2)}) async-start(f32[32,12,1,128]{3,2,1,0:T(1,128)} %bitcast.5), calls=%async_computation.2 | async-start | bytes 393216 | tf_op jit(solution)/shard_map/all_to_all | solution.py:39
  55.8 9.3 %collective-permute-start.8 = (f32[264,128]{1,0:T(8,128)S(1)}, f32[264,128]{1,0:T(8,128)S(1)}, u32[]{:S(2)}, u32[]{:S(2)}) collective-permute-start(f32[264,128]{1,0:T(8,128)S(1)} %get-tuple-element.40), channel_id=1, source_target_pairs={{0,6},{1,7},{2,0},{3,1},{4,2},{5,3},{6,4},{7,5},{8,14},{9,15},{10,... | collective-permute-start | bytes 405512 | tf_op jit(solution)/shard_map/ppermute | solution.py:242
  56.5 8.6 %collective-permute-start.9 = (f32[264,128]{1,0:T(8,128)S(1)}, f32[264,128]{1,0:T(8,128)S(1)}, u32[]{:S(2)}, u32[]{:S(2)}) collective-permute-start(f32[264,128]{1,0:T(8,128)S(1)} %get-tuple-element.41), channel_id=1, source_target_pairs={{0,4},{1,5},{2,6},{3,7},{4,0},{5,1},{6,2},{7,3},{8,12},{9,13},{10,... | collective-permute-start | bytes 405512 | tf_op jit(solution)/shard_map/ppermute | solution.py:242
  57.0 9.4 %collective-permute-start.10 = (f32[264,128]{1,0:T(8,128)S(1)}, f32[264,128]{1,0:T(8,128)S(1)}, u32[]{:S(2)}, u32[]{:S(2)}) collective-permute-start(f32[264,128]{1,0:T(8,128)S(1)} %get-tuple-element.42), channel_id=1, source_target_pairs={{0,2},{1,3},{2,4},{3,5},{4,6},{5,7},{6,0},{7,1},{8,10},{9,11},{10,... | collective-permute-start | bytes 405512 | tf_op jit(solution)/shard_map/ppermute | solution.py:242

commit v6 on v5

--- a/solution.py
+++ b/solution.py
@@ -9,8 +9,8 @@
 DEVICES = 256
 CO, X = (5, 1), (1, 3)
 QN = 32
-QUERY_TURN = 0
-STATS_TURN = 16
+QUERY_ORDER = (0, 1)
+STATS_ORDER = (7, -1)
 XN = 4
 TOK = 12
 ROWS = QN * TOK
@@ -30,13 +30,14 @@
     return ((member >> 3) << 6) + (((member >> 1) & 3) << 3) + (member & 1)
 
 
-def groups(turn):
-    members = [offset_of((k - turn) % QN) for k in range(QN)]
+def groups(order):
+    first, step = order
+    members = [offset_of((first + step * k) % QN) for k in range(QN)]
     return [[(co << 5) + (x << 1) + m for m in members] for co in range(2) for x in range(XN)]
 
 
-def exchange(value, turn):
-    return lax.all_to_all(value, "d", 0, 0, axis_index_groups=groups(turn), tiled=True)
+def exchange(value, order):
+    return lax.all_to_all(value, "d", 0, 0, axis_index_groups=groups(order), tiled=True)
 
 
 def iota(shape, dim):
@@ -78,7 +79,7 @@
     me = me_ref[0]
     base = me & 0b00100110
     index, lane = iota((NQ, 128), 0), iota((NQ, 128), 1)
-    query = offset_of((lane - QUERY_TURN) & (QN - 1)) + base
+    query = offset_of((QUERY_ORDER[0] + QUERY_ORDER[1] * lane) & (QN - 1)) + base
     chosen = jnp.dot(
         positive_ref[...].astype(f32), (index == query).astype(f32), precision=lax.Precision.HIGHEST,
         preferred_element_type=f32,
@@ -250,7 +251,7 @@
         [pltpu.VMEM((TOK, 1, W), f32), pltpu.VMEM((2 * TOK, W), f32), pltpu.SemaphoreType.DMA],
         anywhere=1,
     )(queries.transpose(1, 0, 2))
-    block = exchange(spread.reshape(QN, TOK, 1, W), QUERY_TURN).reshape(ROWS, W)
+    block = exchange(spread.reshape(QN, TOK, 1, W), QUERY_ORDER).reshape(ROWS, W)
     own = [pages] + [moved(pages, X, s) for s in range(1, XN)]
     other = [moved(page, CO, 1) for page in own]
 
@@ -267,7 +268,7 @@
         [weights, weights, terms, ((8, 128), f32), ((2 * XN, ROWS), f32), ((QN, 1, W), f32)],
         [pltpu.VMEM((2 * XN, ROWS), f32)],
     )(qt, tot_a, chosen, *other)
-    stats = exchange(stats, STATS_TURN)
+    stats = exchange(stats, STATS_ORDER)
     theirs, factors, dq = call(
         coefficient_kernel, [((XN * PT + 8, W), f32), ((2 * XN, ROWS), f32), ((ROWS, W), f32)]
     )(stats, logits, chosen, scale, qt, whi_b, wlo_b, ut_a, ut_b)
@@ -276,7 +277,7 @@
     (mine,) = call(own_gradient_kernel, [((XN * PT, W), f32)])(factors, qt, whi_a, wlo_a)
     blocks = call(pair_kernel, [((PT + 8, W), f32)] * XN)(mine, loss_rows, theirs)
     blocks = [blocks[0]] + [moved(blocks[s], X, -s) for s in range(1, XN)]
-    dq = exchange(dq.reshape(QN, TOK, 1, W), QUERY_TURN)
+    dq = exchange(dq.reshape(QN, TOK, 1, W), QUERY_ORDER)
     page_grad, loss, slope = call(
         final_kernel, [((1, PT, W), f32), ((1, 1), f32), ((TOK, 1, W), f32)]
     )(*blocks, dq.reshape(ROWS, W))

time: 67.4 us -> 67.1 us (level)
  starting transfers between devices: 35.2 us -> 31.9 us
  blocking collectives: 13 us -> 15.9 us
    all_to_all x1, blocking collectives: 13 us -> 15.9 us  [exchange(): lax.all_to_all(value, 'd', 0, 0, axis_index_groups=groups(order), tiled=T...]
    all_to_all x2, starting transfers between devices: 19.4 us -> 16.5 us  [exchange(): lax.all_to_all(value, 'd', 0, 0, axis_index_groups=groups(order), tiled=T...]
where the time goes in v6:
time: 67.1 us; the launch traced here: 66.8 us
  starting transfers between devices  31.9 us (48%)
  blocking collectives  15.9 us (24%)
  waiting for transfers between devices  9.09 us (14%)
  Pallas kernels  9.05 us (13%)
  between operations  0.74 us (1%)
    all_to_all x2, starting transfers between devices, exchange(): lax.all_to_all(value, 'd', 0, 0, axis_index_groups=groups(order), tiled=T...  16.5 us
    all_to_all x1, blocking collectives, exchange(): lax.all_to_all(value, 'd', 0, 0, axis_index_groups=groups(order), tiled=T...  15.9 us
    ppermute x11, starting transfers between devices, moved(): return lax.ppermute(value, 'd', pairs)  15.4 us
    pallas_call x7, Pallas kernels, run(): pl.pallas_call(kernel, out_shape=[jax.ShapeDtypeStruct(s, d) for s, d in...  9.05 us
    all_to_all x2, waiting for transfers between devices, exchange(): lax.all_to_all(value, 'd', 0, 0, axis_index_groups=groups(order), tiled=T...  7.79 us
  transfers between devices with their start and end apart: 13, of which 3 were waited for; matrix products, arithmetic and copies ran while one was open for 0% of the time, Pallas kernels for 5%

profile of v6, /device:TPU:1, one launch (start us, length us, event | category | flops | bytes accessed | tf_op | source)
XLA Modules:
  0.0 66.8 jit_solution(10055575358560818715)
XLA Ops:
  0.6 1.4 %shard_map.58 = f32[384,128]{1,0:T(8,128)} custom-call(f32[12,1,128]{2,1,0:T(1,128)} %bitcast.11), custom_call_target="tpu_custom_call" | custom-call | tf_op jit(solution)/shard_map/pallas_call | solution.py:226
  2.0 0.0 copy-start
  2.0 12.2 %all-to-all-start = ((f32[32,12,1,128]{3,2,1,0:T(1,128)}), f32[32,12,1,128]{3,2,1,0:T(1,128)S(1)}, u32[]{:S(2)}, u32[]{:S(2)}) async-start(f32[32,12,1,128]{3,2,1,0:T(1,128)} %bitcast.3), calls=%async_computation | async-start | bytes 393216 | tf_op jit(solution)/shard_map/all_to_all | solution.py:40
  14.2 0.0 copy-done
  14.2 2.6 %collective-permute-start.2 = (f32[1,256,128]{2,1,0:T(8,128)S(1)}, f32[1,256,128]{2,1,0:T(8,128)S(1)}, u32[]{:S(2)}, u32[]{:S(2)}) collective-permute-start(f32[1,256,128]{2,1,0:T(8,128)S(1)} %copy-done), channel_id=1, source_target_pairs={{0,6},{1,7},{2,0},{3,1},{4,2},{5,3},{6,4},{7,5},{8,14},{9,15},{10,... | collective-permute-start | bytes 393224 | tf_op jit(solution)/shard_map/ppermute | solution.py:243
  16.8 0.5 collective-permute-start.1
  17.3 0.6 collective-permute-start
  17.9 1.8 %collective-permute-start.3 = (f32[1,256,128]{2,1,0:T(8,128)S(1)}, f32[1,256,128]{2,1,0:T(8,128)S(1)}, u32[]{:S(2)}, u32[]{:S(2)}) collective-permute-start(f32[1,256,128]{2,1,0:T(8,128)S(1)} %copy-done), channel_id=1, source_target_pairs={{0,32},{1,33},{2,34},{3,35},{4,36},{5,37},{6,38},{7,39},{8,40},{9,... | collective-permute-start | bytes 393224 | tf_op jit(solution)/shard_map/ppermute | solution.py:243
  19.7 0.0 collective-permute-done.2.p3
  19.7 3.6 %collective-permute-start.6 = (f32[1,256,128]{2,1,0:T(8,128)S(1)}, f32[1,256,128]{2,1,0:T(8,128)S(1)}, u32[]{:S(2)}, u32[]{:S(2)}) collective-permute-start(f32[1,256,128]{2,1,0:T(8,128)S(1)} %collective-permute-done.2.p3), channel_id=1, source_target_pairs={{0,32},{1,33},{2,34},{3,35},{4,36},{5,37},{6,38},{7,39},{8,40},{9,... | collective-permute-start | bytes 393224 | tf_op jit(solution)/shard_map/ppermute | solution.py:243
  23.3 0.0 collective-permute-done.1.p2
  23.3 2.3 %collective-permute-start.5 = (f32[1,256,128]{2,1,0:T(8,128)S(1)}, f32[1,256,128]{2,1,0:T(8,128)S(1)}, u32[]{:S(2)}, u32[]{:S(2)}) collective-permute-start(f32[1,256,128]{2,1,0:T(8,128)S(1)} %collective-permute-done.1.p2), channel_id=1, source_target_pairs={{0,32},{1,33},{2,34},{3,35},{4,36},{5,37},{6,38},{7,39},{8,40},{9,... | collective-permute-start | bytes 393224 | tf_op jit(solution)/shard_map/ppermute | solution.py:243
  25.6 0.3 collective-permute-done.p1
  26.0 1.0 %collective-permute-start.4 = (f32[1,256,128]{2,1,0:T(8,128)S(1)}, f32[1,256,128]{2,1,0:T(8,128)S(1)}, u32[]{:S(2)}, u32[]{:S(2)}) collective-permute-start(f32[1,256,128]{2,1,0:T(8,128)S(1)} %collective-permute-done.p1), channel_id=1, source_target_pairs={{0,32},{1,33},{2,34},{3,35},{4,36},{5,37},{6,38},{7,39},{8,40},{9,... | collective-permute-start | bytes 393224 | tf_op jit(solution)/shard_map/ppermute | solution.py:243
  27.0 0.0 all-to-all-done
  27.0 2.4 %shard_map.59 = (bf16[4,256,384]{2,1,0:T(8,128)(2,1)S(1)}, bf16[4,256,384]{2,1,0:T(8,128)(2,1)S(1)}, f32[4,128,384]{2,1,0:T(8,128)S(1)}, f32[4,384]{1,0:T(4,128)...) custom-call(s32[1]{0:T(128)} %bitcast.me_ref, f32[1,256,128]{2,1,0:T(8,128)} %own_hbm.1, s32[1,256]{1,0:T(1,128)} %bitcast.12, ...), custom_call_target="tpu_custom_call" | custom-call | tf_op jit(solution)/shard_map/pallas_call | solution.py:226
  29.4 0.0 collective-permute-done.3.p0
  29.4 0.0 collective-permute-done.6.p3
  29.4 0.0 collective-permute-done.5.p2
  29.4 0.0 collective-permute-done.4.p1
  29.5 1.8 %shard_map.60 = (bf16[4,256,384]{2,1,0:T(8,128)(2,1)S(1)}, bf16[4,256,384]{2,1,0:T(8,128)(2,1)S(1)}, f32[4,128,384]{2,1,0:T(8,128)S(1)}, f32[8,128]{1,0:T(8,128)...) custom-call(f32[128,384]{1,0:T(8,128)S(1)} %get-tuple-element.25.qt_ref, ...), custom_call_target="tpu_custom_call" | custom-call | tf_op jit(solution)/shard_map/pallas_call | solution.py:226
  31.3 15.9 %all_to_all.15.stats_ref = f32[32,1,128]{2,1,0:T(1,128)S(1)} all-to-all(f32[32,1,128]{2,1,0:T(1,128)S(1)} %get-tuple-element.28), channel_id=1, replica_groups={{25,24,17,16,9,8,1,0,217,216,209,208,201,200,193,192,153,152,145,144,13..., dimensions={0} | all-to-all | bytes 32768 | tf_op jit(solution)/shard_map/all_to_all | solution.py:40
  47.2 1.9 %shard_map.61 = (f32[1032,128]{1,0:T(8,128)S(1)}, f32[8,384]{1,0:T(8,128)S(1)}, f32[384,128]{1,0:T(8,128)}) custom-call(f32[32,1,128]{2,1,0:T(1,128)S(1)} %all_to_all.15.stats_ref, f32[8,128]{1,0:T(8,128)S(1)} %get-tuple-element.29.logits_ref, f32[8,128]{1,0:T(8,128)S(1)} %get-tuple-element.27.chosen_ref, f32[8,384]{1,0:T(8,128)S(1)} %get-tuple-element.30.scale_ref, ...), custom_call_target="tpu_custom_call" | custom-call | tf_op jit(solution)/shard_map/pallas_call | solution.py:226
  49.1 1.4 %collective-permute-start.7 = (f32[1032,128]{1,0:T(8,128)S(1)}, f32[1032,128]{1,0:T(8,128)S(1)}, u32[]{:S(2)}, u32[]{:S(2)}) collective-permute-start(f32[1032,128]{1,0:T(8,128)S(1)} %get-tuple-element.38), channel_id=1, source_target_pairs={{0,32},{1,33},{2,34},{3,35},{4,36},{5,37},{6,38},{7,39},{8,40},{9,... | collective-permute-start | bytes 1585160 | tf_op jit(solution)/shard_map/ppermute | solution.py:243
  50.5 4.3 %all-to-all-start.2 = ((f32[32,12,1,128]{3,2,1,0:T(1,128)}), f32[32,12,1,128]{3,2,1,0:T(1,128)S(1)}, u32[]{:S(2)}, u32[]{:S(2)}) async-start(f32[32,12,1,128]{3,2,1,0:T(1,128)} %bitcast.5), calls=%async_computation.2 | async-start | bytes 393216 | tf_op jit(solution)/shard_map/all_to_all | solution.py:40
  54.9 0.8 %shard_map.62.mine_ref = f32[1024,128]{1,0:T(8,128)S(1)} custom-call(f32[8,384]{1,0:T(8,128)S(1)} %get-tuple-element.35.factors_ref, f32[128,384]{1,0:T(8,128)S(1)} %get-tuple-element.25.qt_ref, bf16[4,256,384]{2,1,0:T(8,128)(2,1)S(1)} %get-tuple-element.36.whi_ref, bf16[4,256,384]{2,1,0:T(8,128)(2,1)S(1)} %get-tuple-element.37.wlo_ref), custom_call_target="tpu_custom_call" | custom-call | tf_op jit(solution)/shard_map/pallas_call | solution.py:226
  55.7 0.0 collective-permute-done.7.theirs_ref
  55.7 0.1 shard_map.63
  55.8 0.4 collective-permute-start.8
  56.2 0.5 collective-permute-start.9
  56.7 0.7 collective-permute-start.10
  57.3 7.8 %all-to-all-done.2 = f32[32,12,1,128]{3,2,1,0:T(1,128)S(1)} async-done(((f32[32,12,1,128]{3,2,1,0:T(1,128)}), f32[32,12,1,128]{3,2,1,0:T(1,128)S(1)}, u32[]{:S(2)}, u32[]{:S(2)}) %all-to-all-start.2) | async-done | bytes 196640 | tf_op jit(solution)/shard_map/all_to_all | solution.py:40
  65.1 0.0 collective-permute-done.8.r1
  65.1 0.0 collective-permute-done.9.r2
  65.1 1.0 %collective-permute-done.10.r3 = f32[264,128]{1,0:T(8,128)S(1)} collective-permute-done((f32[264,128]{1,0:T(8,128)S(1)}, f32[264,128]{1,0:T(8,128)S(1)}, u32[]{:S(2)}, u32[]{:S(2)}) %collective-permute-start.10) | collective-permute-done | bytes 135200 | tf_op jit(solution)/shard_map/ppermute | solution.py:243
  66.1 0.7 %shard_map.64 = (f32[1,256,128]{2,1,0:T(8,128)}, f32[1,1]{1,0:T(1,128)}, f32[12,1,128]{2,1,0:T(1,128)}) custom-call(f32[264,128]{1,0:T(8,128)S(1)} %get-tuple-element.39.r0, f32[264,128]{1,0:T(8,128)S(1)} %collective-permute-done.8.r1, f32[264,128]{1,0:T(8,128)S(1)} %collective-permute-done.9.r2, f32[264,128]{1,0:T(8,128)S(1)} %collective-permute-done.10.r3, ...), custom_call_target="tpu_custom_call" | custom-call | tf_op jit(solution)/shard_map/pallas_call | solution.py:226
  (1 shorter events, 0.0 us)
Async XLA Ops:
  2.0 12.2 %copy-start = (f32[1,256,128]{2,1,0:T(8,128)S(1)}, f32[1,256,128]{2,1,0:T(8,128)}, u32[]{:S(2)}) copy-start(f32[1,256,128]{2,1,0:T(8,128)} %own_hbm.1) | copy-start | bytes 393220
  2.0 25.0 %all-to-all-start = ((f32[32,12,1,128]{3,2,1,0:T(1,128)}), f32[32,12,1,128]{3,2,1,0:T(1,128)S(1)}, u32[]{:S(2)}, u32[]{:S(2)}) async-start(f32[32,12,1,128]{3,2,1,0:T(1,128)} %bitcast.3), calls=%async_computation | async-start | bytes 393216 | tf_op jit(solution)/shard_map/all_to_all | solution.py:40
  14.2 5.5 %collective-permute-start.2 = (f32[1,256,128]{2,1,0:T(8,128)S(1)}, f32[1,256,128]{2,1,0:T(8,128)S(1)}, u32[]{:S(2)}, u32[]{:S(2)}) collective-permute-start(f32[1,256,128]{2,1,0:T(8,128)S(1)} %copy-done), channel_id=1, source_target_pairs={{0,6},{1,7},{2,0},{3,1},{4,2},{5,3},{6,4},{7,5},{8,14},{9,15},{10,... | collective-permute-start | bytes 393224 | tf_op jit(solution)/shard_map/ppermute | solution.py:243
  16.8 6.5 %collective-permute-start.1 = (f32[1,256,128]{2,1,0:T(8,128)S(1)}, f32[1,256,128]{2,1,0:T(8,128)S(1)}, u32[]{:S(2)}, u32[]{:S(2)}) collective-permute-start(f32[1,256,128]{2,1,0:T(8,128)S(1)} %copy-done), channel_id=1, source_target_pairs={{0,4},{1,5},{2,6},{3,7},{4,0},{5,1},{6,2},{7,3},{8,12},{9,13},{10,... | collective-permute-start | bytes 393224 | tf_op jit(solution)/shard_map/ppermute | solution.py:243
  17.3 8.7 %collective-permute-start = (f32[1,256,128]{2,1,0:T(8,128)S(1)}, f32[1,256,128]{2,1,0:T(8,128)S(1)}, u32[]{:S(2)}, u32[]{:S(2)}) collective-permute-start(f32[1,256,128]{2,1,0:T(8,128)S(1)} %copy-done), channel_id=1, source_target_pairs={{0,2},{1,3},{2,4},{3,5},{4,6},{5,7},{6,0},{7,1},{8,10},{9,11},{10,... | collective-permute-start | bytes 393224 | tf_op jit(solution)/shard_map/ppermute | solution.py:243
  17.9 11.5 %collective-permute-start.3 = (f32[1,256,128]{2,1,0:T(8,128)S(1)}, f32[1,256,128]{2,1,0:T(8,128)S(1)}, u32[]{:S(2)}, u32[]{:S(2)}) collective-permute-start(f32[1,256,128]{2,1,0:T(8,128)S(1)} %copy-done), channel_id=1, source_target_pairs={{0,32},{1,33},{2,34},{3,35},{4,36},{5,37},{6,38},{7,39},{8,40},{9,... | collective-permute-start | bytes 393224 | tf_op jit(solution)/shard_map/ppermute | solution.py:243
  19.7 9.7 %collective-permute-start.6 = (f32[1,256,128]{2,1,0:T(8,128)S(1)}, f32[1,256,128]{2,1,0:T(8,128)S(1)}, u32[]{:S(2)}, u32[]{:S(2)}) collective-permute-start(f32[1,256,128]{2,1,0:T(8,128)S(1)} %collective-permute-done.2.p3), channel_id=1, source_target_pairs={{0,32},{1,33},{2,34},{3,35},{4,36},{5,37},{6,38},{7,39},{8,40},{9,... | collective-permute-start | bytes 393224 | tf_op jit(solution)/shard_map/ppermute | solution.py:243
  23.3 6.1 %collective-permute-start.5 = (f32[1,256,128]{2,1,0:T(8,128)S(1)}, f32[1,256,128]{2,1,0:T(8,128)S(1)}, u32[]{:S(2)}, u32[]{:S(2)}) collective-permute-start(f32[1,256,128]{2,1,0:T(8,128)S(1)} %collective-permute-done.1.p2), channel_id=1, source_target_pairs={{0,32},{1,33},{2,34},{3,35},{4,36},{5,37},{6,38},{7,39},{8,40},{9,... | collective-permute-start | bytes 393224 | tf_op jit(solution)/shard_map/ppermute | solution.py:243
  26.0 3.5 %collective-permute-start.4 = (f32[1,256,128]{2,1,0:T(8,128)S(1)}, f32[1,256,128]{2,1,0:T(8,128)S(1)}, u32[]{:S(2)}, u32[]{:S(2)}) collective-permute-start(f32[1,256,128]{2,1,0:T(8,128)S(1)} %collective-permute-done.p1), channel_id=1, source_target_pairs={{0,32},{1,33},{2,34},{3,35},{4,36},{5,37},{6,38},{7,39},{8,40},{9,... | collective-permute-start | bytes 393224 | tf_op jit(solution)/shard_map/ppermute | solution.py:243
  49.1 6.6 %collective-permute-start.7 = (f32[1032,128]{1,0:T(8,128)S(1)}, f32[1032,128]{1,0:T(8,128)S(1)}, u32[]{:S(2)}, u32[]{:S(2)}) collective-permute-start(f32[1032,128]{1,0:T(8,128)S(1)} %get-tuple-element.38), channel_id=1, source_target_pairs={{0,32},{1,33},{2,34},{3,35},{4,36},{5,37},{6,38},{7,39},{8,40},{9,... | collective-permute-start | bytes 1585160 | tf_op jit(solution)/shard_map/ppermute | solution.py:243
  50.5 14.6 %all-to-all-start.2 = ((f32[32,12,1,128]{3,2,1,0:T(1,128)}), f32[32,12,1,128]{3,2,1,0:T(1,128)S(1)}, u32[]{:S(2)}, u32[]{:S(2)}) async-start(f32[32,12,1,128]{3,2,1,0:T(1,128)} %bitcast.5), calls=%async_computation.2 | async-start | bytes 393216 | tf_op jit(solution)/shard_map/all_to_all | solution.py:40
  55.8 9.3 %collective-permute-start.8 = (f32[264,128]{1,0:T(8,128)S(1)}, f32[264,128]{1,0:T(8,128)S(1)}, u32[]{:S(2)}, u32[]{:S(2)}) collective-permute-start(f32[264,128]{1,0:T(8,128)S(1)} %get-tuple-element.40), channel_id=1, source_target_pairs={{0,6},{1,7},{2,0},{3,1},{4,2},{5,3},{6,4},{7,5},{8,14},{9,15},{10,... | collective-permute-start | bytes 405512 | tf_op jit(solution)/shard_map/ppermute | solution.py:243
  56.2 9.0 %collective-permute-start.9 = (f32[264,128]{1,0:T(8,128)S(1)}, f32[264,128]{1,0:T(8,128)S(1)}, u32[]{:S(2)}, u32[]{:S(2)}) collective-permute-start(f32[264,128]{1,0:T(8,128)S(1)} %get-tuple-element.41), channel_id=1, source_target_pairs={{0,4},{1,5},{2,6},{3,7},{4,0},{5,1},{6,2},{7,3},{8,12},{9,13},{10,... | collective-permute-start | bytes 405512 | tf_op jit(solution)/shard_map/ppermute | solution.py:243
  56.7 9.4 %collective-permute-start.10 = (f32[264,128]{1,0:T(8,128)S(1)}, f32[264,128]{1,0:T(8,128)S(1)}, u32[]{:S(2)}, u32[]{:S(2)}) collective-permute-start(f32[264,128]{1,0:T(8,128)S(1)} %get-tuple-element.42), channel_id=1, source_target_pairs={{0,2},{1,3},{2,4},{3,5},{4,6},{5,7},{6,0},{7,1},{8,10},{9,11},{10,... | collective-permute-start | bytes 405512 | tf_op jit(solution)/shard_map/ppermute | solution.py:243

commit v7 on v6

--- a/solution.py
+++ b/solution.py
@@ -252,7 +252,8 @@
         anywhere=1,
     )(queries.transpose(1, 0, 2))
     block = exchange(spread.reshape(QN, TOK, 1, W), QUERY_ORDER).reshape(ROWS, W)
-    own = [pages] + [moved(pages, X, s) for s in range(1, XN)]
+    passed = {s: moved(pages, X, s) for s in (1, 3, 2)}
+    own = [pages] + [passed[s] for s in range(1, XN)]
     other = [moved(page, CO, 1) for page in own]
 
     weights, terms = ((XN, PT, ROWS), bf16), ((XN, W, ROWS), f32)
@@ -276,7 +277,8 @@
     theirs = moved(theirs, CO, 1)
     (mine,) = call(own_gradient_kernel, [((XN * PT, W), f32)])(factors, qt, whi_a, wlo_a)
     blocks = call(pair_kernel, [((PT + 8, W), f32)] * XN)(mine, loss_rows, theirs)
-    blocks = [blocks[0]] + [moved(blocks[s], X, -s) for s in range(1, XN)]
+    returned = {s: moved(blocks[s], X, -s) for s in (2, 1, 3)}
+    blocks = [blocks[0]] + [returned[s] for s in range(1, XN)]
     dq = exchange(dq.reshape(QN, TOK, 1, W), QUERY_ORDER)
     page_grad, loss, slope = call(
         final_kernel, [((1, PT, W), f32), ((1, 1), f32), ((TOK, 1, W), f32)]

time: 67.1 us -> 67.1 us (level)
  no operation moved by 1% of the time
where the time goes in v7:
time: 67.1 us; the launch traced here: 66.8 us
  starting transfers between devices  31.9 us (48%)
  blocking collectives  15.9 us (24%)
  waiting for transfers between devices  9.09 us (14%)
  Pallas kernels  9.05 us (13%)
  between operations  0.74 us (1%)
    all_to_all x2, starting transfers between devices, exchange(): lax.all_to_all(value, 'd', 0, 0, axis_index_groups=groups(order), tiled=T...  16.5 us
    all_to_all x1, blocking collectives, exchange(): lax.all_to_all(value, 'd', 0, 0, axis_index_groups=groups(order), tiled=T...  15.9 us
    ppermute x11, starting transfers between devices, moved(): return lax.ppermute(value, 'd', pairs)  15.4 us
    pallas_call x7, Pallas kernels, run(): pl.pallas_call(kernel, out_shape=[jax.ShapeDtypeStruct(s, d) for s, d in...  9.05 us
    all_to_all x2, waiting for transfers between devices, exchange(): lax.all_to_all(value, 'd', 0, 0, axis_index_groups=groups(order), tiled=T...  7.79 us
  transfers between devices with their start and end apart: 13, of which 3 were waited for; matrix products, arithmetic and copies ran while one was open for 0% of the time, Pallas kernels for 5%

profile of v7, /device:TPU:1, one launch (start us, length us, event | category | flops | bytes accessed | tf_op | source)
XLA Modules:
  0.0 66.8 jit_solution(10055575358560818715)
XLA Ops:
  0.6 1.4 %shard_map.58 = f32[384,128]{1,0:T(8,128)} custom-call(f32[12,1,128]{2,1,0:T(1,128)} %bitcast.11), custom_call_target="tpu_custom_call" | custom-call | tf_op jit(solution)/shard_map/pallas_call | solution.py:226
  2.0 0.0 copy-start
  2.0 12.2 %all-to-all-start = ((f32[32,12,1,128]{3,2,1,0:T(1,128)}), f32[32,12,1,128]{3,2,1,0:T(1,128)S(1)}, u32[]{:S(2)}, u32[]{:S(2)}) async-start(f32[32,12,1,128]{3,2,1,0:T(1,128)} %bitcast.3), calls=%async_computation | async-start | bytes 393216 | tf_op jit(solution)/shard_map/all_to_all | solution.py:40
  14.2 0.0 copy-done
  14.2 2.6 %collective-permute-start.2 = (f32[1,256,128]{2,1,0:T(8,128)S(1)}, f32[1,256,128]{2,1,0:T(8,128)S(1)}, u32[]{:S(2)}, u32[]{:S(2)}) collective-permute-start(f32[1,256,128]{2,1,0:T(8,128)S(1)} %copy-done), channel_id=1, source_target_pairs={{0,6},{1,7},{2,0},{3,1},{4,2},{5,3},{6,4},{7,5},{8,14},{9,15},{10,... | collective-permute-start | bytes 393224 | tf_op jit(solution)/shard_map/ppermute | solution.py:243
  16.8 0.5 collective-permute-start.1
  17.3 0.6 collective-permute-start
  17.9 1.8 %collective-permute-start.3 = (f32[1,256,128]{2,1,0:T(8,128)S(1)}, f32[1,256,128]{2,1,0:T(8,128)S(1)}, u32[]{:S(2)}, u32[]{:S(2)}) collective-permute-start(f32[1,256,128]{2,1,0:T(8,128)S(1)} %copy-done), channel_id=1, source_target_pairs={{0,32},{1,33},{2,34},{3,35},{4,36},{5,37},{6,38},{7,39},{8,40},{9,... | collective-permute-start | bytes 393224 | tf_op jit(solution)/shard_map/ppermute | solution.py:243
  19.7 0.0 collective-permute-done.2.p3
  19.7 3.6 %collective-permute-start.6 = (f32[1,256,128]{2,1,0:T(8,128)S(1)}, f32[1,256,128]{2,1,0:T(8,128)S(1)}, u32[]{:S(2)}, u32[]{:S(2)}) collective-permute-start(f32[1,256,128]{2,1,0:T(8,128)S(1)} %collective-permute-done.2.p3), channel_id=1, source_target_pairs={{0,32},{1,33},{2,34},{3,35},{4,36},{5,37},{6,38},{7,39},{8,40},{9,... | collective-permute-start | bytes 393224 | tf_op jit(solution)/shard_map/ppermute | solution.py:243
  23.3 0.0 collective-permute-done.1.p2
  23.3 2.3 %collective-permute-start.5 = (f32[1,256,128]{2,1,0:T(8,128)S(1)}, f32[1,256,128]{2,1,0:T(8,128)S(1)}, u32[]{:S(2)}, u32[]{:S(2)}) collective-permute-start(f32[1,256,128]{2,1,0:T(8,128)S(1)} %collective-permute-done.1.p2), channel_id=1, source_target_pairs={{0,32},{1,33},{2,34},{3,35},{4,36},{5,37},{6,38},{7,39},{8,40},{9,... | collective-permute-start | bytes 393224 | tf_op jit(solution)/shard_map/ppermute | solution.py:243
  25.6 0.3 collective-permute-done.p1
  26.0 1.0 %collective-permute-start.4 = (f32[1,256,128]{2,1,0:T(8,128)S(1)}, f32[1,256,128]{2,1,0:T(8,128)S(1)}, u32[]{:S(2)}, u32[]{:S(2)}) collective-permute-start(f32[1,256,128]{2,1,0:T(8,128)S(1)} %collective-permute-done.p1), channel_id=1, source_target_pairs={{0,32},{1,33},{2,34},{3,35},{4,36},{5,37},{6,38},{7,39},{8,40},{9,... | collective-permute-start | bytes 393224 | tf_op jit(solution)/shard_map/ppermute | solution.py:243
  27.0 0.0 all-to-all-done
  27.0 2.4 %shard_map.59 = (bf16[4,256,384]{2,1,0:T(8,128)(2,1)S(1)}, bf16[4,256,384]{2,1,0:T(8,128)(2,1)S(1)}, f32[4,128,384]{2,1,0:T(8,128)S(1)}, f32[4,384]{1,0:T(4,128)...) custom-call(s32[1]{0:T(128)} %bitcast.me_ref, f32[1,256,128]{2,1,0:T(8,128)} %own_hbm.1, s32[1,256]{1,0:T(1,128)} %bitcast.12, ...), custom_call_target="tpu_custom_call" | custom-call | tf_op jit(solution)/shard_map/pallas_call | solution.py:226
  29.4 0.0 collective-permute-done.3.p0
  29.4 0.0 collective-permute-done.6.p3
  29.4 0.0 collective-permute-done.5.p2
  29.4 0.0 collective-permute-done.4.p1
  29.5 1.8 %shard_map.60 = (bf16[4,256,384]{2,1,0:T(8,128)(2,1)S(1)}, bf16[4,256,384]{2,1,0:T(8,128)(2,1)S(1)}, f32[4,128,384]{2,1,0:T(8,128)S(1)}, f32[8,128]{1,0:T(8,128)...) custom-call(f32[128,384]{1,0:T(8,128)S(1)} %get-tuple-element.25.qt_ref, ...), custom_call_target="tpu_custom_call" | custom-call | tf_op jit(solution)/shard_map/pallas_call | solution.py:226
  31.3 15.9 %all_to_all.15.stats_ref = f32[32,1,128]{2,1,0:T(1,128)S(1)} all-to-all(f32[32,1,128]{2,1,0:T(1,128)S(1)} %get-tuple-element.28), channel_id=1, replica_groups={{25,24,17,16,9,8,1,0,217,216,209,208,201,200,193,192,153,152,145,144,13..., dimensions={0} | all-to-all | bytes 32768 | tf_op jit(solution)/shard_map/all_to_all | solution.py:40
  47.2 1.9 %shard_map.61 = (f32[1032,128]{1,0:T(8,128)S(1)}, f32[8,384]{1,0:T(8,128)S(1)}, f32[384,128]{1,0:T(8,128)}) custom-call(f32[32,1,128]{2,1,0:T(1,128)S(1)} %all_to_all.15.stats_ref, f32[8,128]{1,0:T(8,128)S(1)} %get-tuple-element.29.logits_ref, f32[8,128]{1,0:T(8,128)S(1)} %get-tuple-element.27.chosen_ref, f32[8,384]{1,0:T(8,128)S(1)} %get-tuple-element.30.scale_ref, ...), custom_call_target="tpu_custom_call" | custom-call | tf_op jit(solution)/shard_map/pallas_call | solution.py:226
  49.1 1.4 %collective-permute-start.7 = (f32[1032,128]{1,0:T(8,128)S(1)}, f32[1032,128]{1,0:T(8,128)S(1)}, u32[]{:S(2)}, u32[]{:S(2)}) collective-permute-start(f32[1032,128]{1,0:T(8,128)S(1)} %get-tuple-element.38), channel_id=1, source_target_pairs={{0,32},{1,33},{2,34},{3,35},{4,36},{5,37},{6,38},{7,39},{8,40},{9,... | collective-permute-start | bytes 1585160 | tf_op jit(solution)/shard_map/ppermute | solution.py:243
  50.5 4.3 %all-to-all-start.2 = ((f32[32,12,1,128]{3,2,1,0:T(1,128)}), f32[32,12,1,128]{3,2,1,0:T(1,128)S(1)}, u32[]{:S(2)}, u32[]{:S(2)}) async-start(f32[32,12,1,128]{3,2,1,0:T(1,128)} %bitcast.5), calls=%async_computation.2 | async-start | bytes 393216 | tf_op jit(solution)/shard_map/all_to_all | solution.py:40
  54.9 0.8 %shard_map.62.mine_ref = f32[1024,128]{1,0:T(8,128)S(1)} custom-call(f32[8,384]{1,0:T(8,128)S(1)} %get-tuple-element.35.factors_ref, f32[128,384]{1,0:T(8,128)S(1)} %get-tuple-element.25.qt_ref, bf16[4,256,384]{2,1,0:T(8,128)(2,1)S(1)} %get-tuple-element.36.whi_ref, bf16[4,256,384]{2,1,0:T(8,128)(2,1)S(1)} %get-tuple-element.37.wlo_ref), custom_call_target="tpu_custom_call" | custom-call | tf_op jit(solution)/shard_map/pallas_call | solution.py:226
  55.7 0.0 collective-permute-done.7.theirs_ref
  55.7 0.1 shard_map.63
  55.8 0.4 collective-permute-start.8
  56.2 0.5 collective-permute-start.9
  56.7 0.7 collective-permute-start.10
  57.3 7.8 %all-to-all-done.2 = f32[32,12,1,128]{3,2,1,0:T(1,128)S(1)} async-done(((f32[32,12,1,128]{3,2,1,0:T(1,128)}), f32[32,12,1,128]{3,2,1,0:T(1,128)S(1)}, u32[]{:S(2)}, u32[]{:S(2)}) %all-to-all-start.2) | async-done | bytes 196640 | tf_op jit(solution)/shard_map/all_to_all | solution.py:40
  65.1 0.0 collective-permute-done.8.r1
  65.1 0.0 collective-permute-done.9.r2
  65.1 1.0 %collective-permute-done.10.r3 = f32[264,128]{1,0:T(8,128)S(1)} collective-permute-done((f32[264,128]{1,0:T(8,128)S(1)}, f32[264,128]{1,0:T(8,128)S(1)}, u32[]{:S(2)}, u32[]{:S(2)}) %collective-permute-start.10) | collective-permute-done | bytes 135200 | tf_op jit(solution)/shard_map/ppermute | solution.py:243
  66.1 0.7 %shard_map.64 = (f32[1,256,128]{2,1,0:T(8,128)}, f32[1,1]{1,0:T(1,128)}, f32[12,1,128]{2,1,0:T(1,128)}) custom-call(f32[264,128]{1,0:T(8,128)S(1)} %get-tuple-element.39.r0, f32[264,128]{1,0:T(8,128)S(1)} %collective-permute-done.8.r1, f32[264,128]{1,0:T(8,128)S(1)} %collective-permute-done.9.r2, f32[264,128]{1,0:T(8,128)S(1)} %collective-permute-done.10.r3, ...), custom_call_target="tpu_custom_call" | custom-call | tf_op jit(solution)/shard_map/pallas_call | solution.py:226
  (1 shorter events, 0.0 us)
Async XLA Ops:
  2.0 12.2 %copy-start = (f32[1,256,128]{2,1,0:T(8,128)S(1)}, f32[1,256,128]{2,1,0:T(8,128)}, u32[]{:S(2)}) copy-start(f32[1,256,128]{2,1,0:T(8,128)} %own_hbm.1) | copy-start | bytes 393220
  2.0 25.0 %all-to-all-start = ((f32[32,12,1,128]{3,2,1,0:T(1,128)}), f32[32,12,1,128]{3,2,1,0:T(1,128)S(1)}, u32[]{:S(2)}, u32[]{:S(2)}) async-start(f32[32,12,1,128]{3,2,1,0:T(1,128)} %bitcast.3), calls=%async_computation | async-start | bytes 393216 | tf_op jit(solution)/shard_map/all_to_all | solution.py:40
  14.2 5.5 %collective-permute-start.2 = (f32[1,256,128]{2,1,0:T(8,128)S(1)}, f32[1,256,128]{2,1,0:T(8,128)S(1)}, u32[]{:S(2)}, u32[]{:S(2)}) collective-permute-start(f32[1,256,128]{2,1,0:T(8,128)S(1)} %copy-done), channel_id=1, source_target_pairs={{0,6},{1,7},{2,0},{3,1},{4,2},{5,3},{6,4},{7,5},{8,14},{9,15},{10,... | collective-permute-start | bytes 393224 | tf_op jit(solution)/shard_map/ppermute | solution.py:243
  16.8 6.5 %collective-permute-start.1 = (f32[1,256,128]{2,1,0:T(8,128)S(1)}, f32[1,256,128]{2,1,0:T(8,128)S(1)}, u32[]{:S(2)}, u32[]{:S(2)}) collective-permute-start(f32[1,256,128]{2,1,0:T(8,128)S(1)} %copy-done), channel_id=1, source_target_pairs={{0,4},{1,5},{2,6},{3,7},{4,0},{5,1},{6,2},{7,3},{8,12},{9,13},{10,... | collective-permute-start | bytes 393224 | tf_op jit(solution)/shard_map/ppermute | solution.py:243
  17.3 8.7 %collective-permute-start = (f32[1,256,128]{2,1,0:T(8,128)S(1)}, f32[1,256,128]{2,1,0:T(8,128)S(1)}, u32[]{:S(2)}, u32[]{:S(2)}) collective-permute-start(f32[1,256,128]{2,1,0:T(8,128)S(1)} %copy-done), channel_id=1, source_target_pairs={{0,2},{1,3},{2,4},{3,5},{4,6},{5,7},{6,0},{7,1},{8,10},{9,11},{10,... | collective-permute-start | bytes 393224 | tf_op jit(solution)/shard_map/ppermute | solution.py:243
  17.9 11.5 %collective-permute-start.3 = (f32[1,256,128]{2,1,0:T(8,128)S(1)}, f32[1,256,128]{2,1,0:T(8,128)S(1)}, u32[]{:S(2)}, u32[]{:S(2)}) collective-permute-start(f32[1,256,128]{2,1,0:T(8,128)S(1)} %copy-done), channel_id=1, source_target_pairs={{0,32},{1,33},{2,34},{3,35},{4,36},{5,37},{6,38},{7,39},{8,40},{9,... | collective-permute-start | bytes 393224 | tf_op jit(solution)/shard_map/ppermute | solution.py:243
  19.7 9.7 %collective-permute-start.6 = (f32[1,256,128]{2,1,0:T(8,128)S(1)}, f32[1,256,128]{2,1,0:T(8,128)S(1)}, u32[]{:S(2)}, u32[]{:S(2)}) collective-permute-start(f32[1,256,128]{2,1,0:T(8,128)S(1)} %collective-permute-done.2.p3), channel_id=1, source_target_pairs={{0,32},{1,33},{2,34},{3,35},{4,36},{5,37},{6,38},{7,39},{8,40},{9,... | collective-permute-start | bytes 393224 | tf_op jit(solution)/shard_map/ppermute | solution.py:243
  23.3 6.1 %collective-permute-start.5 = (f32[1,256,128]{2,1,0:T(8,128)S(1)}, f32[1,256,128]{2,1,0:T(8,128)S(1)}, u32[]{:S(2)}, u32[]{:S(2)}) collective-permute-start(f32[1,256,128]{2,1,0:T(8,128)S(1)} %collective-permute-done.1.p2), channel_id=1, source_target_pairs={{0,32},{1,33},{2,34},{3,35},{4,36},{5,37},{6,38},{7,39},{8,40},{9,... | collective-permute-start | bytes 393224 | tf_op jit(solution)/shard_map/ppermute | solution.py:243
  26.0 3.5 %collective-permute-start.4 = (f32[1,256,128]{2,1,0:T(8,128)S(1)}, f32[1,256,128]{2,1,0:T(8,128)S(1)}, u32[]{:S(2)}, u32[]{:S(2)}) collective-permute-start(f32[1,256,128]{2,1,0:T(8,128)S(1)} %collective-permute-done.p1), channel_id=1, source_target_pairs={{0,32},{1,33},{2,34},{3,35},{4,36},{5,37},{6,38},{7,39},{8,40},{9,... | collective-permute-start | bytes 393224 | tf_op jit(solution)/shard_map/ppermute | solution.py:243
  49.1 6.6 %collective-permute-start.7 = (f32[1032,128]{1,0:T(8,128)S(1)}, f32[1032,128]{1,0:T(8,128)S(1)}, u32[]{:S(2)}, u32[]{:S(2)}) collective-permute-start(f32[1032,128]{1,0:T(8,128)S(1)} %get-tuple-element.38), channel_id=1, source_target_pairs={{0,32},{1,33},{2,34},{3,35},{4,36},{5,37},{6,38},{7,39},{8,40},{9,... | collective-permute-start | bytes 1585160 | tf_op jit(solution)/shard_map/ppermute | solution.py:243
  50.5 14.6 %all-to-all-start.2 = ((f32[32,12,1,128]{3,2,1,0:T(1,128)}), f32[32,12,1,128]{3,2,1,0:T(1,128)S(1)}, u32[]{:S(2)}, u32[]{:S(2)}) async-start(f32[32,12,1,128]{3,2,1,0:T(1,128)} %bitcast.5), calls=%async_computation.2 | async-start | bytes 393216 | tf_op jit(solution)/shard_map/all_to_all | solution.py:40
  55.8 9.3 %collective-permute-start.8 = (f32[264,128]{1,0:T(8,128)S(1)}, f32[264,128]{1,0:T(8,128)S(1)}, u32[]{:S(2)}, u32[]{:S(2)}) collective-permute-start(f32[264,128]{1,0:T(8,128)S(1)} %get-tuple-element.40), channel_id=1, source_target_pairs={{0,6},{1,7},{2,0},{3,1},{4,2},{5,3},{6,4},{7,5},{8,14},{9,15},{10,... | collective-permute-start | bytes 405512 | tf_op jit(solution)/shard_map/ppermute | solution.py:243
  56.2 9.0 %collective-permute-start.9 = (f32[264,128]{1,0:T(8,128)S(1)}, f32[264,128]{1,0:T(8,128)S(1)}, u32[]{:S(2)}, u32[]{:S(2)}) collective-permute-start(f32[264,128]{1,0:T(8,128)S(1)} %get-tuple-element.41), channel_id=1, source_target_pairs={{0,4},{1,5},{2,6},{3,7},{4,0},{5,1},{6,2},{7,3},{8,12},{9,13},{10,... | collective-permute-start | bytes 405512 | tf_op jit(solution)/shard_map/ppermute | solution.py:243
  56.7 9.4 %collective-permute-start.10 = (f32[264,128]{1,0:T(8,128)S(1)}, f32[264,128]{1,0:T(8,128)S(1)}, u32[]{:S(2)}, u32[]{:S(2)}) collective-permute-start(f32[264,128]{1,0:T(8,128)S(1)} %get-tuple-element.42), channel_id=1, source_target_pairs={{0,2},{1,3},{2,4},{3,5},{4,6},{5,7},{6,0},{7,1},{8,10},{9,11},{10,... | collective-permute-start | bytes 405512 | tf_op jit(solution)/shard_map/ppermute | solution.py:243
